TPU v7x, 256 devices: a whole 4x4x8 slice. The times are simulated.
256 devices in a mesh: depth: 4 (over z_hi), tile: 64 (over x, y, z_lo, core).
Axes of the slice: x: 4, y: 4, z: 8 (z_hi: 4, z_lo: 2; z = z_hi * 2 + z_lo), core: 2. Of those that a mesh axis runs over, the one named last changes fastest.
Arguments:
- amplitude: float32 [8, 64, 256, 256], P('depth', 'tile'), may hold values from 0.7 to 1.3
- phase_map: float32 [8, 64, 256, 256], P('depth', 'tile'), may hold values from -3.140625 to 3.140625
- probe_wave: float32 [2, 128, 128], replicated, may hold values from -4 to 4
- propagator_phase: float32 [2, 128], replicated, may hold values from -3.140625 to 3.140625
- positions: int32 [64, 4, 2], P('tile'), may hold values from -64 to 192
- measured: float32 [64, 4, 128, 128], P('tile'), may hold values from 0 to 1
Outputs:
- object_gradient: float32 [2, 8, 64, 256, 256], P(None, 'depth', 'tile')
Inputs may be any that keep to these rules, and one draw needn't show every extreme that they name: `positions`: every window of 128 x 128 pixels starting at a position lies within 64 pixels of its tile.
All inputs are finite; a program needn't handle non-finite values.
Results may differ from a plain program's by a relative error of at most 0.02.
Values may be sent and summed in bfloat16 or wider, within the bound.
No kernel may reach another device: no remote copies, remote signals or barrier semaphores. Data moves between devices by JAX's collectives and lax.ppermute only.
A program may use at most 128 MiB of HBM per device.

v0:
```python
import functools
import math

import jax
import jax.numpy as jnp
import numpy as np
from jax import lax
from jax.experimental import pallas as pl
from jax.experimental.pallas import tpu as pltpu
from jax.sharding import PartitionSpec as P

RIM = 64
LANES = 128
F32 = jnp.float32
BF16 = jnp.bfloat16
VMEM = pl.BlockSpec(memory_space=pltpu.VMEM)
SMEM = pl.BlockSpec(memory_space=pltpu.SMEM)


def call(body, out_shape, inputs, specs=None, scratch=(), flops=0, limit=24, name=None):
    out_specs = jax.tree.map(lambda _: VMEM, out_shape)
    moved = sum(x.size * x.dtype.itemsize for x in inputs)
    moved += sum(x.size * x.dtype.itemsize for x in jax.tree.leaves(out_shape))
    return pl.pallas_call(
        body,
        out_shape=out_shape,
        in_specs=specs or [VMEM] * len(inputs),
        out_specs=out_specs,
        scratch_shapes=list(scratch),
        compiler_params=pltpu.CompilerParams(vmem_limit_bytes=limit << 20),
        cost_estimate=pl.CostEstimate(flops=flops, bytes_accessed=moved, transcendentals=0),
        name=name,
    )(*inputs)


def sds(*shape, dtype=BF16):
    return jax.ShapeDtypeStruct(shape, dtype)


def sincos(x):
    y = x * 0.5
    q = y * y
    sine = 1.0
    for n in (11, 9, 7, 5, 3):
        sine = 1.0 - q * sine * (1.0 / (n * (n - 1)))
    sine = sine * y
    cosine = 1.0
    for n in (12, 10, 8, 6, 4, 2):
        cosine = 1.0 - q * cosine * (1.0 / (n * (n - 1)))
    return 2.0 * sine * cosine, 1.0 - 2.0 * sine * sine


def dft_tables(points):
    products = np.outer(np.arange(points), np.arange(points)) % points
    angles = products * (-2.0 * math.pi / points)
    scale = 1.0 / math.sqrt(points)
    return (np.cos(angles) * scale).astype(np.float32), (np.sin(angles) * scale).astype(np.float32)


def transmit_body(amp_ref, phase_ref, t_ref, up_ref, down_ref):
    size = amp_ref.shape[-1]
    for s in range(amp_ref.shape[0]):
        sine, cosine = sincos(phase_ref[s])
        amp = amp_ref[s]
        for part, value in enumerate((amp * cosine, amp * sine)):
            value = value.astype(BF16)
            t_ref[s, part] = value
            up_ref[s, part] = value[:RIM]
            down_ref[s, part] = value[size - RIM :]


def lane_halves(low, high):
    lane = lax.broadcasted_iota(jnp.int32, low.shape, 1)
    return jnp.where(lane < RIM, low, high)


def swap(x):
    return pltpu.roll(x, RIM, 1)


def column_body(t_ref, above_ref, below_ref, left_ref, right_ref):
    size = t_ref.shape[-1]
    for s in range(t_ref.shape[0]):
        for start, rows, ref in (
            (0, RIM, above_ref),
            (RIM, size, t_ref),
            (RIM + size, RIM, below_ref),
        ):
            dst = pl.ds(start, rows)
            real = ref[s, 0, :, :LANES].astype(F32)
            imag = ref[s, 1, :, :LANES].astype(F32)
            left_ref[s, dst, :] = lane_halves(real, swap(imag)).astype(BF16)
            real = ref[s, 0, :, size - LANES :].astype(F32)
            imag = ref[s, 1, :, size - LANES :].astype(F32)
            right_ref[s, dst, :] = lane_halves(swap(real), imag).astype(BF16)


def lane_place(column, size):
    tiles = (size + 2 * RIM) // LANES
    place = jnp.where(column < 0, column + size + 2 * RIM, column)
    first = place // LANES
    second = jnp.where(first == tiles - 1, 0, first + 1)
    return first, second, place % LANES


def cut_body(count, pos_ref, t_ref, above_ref, below_ref, lrim_ref, rrim_ref, *rest):
    outs, ext = rest[:count], rest[count]
    size = t_ref.shape[-1]
    slices = t_ref.shape[0]
    for s in range(slices):
        for part in range(2):
            for start, rows, ref in (
                (0, RIM, above_ref),
                (RIM, size, t_ref),
                (RIM + size, RIM, below_ref),
            ):
                for tile in range(size // LANES):
                    ext[tile, s, part, pl.ds(start, rows), :] = ref[
                        s, part, :, tile * LANES : (tile + 1) * LANES
                    ].astype(F32)
        left = lrim_ref[s].astype(F32)
        right = rrim_ref[s].astype(F32)
        ext[size // LANES, s, 0] = lane_halves(right, swap(left))
        ext[size // LANES, s, 1] = lane_halves(swap(right), left)
    depth = lax.axis_index("depth")
    for k in range(count):
        wave = lax.rem(depth + k, count)
        row = pos_ref[wave, 0] + RIM
        first, second, shift = lane_place(pos_ref[wave, 1], size)
        turn = lax.rem(LANES - shift, LANES)
        lane = lax.broadcasted_iota(jnp.int32, (LANES, LANES), 1)
        for s in range(slices):
            for part in range(2):
                low = pltpu.roll(ext[first, s, part, pl.ds(row, LANES), :], turn, 1)
                high = pltpu.roll(ext[second, s, part, pl.ds(row, LANES), :], turn, 1)
                outs[k][s, part] = jnp.where(lane < LANES - shift, low, high).astype(BF16)


def operator_body(phase_ref, dft_real_ref, dft_imag_ref, fwd_ref, bwd_ref):
    fr = dft_real_ref[...]
    fi = dft_imag_ref[...]
    n = fr.shape[0]

    def dot(a, b):
        return jnp.dot(a, b, precision=lax.Precision.HIGHEST, preferred_element_type=F32)

    def put(index, real, imag, flip):
        rt, it = real.T, imag.T
        plain = ((real, imag), (-imag, real))
        turned = ((rt, -it), (it, rt))
        for i in range(2):
            for j in range(2):
                rows, cols = pl.ds(i * n, n), pl.ds(j * n, n)
                value = (turned if flip else plain)[i][j]
                high = value.astype(BF16)
                fwd_ref[index, 0, rows, cols] = high
                fwd_ref[index, 1, rows, cols] = (value - high.astype(F32)).astype(BF16)
                bwd_ref[index, rows, cols] = (plain if flip else turned)[i][j].astype(BF16)

    for axis in range(2):
        sine, cosine = sincos(phase_ref[axis : axis + 1, :])
        er = fr * cosine - fi * sine
        ei = fr * sine + fi * cosine
        real = dot(er, fr) + dot(ei, fi)
        imag = dot(ei, fr) - dot(er, fi)
        put(axis, real, imag, axis == 0)
        put(2 + axis, er, ei, axis == 0)


def split(x):
    high = x.astype(BF16)
    return high, (x - high.astype(F32)).astype(BF16)


def mm(a, b):
    return jnp.dot(a, b, preferred_element_type=F32)


def left_fine(fwd_ref, index, real, imag):
    n = real.shape[0]
    high, low = split(jnp.concatenate([real, imag], axis=0))
    both = mm(fwd_ref[index, 0], jnp.concatenate([high, low], axis=1))
    out = both[:, :n] + both[:, n:] + mm(fwd_ref[index, 1], high)
    return out[:n], out[n:]


def right_fine(fwd_ref, index, real, imag):
    n = real.shape[0]
    high, low = split(jnp.concatenate([real, imag], axis=1))
    both = mm(jnp.concatenate([high, low], axis=0), fwd_ref[index, 0])
    out = both[:n] + both[n:] + mm(high, fwd_ref[index, 1])
    return out[:, :n], out[:, n:]


def left_plain(bwd_ref, index, real, imag):
    n = real.shape[0]
    out = mm(bwd_ref[index], jnp.concatenate([real, imag], axis=0).astype(BF16))
    return out[:n], out[n:]


def right_plain(bwd_ref, index, real, imag):
    n = real.shape[0]
    out = mm(jnp.concatenate([real, imag], axis=1).astype(BF16), bwd_ref[index])
    return out[:, :n], out[:, n:]


def wave_body(count, fwd_ref, bwd_ref, probe_ref, measured_ref, *rest):
    windows, outs = rest[:count], rest[count : 2 * count]
    patch, waves, grads = rest[2 * count :]
    depth = lax.axis_index("depth")
    slices = windows[0].shape[0]
    total = slices * count
    for k in range(count):
        group = lax.rem(depth + count - k, count)
        patch[group] = windows[k][...]

    def patch_of(s):
        group, local = s // slices, s % slices
        return patch[group, local, 0].astype(F32), patch[group, local, 1].astype(F32)

    def mix(s, wr, wi):
        pr, pi = patch_of(s)
        waves[s, 0] = wr
        waves[s, 1] = wi
        return pr * wr - pi * wi, pr * wi + pi * wr

    def forward(s, wave):
        half = left_fine(fwd_ref, 0, *mix(s, *wave))
        return right_fine(fwd_ref, 1, *half)

    wave = lax.fori_loop(0, total - 1, forward, (probe_ref[0], probe_ref[1]))
    half = left_fine(fwd_ref, 2, *mix(total - 1, *wave))
    far_real, far_imag = right_fine(fwd_ref, 3, *half)
    misfit = far_real * far_real + far_imag * far_imag - measured_ref[depth]
    half = left_plain(bwd_ref, 2, misfit * far_real, misfit * far_imag)
    spread = right_plain(bwd_ref, 3, *half)

    def contribute(s, sr, si):
        wr, wi = waves[s, 0], waves[s, 1]
        group, local = s // slices, s % slices
        grads[group, local, 0] = (wr * sr + wi * si).astype(BF16)
        grads[group, local, 1] = (wr * si - wi * sr).astype(BF16)

    def backward(step, spread):
        s = total - 1 - step
        sr, si = spread
        contribute(s, sr, si)
        pr, pi = patch_of(s)
        half = left_plain(bwd_ref, 0, pr * sr + pi * si, pr * si - pi * sr)
        return right_plain(bwd_ref, 1, *half)

    spread = lax.fori_loop(0, total - 1, backward, spread)
    contribute(0, *spread)
    for k in range(count):
        outs[k][...] = grads[lax.rem(depth + k, count)]


def deposit_body(count, pos_ref, *rest):
    grads = rest[:count]
    inner_ref, left_ref, right_ref, ext = rest[count:]
    size = inner_ref.shape[-1]
    tiles = ext.shape[0]
    slices = grads[0].shape[0]
    ext[...] = jnp.zeros_like(ext)
    depth = lax.axis_index("depth")
    for k in range(count):
        wave = lax.rem(depth + count - k, count)
        row = pos_ref[wave, 0] + RIM
        first, second, shift = lane_place(pos_ref[wave, 1], size)
        lane = lax.broadcasted_iota(jnp.int32, (LANES, LANES), 1)
        rows = pl.ds(row, LANES)
        for s in range(slices):
            for part in range(2):
                moved = pltpu.roll(grads[k][s, part].astype(F32), shift, 1)
                low = jnp.where(lane >= shift, moved, 0.0)
                ext[first, s, part, rows, :] += low
                ext[second, s, part, rows, :] += moved - low
    for s in range(slices):
        real, imag = ext[tiles - 1, s, 0], ext[tiles - 1, s, 1]
        right_ref[s] = lane_halves(real, swap(imag)).astype(BF16)
        left_ref[s] = lane_halves(swap(real), imag).astype(BF16)
        for part in range(2):
            for tile in range(tiles - 1):
                inner_ref[s, part, :, tile * LANES : (tile + 1) * LANES] = ext[tile, s, part]


def halves_added(inner_ref, left_ref, right_ref, s, part, rows):
    size = inner_ref.shape[-1]
    left = left_ref[s, rows, :].astype(F32)
    right = right_ref[s, rows, :].astype(F32)
    if part == 0:
        right = swap(right)
    else:
        left = swap(left)
    zero = jnp.zeros_like(left)
    first = inner_ref[s, part, rows, :LANES] + lane_halves(left, zero)
    last = inner_ref[s, part, rows, size - LANES :] + lane_halves(zero, right)
    return first, last


def row_body(inner_ref, left_ref, right_ref, up_ref, down_ref):
    size = inner_ref.shape[-1]
    height = inner_ref.shape[-2]
    for s in range(inner_ref.shape[0]):
        for part in range(2):
            for start, out in ((0, up_ref), (height - RIM, down_ref)):
                rows = pl.ds(start, RIM)
                first, last = halves_added(inner_ref, left_ref, right_ref, s, part, rows)
                out[s, part, :, :LANES] = first.astype(BF16)
                out[s, part, :, size - LANES :] = last.astype(BF16)


def finish_body(inner_ref, left_ref, right_ref, above_ref, below_ref, out_ref):
    size = inner_ref.shape[-1]
    for s in range(inner_ref.shape[0]):
        for part in range(2):
            for start in range(0, size, RIM):
                rows = pl.ds(RIM + start, RIM)
                pieces = halves_added(inner_ref, left_ref, right_ref, s, part, rows)
                for tile, piece in enumerate(pieces):
                    lanes = slice(tile * LANES, (tile + 1) * LANES)
                    if start == 0:
                        piece = piece + above_ref[s, part, :, lanes].astype(F32)
                    if start == size - RIM:
                        piece = piece + below_ref[s, part, :, lanes].astype(F32)
                    out_ref[part, s, start : start + RIM, lanes] = piece


def shards(amplitude, phase_map, probe_wave, propagator_phase, positions, measured):
    slices, size = amplitude.shape[0], amplitude.shape[-1]
    points = probe_wave.shape[-1]
    count = lax.axis_size("depth")
    tiles = lax.axis_size("tile")
    columns = max(2, tiles // 8)
    pos = positions[0]

    def row_shift(x, by):
        pairs = [(i, i + by * columns) for i in range(tiles) if 0 <= i + by * columns < tiles]
        return lax.ppermute(x, "tile", pairs)

    def column_shift(x, by):
        pairs = [(i, i + by) for i in range(tiles) if 0 <= i % columns + by < columns]
        return lax.ppermute(x, "tile", pairs)

    def depth_shift(x, by):
        return lax.ppermute(x, "depth", [(i, (i + by) % count) for i in range(count)])

    rim_rows = sds(slices, 2, RIM, size)
    rim_cols = sds(slices, size + 2 * RIM, LANES)
    window = sds(slices, 2, points, points)
    trans, up, down = call(
        transmit_body,
        (sds(slices, 2, size, size), rim_rows, rim_rows),
        (amplitude[:, 0], phase_map[:, 0]),
        flops=40 * 2 * size * size,
        name="transmit",
    )
    below = row_shift(up, -1)
    above = row_shift(down, 1)
    dft_real, dft_imag = dft_tables(points)
    fwd, bwd = call(
        operator_body,
        (sds(4, 2, 2 * points, 2 * points), sds(4, 2 * points, 2 * points)),
        (propagator_phase, jnp.asarray(dft_real), jnp.asarray(dft_imag)),
        flops=8 * 6 * 2 * points**3,
        name="operators",
    )
    left, right = call(
        column_body, (rim_cols, rim_cols), (trans, above, below), name="column_rims"
    )
    right_rim = column_shift(left, -1)
    left_rim = column_shift(right, 1)
    ext_tiles = (size + 2 * RIM) // LANES
    ext = pltpu.VMEM((ext_tiles, slices, 2, size + 2 * RIM, LANES), F32)
    windows = call(
        functools.partial(cut_body, count),
        (window,) * count,
        (pos, trans, above, below, left_rim, right_rim),
        specs=[SMEM] + [VMEM] * 5,
        scratch=(ext,),
        name="cut",
    )
    arrived = [windows[0]] + [depth_shift(windows[k], k) for k in range(1, count)]
    total = slices * count
    grads = call(
        functools.partial(wave_body, count),
        (window,) * count,
        (fwd, bwd, probe_wave, measured[0], *arrived),
        scratch=(
            pltpu.VMEM((count, slices, 2, points, points), BF16),
            pltpu.VMEM((total, 2, points, points), F32),
            pltpu.VMEM((count, slices, 2, points, points), BF16),
        ),
        flops=36 * 8 * 2 * points**3,
        name="waves",
    )
    returned = [grads[0]] + [depth_shift(grads[k], k) for k in range(1, count)]
    inner, left, right = call(
        functools.partial(deposit_body, count),
        (sds(slices, 2, size + 2 * RIM, size, dtype=F32), rim_cols, rim_cols),
        (pos, *returned),
        specs=[SMEM] + [VMEM] * count,
        scratch=(ext,),
        name="deposit",
    )
    from_right = column_shift(left, -1)
    from_left = column_shift(right, 1)
    up, down = call(
        row_body, (rim_rows, rim_rows), (inner, from_left, from_right), name="row_rims"
    )
    from_below = row_shift(up, -1)
    from_above = row_shift(down, 1)
    gradient = call(
        finish_body,
        sds(2, slices, size, size, dtype=F32),
        (inner, from_left, from_right, from_above, from_below),
        name="finish",
    )
    return gradient[:, :, None]


def solution(mesh):
    in_specs = (
        P("depth", "tile", None, None),
        P("depth", "tile", None, None),
        P(),
        P(),
        P("tile", None, None),
        P("tile", None, None, None),
    )
    out_specs = P(None, "depth", "tile", None, None)
    return jax.shard_map(shards, mesh=mesh, in_specs=in_specs, out_specs=out_specs, check_vma=False)
```

profile of v0, /device:TPU:34, one launch (start us, length us, event | category | flops | bytes accessed | tf_op | source)
XLA Modules:
  0.0 94.0 jit_solution(15327709666792020197)
XLA Ops:
  0.0 0.0 copy-start.7
  0.0 1.1 %copy-done = f32[2,1,256,256]{3,2,1,0:T(8,128)S(1)} copy-done((f32[2,1,256,256]{3,2,1,0:T(8,128)S(1)}, f32[2,1,256,256]{3,2,1,0:T(8,128)}, u32[]{:S(2)}) %copy-start) | copy-done | bytes 524312
  1.1 1.0 %copy-done.1 = f32[2,1,256,256]{3,2,1,0:T(8,128)S(1)} copy-done((f32[2,1,256,256]{3,2,1,0:T(8,128)S(1)}, f32[2,1,256,256]{3,2,1,0:T(8,128)}, u32[]{:S(2)}) %copy-start.1) | copy-done | bytes 524312
  2.1 0.7 transmit.1
  2.9 0.0 copy-start.2
  2.9 0.0 copy-start.3
  2.9 5.2 %collective-permute-start = (bf16[2,2,64,256]{3,2,1,0:T(8,128)(2,1)S(1)}, bf16[2,2,64,256]{3,2,1,0:T(8,128)(2,1)S(1)}, u32[]{:S(2)}, u32[]{:S(2)}) collective-permute-start(bf16[2,2,64,256]{3,2,1,0:T(8,128)(2,1)S(1)} %get-tuple-element.28), channel_id=1, source_target_pairs={{0,8},{1,9},{2,10},{3,11},{4,12},{5,13},{6,14},{7,15},{8,16},{9,17... | collective-permute-start | bytes 393224 | tf_op jit(solution)/shard_map/ppermute | solution.py:339
  8.1 3.1 %collective-permute-start.1 = (bf16[2,2,64,256]{3,2,1,0:T(8,128)(2,1)S(1)}, bf16[2,2,64,256]{3,2,1,0:T(8,128)(2,1)S(1)}, u32[]{:S(2)}, u32[]{:S(2)}) collective-permute-start(bf16[2,2,64,256]{3,2,1,0:T(8,128)(2,1)S(1)} %get-tuple-element.29), channel_id=1, source_target_pairs={{8,0},{9,1},{10,2},{11,3},{12,4},{13,5},{14,6},{15,7},{16,8},{17,9... | collective-permute-start | bytes 393224 | tf_op jit(solution)/shard_map/ppermute | solution.py:339
  11.3 1.3 %collective-permute-done.above_ref = bf16[2,2,64,256]{3,2,1,0:T(8,128)(2,1)S(1)} collective-permute-done((bf16[2,2,64,256]{3,2,1,0:T(8,128)(2,1)S(1)}, bf16[2,2,64,256]{3,2,1,0:T(8,128)(2,1)S(1)}, u32[]{:S(2)}, u32[]{:S(2)}) %collective-permute-start) | collective-permute-done | bytes 131104 | tf_op jit(solution)/shard_map/ppermute | solution.py:339
  12.5 3.9 %collective-permute-done.1.below_ref = bf16[2,2,64,256]{3,2,1,0:T(8,128)(2,1)S(1)} collective-permute-done((bf16[2,2,64,256]{3,2,1,0:T(8,128)(2,1)S(1)}, bf16[2,2,64,256]{3,2,1,0:T(8,128)(2,1)S(1)}, u32[]{:S(2)}, u32[]{:S(2)}) %collective-permute-start.1) | collective-permute-done | bytes 131104 | tf_op jit(solution)/shard_map/ppermute | solution.py:339
  16.5 0.2 column_rims.1
  16.7 1.9 %collective-permute-start.2 = (bf16[2,384,128]{2,1,0:T(8,128)(2,1)S(1)}, bf16[2,384,128]{2,1,0:T(8,128)(2,1)S(1)}, u32[]{:S(2)}, u32[]{:S(2)}) collective-permute-start(bf16[2,384,128]{2,1,0:T(8,128)(2,1)S(1)} %get-tuple-element.30), channel_id=1, source_target_pairs={{0,1},{1,2},{2,3},{3,4},{4,5},{5,6},{6,7},{8,9},{9,10},{10,11},{11... | collective-permute-start | bytes 589832 | tf_op jit(solution)/shard_map/ppermute | solution.py:343
  18.6 3.6 %collective-permute-start.3 = (bf16[2,384,128]{2,1,0:T(8,128)(2,1)S(1)}, bf16[2,384,128]{2,1,0:T(8,128)(2,1)S(1)}, u32[]{:S(2)}, u32[]{:S(2)}) collective-permute-start(bf16[2,384,128]{2,1,0:T(8,128)(2,1)S(1)} %get-tuple-element.31), channel_id=1, source_target_pairs={{1,0},{2,1},{3,2},{4,3},{5,4},{6,5},{7,6},{9,8},{10,9},{11,10},{12... | collective-permute-start | bytes 589832 | tf_op jit(solution)/shard_map/ppermute | solution.py:343
  22.2 0.0 copy-done.7
  22.3 0.1 copy.10.pos_ref
  22.3 1.3 %collective-permute-done.2.lrim_ref = bf16[2,384,128]{2,1,0:T(8,128)(2,1)S(1)} collective-permute-done((bf16[2,384,128]{2,1,0:T(8,128)(2,1)S(1)}, bf16[2,384,128]{2,1,0:T(8,128)(2,1)S(1)}, u32[]{:S(2)}, u32[]{:S(2)}) %collective-permute-start.2) | collective-permute-done | bytes 196640 | tf_op jit(solution)/shard_map/ppermute | solution.py:343
  23.7 1.8 %collective-permute-done.3.rrim_ref = bf16[2,384,128]{2,1,0:T(8,128)(2,1)S(1)} collective-permute-done((bf16[2,384,128]{2,1,0:T(8,128)(2,1)S(1)}, bf16[2,384,128]{2,1,0:T(8,128)(2,1)S(1)}, u32[]{:S(2)}, u32[]{:S(2)}) %collective-permute-start.3) | collective-permute-done | bytes 196640 | tf_op jit(solution)/shard_map/ppermute | solution.py:343
  25.4 1.1 %cut.1 = (bf16[2,2,128,128]{3,2,1,0:T(8,128)(2,1)S(1)}, bf16[2,2,128,128]{3,2,1,0:T(8,128)(2,1)S(1)}, bf16[2,2,128,128]{3,2,1,0:T(8,128)(2,1)S(1)}, bf16[2,2,128,128]{3,2,1,0:T(8,128)(2,1)S(1)}) custom-call(s32[4,2]{1,0:T(4,128)S(1)} %copy.10.pos_ref, bf16[2,2,256,256]{3,2,1,0:T(8,128)(2,1)S(1)} %get-tuple-element.27.t_ref, ...), custom_call_target="tpu_custom_call" | custom-call | bytes 1703968 | tf_op jit(solution)/shard_map/cut/pallas_call | solution.py:24
  26.6 3.3 %collective-permute-start.4 = (bf16[2,2,128,128]{3,2,1,0:T(8,128)(2,1)S(1)}, bf16[2,2,128,128]{3,2,1,0:T(8,128)(2,1)S(1)}, u32[]{:S(2)}, u32[]{:S(2)}) collective-permute-start(bf16[2,2,128,128]{3,2,1,0:T(8,128)(2,1)S(1)} %get-tuple-element.33), channel_id=1, source_target_pairs={{0,64},{64,128},{128,192},{192,0},{1,65},{65,129},{129,193},{193,1... | collective-permute-start | bytes 393224 | tf_op jit(solution)/shard_map/ppermute | solution.py:346
  29.9 4.5 %collective-permute-start.5 = (bf16[2,2,128,128]{3,2,1,0:T(8,128)(2,1)S(1)}, bf16[2,2,128,128]{3,2,1,0:T(8,128)(2,1)S(1)}, u32[]{:S(2)}, u32[]{:S(2)}) collective-permute-start(bf16[2,2,128,128]{3,2,1,0:T(8,128)(2,1)S(1)} %get-tuple-element.34), channel_id=1, source_target_pairs={{0,128},{64,192},{128,0},{192,64},{1,129},{65,193},{129,1},{193,65... | collective-permute-start | bytes 393224 | tf_op jit(solution)/shard_map/ppermute | solution.py:346
  34.4 2.7 %collective-permute-start.6 = (bf16[2,2,128,128]{3,2,1,0:T(8,128)(2,1)S(1)}, bf16[2,2,128,128]{3,2,1,0:T(8,128)(2,1)S(1)}, u32[]{:S(2)}, u32[]{:S(2)}) collective-permute-start(bf16[2,2,128,128]{3,2,1,0:T(8,128)(2,1)S(1)} %get-tuple-element.35), channel_id=1, source_target_pairs={{0,192},{64,0},{128,64},{192,128},{1,193},{65,1},{129,65},{193,129... | collective-permute-start | bytes 393224 | tf_op jit(solution)/shard_map/ppermute | solution.py:346
  37.1 0.0 copy-done.4
  37.1 0.0 copy-done.5
  37.1 0.0 copy-done.6
  37.1 0.7 operators.1
  37.8 1.4 %collective-permute-done.4.rest_1_ = bf16[2,2,128,128]{3,2,1,0:T(8,128)(2,1)S(1)} collective-permute-done((bf16[2,2,128,128]{3,2,1,0:T(8,128)(2,1)S(1)}, bf16[2,2,128,128]{3,2,1,0:T(8,128)(2,1)S(1)}, u32[]{:S(2)}, u32[]{:S(2)}) %collective-permute-start.4) | collective-permute-done | bytes 131104 | tf_op jit(solution)/shard_map/ppermute | solution.py:346
  39.2 4.8 %collective-permute-done.5.rest_2_ = bf16[2,2,128,128]{3,2,1,0:T(8,128)(2,1)S(1)} collective-permute-done((bf16[2,2,128,128]{3,2,1,0:T(8,128)(2,1)S(1)}, bf16[2,2,128,128]{3,2,1,0:T(8,128)(2,1)S(1)}, u32[]{:S(2)}, u32[]{:S(2)}) %collective-permute-start.5) | collective-permute-done | bytes 131104 | tf_op jit(solution)/shard_map/ppermute | solution.py:346
  44.0 2.3 %collective-permute-done.6.rest_3_ = bf16[2,2,128,128]{3,2,1,0:T(8,128)(2,1)S(1)} collective-permute-done((bf16[2,2,128,128]{3,2,1,0:T(8,128)(2,1)S(1)}, bf16[2,2,128,128]{3,2,1,0:T(8,128)(2,1)S(1)}, u32[]{:S(2)}, u32[]{:S(2)}) %collective-permute-start.6) | collective-permute-done | bytes 131104 | tf_op jit(solution)/shard_map/ppermute | solution.py:346
  46.3 0.0 copy-done.2
  46.3 0.0 copy-done.3
  46.3 6.5 %waves.1 = (bf16[2,2,128,128]{3,2,1,0:T(8,128)(2,1)S(1)}, bf16[2,2,128,128]{3,2,1,0:T(8,128)(2,1)S(1)}, bf16[2,2,128,128]{3,2,1,0:T(8,128)(2,1)S(1)}, bf16[2,2,128,128]{3,2,1,0:T(8,128)(2,1)S(1)}) custom-call(bf16[4,2,256,256]{3,2,1,0:T(8,128)(2,1)S(1)} %get-tuple-element.25.fwd_ref, bf16[4,256,256]{2,1,0:T(8,128)(2,1)S(1)} %get-tuple-element.26.bwd_ref, ...), custom_call_target="tpu_custom_call" | custom-call | flops 1207959552 | bytes 3014656 | tf_op jit(solution)/shard_map/waves/pallas_call | solution.py:24
  52.8 2.0 %collective-permute-start.7 = (bf16[2,2,128,128]{3,2,1,0:T(8,128)(2,1)S(1)}, bf16[2,2,128,128]{3,2,1,0:T(8,128)(2,1)S(1)}, u32[]{:S(2)}, u32[]{:S(2)}) collective-permute-start(bf16[2,2,128,128]{3,2,1,0:T(8,128)(2,1)S(1)} %get-tuple-element.37), channel_id=1, source_target_pairs={{0,64},{64,128},{128,192},{192,0},{1,65},{65,129},{129,193},{193,1... | collective-permute-start | bytes 393224 | tf_op jit(solution)/shard_map/ppermute | solution.py:346
  54.8 3.7 %collective-permute-start.8 = (bf16[2,2,128,128]{3,2,1,0:T(8,128)(2,1)S(1)}, bf16[2,2,128,128]{3,2,1,0:T(8,128)(2,1)S(1)}, u32[]{:S(2)}, u32[]{:S(2)}) collective-permute-start(bf16[2,2,128,128]{3,2,1,0:T(8,128)(2,1)S(1)} %get-tuple-element.38), channel_id=1, source_target_pairs={{0,128},{64,192},{128,0},{192,64},{1,129},{65,193},{129,1},{193,65... | collective-permute-start | bytes 393224 | tf_op jit(solution)/shard_map/ppermute | solution.py:346
  58.5 3.5 %collective-permute-start.9 = (bf16[2,2,128,128]{3,2,1,0:T(8,128)(2,1)S(1)}, bf16[2,2,128,128]{3,2,1,0:T(8,128)(2,1)S(1)}, u32[]{:S(2)}, u32[]{:S(2)}) collective-permute-start(bf16[2,2,128,128]{3,2,1,0:T(8,128)(2,1)S(1)} %get-tuple-element.39), channel_id=1, source_target_pairs={{0,192},{64,0},{128,64},{192,128},{1,193},{65,1},{129,65},{193,129... | collective-permute-start | bytes 393224 | tf_op jit(solution)/shard_map/ppermute | solution.py:346
  62.0 3.9 %collective-permute-done.7.rest_1_ = bf16[2,2,128,128]{3,2,1,0:T(8,128)(2,1)S(1)} collective-permute-done((bf16[2,2,128,128]{3,2,1,0:T(8,128)(2,1)S(1)}, bf16[2,2,128,128]{3,2,1,0:T(8,128)(2,1)S(1)}, u32[]{:S(2)}, u32[]{:S(2)}) %collective-permute-start.7) | collective-permute-done | bytes 131104 | tf_op jit(solution)/shard_map/ppermute | solution.py:346
  65.9 3.2 %collective-permute-done.8.rest_2_ = bf16[2,2,128,128]{3,2,1,0:T(8,128)(2,1)S(1)} collective-permute-done((bf16[2,2,128,128]{3,2,1,0:T(8,128)(2,1)S(1)}, bf16[2,2,128,128]{3,2,1,0:T(8,128)(2,1)S(1)}, u32[]{:S(2)}, u32[]{:S(2)}) %collective-permute-start.8) | collective-permute-done | bytes 131104 | tf_op jit(solution)/shard_map/ppermute | solution.py:346
  69.1 0.1 collective-permute-done.9.rest_3_
  69.2 1.2 %deposit.1 = (f32[2,2,384,256]{3,2,1,0:T(8,128)S(1)}, bf16[2,384,128]{2,1,0:T(8,128)(2,1)S(1)}, bf16[2,384,128]{2,1,0:T(8,128)(2,1)S(1)}) custom-call(s32[4,2]{1,0:T(4,128)S(1)} %copy.10.pos_ref, bf16[2,2,128,128]{3,2,1,0:T(8,128)(2,1)S(1)} %get-tuple-element.36.rest_0_, bf16[2,2,128,128]{3,2,1,0:T(8,128)(2,1)S(1)} %collective-permute-done.7.rest_1_, ...), custom_call_target="tpu_custom_call" | custom-call | bytes 2490400 | tf_op jit(solution)/shard_map/deposit/pallas_call | solution.py:24
  70.5 1.9 %collective-permute-start.10 = (bf16[2,384,128]{2,1,0:T(8,128)(2,1)S(1)}, bf16[2,384,128]{2,1,0:T(8,128)(2,1)S(1)}, u32[]{:S(2)}, u32[]{:S(2)}) collective-permute-start(bf16[2,384,128]{2,1,0:T(8,128)(2,1)S(1)} %get-tuple-element.41), channel_id=1, source_target_pairs={{0,1},{1,2},{2,3},{3,4},{4,5},{5,6},{6,7},{8,9},{9,10},{10,11},{11... | collective-permute-start | bytes 589832 | tf_op jit(solution)/shard_map/ppermute | solution.py:343
  72.4 3.9 %collective-permute-start.11 = (bf16[2,384,128]{2,1,0:T(8,128)(2,1)S(1)}, bf16[2,384,128]{2,1,0:T(8,128)(2,1)S(1)}, u32[]{:S(2)}, u32[]{:S(2)}) collective-permute-start(bf16[2,384,128]{2,1,0:T(8,128)(2,1)S(1)} %get-tuple-element.42), channel_id=1, source_target_pairs={{1,0},{2,1},{3,2},{4,3},{5,4},{6,5},{7,6},{9,8},{10,9},{11,10},{12... | collective-permute-start | bytes 589832 | tf_op jit(solution)/shard_map/ppermute | solution.py:343
  76.4 1.4 %collective-permute-done.10.left_ref = bf16[2,384,128]{2,1,0:T(8,128)(2,1)S(1)} collective-permute-done((bf16[2,384,128]{2,1,0:T(8,128)(2,1)S(1)}, bf16[2,384,128]{2,1,0:T(8,128)(2,1)S(1)}, u32[]{:S(2)}, u32[]{:S(2)}) %collective-permute-start.10) | collective-permute-done | bytes 196640 | tf_op jit(solution)/shard_map/ppermute | solution.py:343
  77.8 1.8 %collective-permute-done.11.right_ref = bf16[2,384,128]{2,1,0:T(8,128)(2,1)S(1)} collective-permute-done((bf16[2,384,128]{2,1,0:T(8,128)(2,1)S(1)}, bf16[2,384,128]{2,1,0:T(8,128)(2,1)S(1)}, u32[]{:S(2)}, u32[]{:S(2)}) %collective-permute-start.11) | collective-permute-done | bytes 196640 | tf_op jit(solution)/shard_map/ppermute | solution.py:343
  79.5 0.1 row_rims.1
  79.7 3.7 %collective-permute-start.12 = (bf16[2,2,64,256]{3,2,1,0:T(8,128)(2,1)S(1)}, bf16[2,2,64,256]{3,2,1,0:T(8,128)(2,1)S(1)}, u32[]{:S(2)}, u32[]{:S(2)}) collective-permute-start(bf16[2,2,64,256]{3,2,1,0:T(8,128)(2,1)S(1)} %get-tuple-element.43), channel_id=1, source_target_pairs={{0,8},{1,9},{2,10},{3,11},{4,12},{5,13},{6,14},{7,15},{8,16},{9,17... | collective-permute-start | bytes 393224 | tf_op jit(solution)/shard_map/ppermute | solution.py:339
  83.4 4.5 %collective-permute-start.13 = (bf16[2,2,64,256]{3,2,1,0:T(8,128)(2,1)S(1)}, bf16[2,2,64,256]{3,2,1,0:T(8,128)(2,1)S(1)}, u32[]{:S(2)}, u32[]{:S(2)}) collective-permute-start(bf16[2,2,64,256]{3,2,1,0:T(8,128)(2,1)S(1)} %get-tuple-element.44), channel_id=1, source_target_pairs={{8,0},{9,1},{10,2},{11,3},{12,4},{13,5},{14,6},{15,7},{16,8},{17,9... | collective-permute-start | bytes 393224 | tf_op jit(solution)/shard_map/ppermute | solution.py:339
  87.9 2.1 %collective-permute-done.12.above_ref = bf16[2,2,64,256]{3,2,1,0:T(8,128)(2,1)S(1)} collective-permute-done((bf16[2,2,64,256]{3,2,1,0:T(8,128)(2,1)S(1)}, bf16[2,2,64,256]{3,2,1,0:T(8,128)(2,1)S(1)}, u32[]{:S(2)}, u32[]{:S(2)}) %collective-permute-start.12) | collective-permute-done | bytes 131104 | tf_op jit(solution)/shard_map/ppermute | solution.py:339
  90.0 2.8 %collective-permute-done.13.below_ref = bf16[2,2,64,256]{3,2,1,0:T(8,128)(2,1)S(1)} collective-permute-done((bf16[2,2,64,256]{3,2,1,0:T(8,128)(2,1)S(1)}, bf16[2,2,64,256]{3,2,1,0:T(8,128)(2,1)S(1)}, u32[]{:S(2)}, u32[]{:S(2)}) %collective-permute-start.13) | collective-permute-done | bytes 131104 | tf_op jit(solution)/shard_map/ppermute | solution.py:339
  92.8 1.2 %finish.1 = f32[2,2,256,256]{3,2,1,0:T(8,128)} custom-call(f32[2,2,384,256]{3,2,1,0:T(8,128)S(1)} %get-tuple-element.40.inner_ref, bf16[2,384,128]{2,1,0:T(8,128)(2,1)S(1)} %collective-permute-done.10.left_ref, bf16[2,384,128]{2,1,0:T(8,128)(2,1)S(1)} %collective-permute-done.11.right_ref, bf16[2,2,64,256]{3,2,1,0:T(8,128)(2,1)S(1)} %collective-permute-done.12.above_ref, ...), custom_call_target="tpu_custom_call" | custom-call | bytes 3276800 | tf_op jit(solution)/shard_map/finish/pallas_call | solution.py:24
  (5 shorter events, 0.0 us)
Async XLA Ops:
  0.0 22.2 %copy-start.7 = (s32[1,4,2]{1,2,0:T(2,128)S(1)}, s32[1,4,2]{1,2,0:T(2,128)}, u32[]{:S(2)}) copy-start(s32[1,4,2]{1,2,0:T(2,128)} %param.12) | copy-start | bytes 100
  0.0 37.1 %copy-start.4 = (f32[2,128]{1,0:T(2,128)S(1)}, f32[2,128]{1,0:T(2,128)}, u32[]{:S(2)}) copy-start(f32[2,128]{1,0:T(2,128)} %phase_ref.1) | copy-start | bytes 3076
  0.0 1.1 %copy-start = (f32[2,1,256,256]{3,2,1,0:T(8,128)S(1)}, f32[2,1,256,256]{3,2,1,0:T(8,128)}, u32[]{:S(2)}) copy-start(f32[2,1,256,256]{3,2,1,0:T(8,128)} %param.8) | copy-start | bytes 1572868
  1.1 1.0 %copy-start.1 = (f32[2,1,256,256]{3,2,1,0:T(8,128)S(1)}, f32[2,1,256,256]{3,2,1,0:T(8,128)}, u32[]{:S(2)}) copy-start(f32[2,1,256,256]{3,2,1,0:T(8,128)} %param.9) | copy-start | bytes 1572868
  2.1 35.0 %copy-start.5 = (f32[128,128]{1,0:T(8,128)S(1)}, f32[128,128]{1,0:T(8,128)}, u32[]{:S(2)}) copy-start(f32[128,128]{1,0:T(8,128)} %constant.5.clone.dft_imag_ref) | copy-start | bytes 196612
  2.1 35.0 %copy-start.6 = (f32[128,128]{1,0:T(8,128)S(1)}, f32[128,128]{1,0:T(8,128)}, u32[]{:S(2)}) copy-start(f32[128,128]{1,0:T(8,128)} %constant.4.clone.dft_real_ref) | copy-start | bytes 196612
  2.9 43.4 %copy-start.2 = (f32[1,4,128,128]{3,2,1,0:T(8,128)S(1)}, f32[1,4,128,128]{3,2,1,0:T(8,128)}, u32[]{:S(2)}) copy-start(f32[1,4,128,128]{3,2,1,0:T(8,128)} %param.13) | copy-start | bytes 786436
  2.9 43.4 %copy-start.3 = (f32[2,128,128]{2,1,0:T(8,128)S(1)}, f32[2,128,128]{2,1,0:T(8,128)}, u32[]{:S(2)}) copy-start(f32[2,128,128]{2,1,0:T(8,128)} %probe_ref.1) | copy-start | bytes 393220
  2.9 9.7 %collective-permute-start = (bf16[2,2,64,256]{3,2,1,0:T(8,128)(2,1)S(1)}, bf16[2,2,64,256]{3,2,1,0:T(8,128)(2,1)S(1)}, u32[]{:S(2)}, u32[]{:S(2)}) collective-permute-start(bf16[2,2,64,256]{3,2,1,0:T(8,128)(2,1)S(1)} %get-tuple-element.28), channel_id=1, source_target_pairs={{0,8},{1,9},{2,10},{3,11},{4,12},{5,13},{6,14},{7,15},{8,16},{9,17... | collective-permute-start | bytes 393224 | tf_op jit(solution)/shard_map/ppermute | solution.py:339
  8.1 8.4 %collective-permute-start.1 = (bf16[2,2,64,256]{3,2,1,0:T(8,128)(2,1)S(1)}, bf16[2,2,64,256]{3,2,1,0:T(8,128)(2,1)S(1)}, u32[]{:S(2)}, u32[]{:S(2)}) collective-permute-start(bf16[2,2,64,256]{3,2,1,0:T(8,128)(2,1)S(1)} %get-tuple-element.29), channel_id=1, source_target_pairs={{8,0},{9,1},{10,2},{11,3},{12,4},{13,5},{14,6},{15,7},{16,8},{17,9... | collective-permute-start | bytes 393224 | tf_op jit(solution)/shard_map/ppermute | solution.py:339
  16.7 7.0 %collective-permute-start.2 = (bf16[2,384,128]{2,1,0:T(8,128)(2,1)S(1)}, bf16[2,384,128]{2,1,0:T(8,128)(2,1)S(1)}, u32[]{:S(2)}, u32[]{:S(2)}) collective-permute-start(bf16[2,384,128]{2,1,0:T(8,128)(2,1)S(1)} %get-tuple-element.30), channel_id=1, source_target_pairs={{0,1},{1,2},{2,3},{3,4},{4,5},{5,6},{6,7},{8,9},{9,10},{10,11},{11... | collective-permute-start | bytes 589832 | tf_op jit(solution)/shard_map/ppermute | solution.py:343
  18.6 6.8 %collective-permute-start.3 = (bf16[2,384,128]{2,1,0:T(8,128)(2,1)S(1)}, bf16[2,384,128]{2,1,0:T(8,128)(2,1)S(1)}, u32[]{:S(2)}, u32[]{:S(2)}) collective-permute-start(bf16[2,384,128]{2,1,0:T(8,128)(2,1)S(1)} %get-tuple-element.31), channel_id=1, source_target_pairs={{1,0},{2,1},{3,2},{4,3},{5,4},{6,5},{7,6},{9,8},{10,9},{11,10},{12... | collective-permute-start | bytes 589832 | tf_op jit(solution)/shard_map/ppermute | solution.py:343
  26.6 12.6 %collective-permute-start.4 = (bf16[2,2,128,128]{3,2,1,0:T(8,128)(2,1)S(1)}, bf16[2,2,128,128]{3,2,1,0:T(8,128)(2,1)S(1)}, u32[]{:S(2)}, u32[]{:S(2)}) collective-permute-start(bf16[2,2,128,128]{3,2,1,0:T(8,128)(2,1)S(1)} %get-tuple-element.33), channel_id=1, source_target_pairs={{0,64},{64,128},{128,192},{192,0},{1,65},{65,129},{129,193},{193,1... | collective-permute-start | bytes 393224 | tf_op jit(solution)/shard_map/ppermute | solution.py:346
  29.9 14.1 %collective-permute-start.5 = (bf16[2,2,128,128]{3,2,1,0:T(8,128)(2,1)S(1)}, bf16[2,2,128,128]{3,2,1,0:T(8,128)(2,1)S(1)}, u32[]{:S(2)}, u32[]{:S(2)}) collective-permute-start(bf16[2,2,128,128]{3,2,1,0:T(8,128)(2,1)S(1)} %get-tuple-element.34), channel_id=1, source_target_pairs={{0,128},{64,192},{128,0},{192,64},{1,129},{65,193},{129,1},{193,65... | collective-permute-start | bytes 393224 | tf_op jit(solution)/shard_map/ppermute | solution.py:346
  34.4 11.9 %collective-permute-start.6 = (bf16[2,2,128,128]{3,2,1,0:T(8,128)(2,1)S(1)}, bf16[2,2,128,128]{3,2,1,0:T(8,128)(2,1)S(1)}, u32[]{:S(2)}, u32[]{:S(2)}) collective-permute-start(bf16[2,2,128,128]{3,2,1,0:T(8,128)(2,1)S(1)} %get-tuple-element.35), channel_id=1, source_target_pairs={{0,192},{64,0},{128,64},{192,128},{1,193},{65,1},{129,65},{193,129... | collective-permute-start | bytes 393224 | tf_op jit(solution)/shard_map/ppermute | solution.py:346
  52.8 13.1 %collective-permute-start.7 = (bf16[2,2,128,128]{3,2,1,0:T(8,128)(2,1)S(1)}, bf16[2,2,128,128]{3,2,1,0:T(8,128)(2,1)S(1)}, u32[]{:S(2)}, u32[]{:S(2)}) collective-permute-start(bf16[2,2,128,128]{3,2,1,0:T(8,128)(2,1)S(1)} %get-tuple-element.37), channel_id=1, source_target_pairs={{0,64},{64,128},{128,192},{192,0},{1,65},{65,129},{129,193},{193,1... | collective-permute-start | bytes 393224 | tf_op jit(solution)/shard_map/ppermute | solution.py:346
  54.8 14.3 %collective-permute-start.8 = (bf16[2,2,128,128]{3,2,1,0:T(8,128)(2,1)S(1)}, bf16[2,2,128,128]{3,2,1,0:T(8,128)(2,1)S(1)}, u32[]{:S(2)}, u32[]{:S(2)}) collective-permute-start(bf16[2,2,128,128]{3,2,1,0:T(8,128)(2,1)S(1)} %get-tuple-element.38), channel_id=1, source_target_pairs={{0,128},{64,192},{128,0},{192,64},{1,129},{65,193},{129,1},{193,65... | collective-permute-start | bytes 393224 | tf_op jit(solution)/shard_map/ppermute | solution.py:346
  58.5 10.8 %collective-permute-start.9 = (bf16[2,2,128,128]{3,2,1,0:T(8,128)(2,1)S(1)}, bf16[2,2,128,128]{3,2,1,0:T(8,128)(2,1)S(1)}, u32[]{:S(2)}, u32[]{:S(2)}) collective-permute-start(bf16[2,2,128,128]{3,2,1,0:T(8,128)(2,1)S(1)} %get-tuple-element.39), channel_id=1, source_target_pairs={{0,192},{64,0},{128,64},{192,128},{1,193},{65,1},{129,65},{193,129... | collective-permute-start | bytes 393224 | tf_op jit(solution)/shard_map/ppermute | solution.py:346
  70.5 7.3 %collective-permute-start.10 = (bf16[2,384,128]{2,1,0:T(8,128)(2,1)S(1)}, bf16[2,384,128]{2,1,0:T(8,128)(2,1)S(1)}, u32[]{:S(2)}, u32[]{:S(2)}) collective-permute-start(bf16[2,384,128]{2,1,0:T(8,128)(2,1)S(1)} %get-tuple-element.41), channel_id=1, source_target_pairs={{0,1},{1,2},{2,3},{3,4},{4,5},{5,6},{6,7},{8,9},{9,10},{10,11},{11... | collective-permute-start | bytes 589832 | tf_op jit(solution)/shard_map/ppermute | solution.py:343
  72.4 7.1 %collective-permute-start.11 = (bf16[2,384,128]{2,1,0:T(8,128)(2,1)S(1)}, bf16[2,384,128]{2,1,0:T(8,128)(2,1)S(1)}, u32[]{:S(2)}, u32[]{:S(2)}) collective-permute-start(bf16[2,384,128]{2,1,0:T(8,128)(2,1)S(1)} %get-tuple-element.42), channel_id=1, source_target_pairs={{1,0},{2,1},{3,2},{4,3},{5,4},{6,5},{7,6},{9,8},{10,9},{11,10},{12... | collective-permute-start | bytes 589832 | tf_op jit(solution)/shard_map/ppermute | solution.py:343
  79.7 10.3 %collective-permute-start.12 = (bf16[2,2,64,256]{3,2,1,0:T(8,128)(2,1)S(1)}, bf16[2,2,64,256]{3,2,1,0:T(8,128)(2,1)S(1)}, u32[]{:S(2)}, u32[]{:S(2)}) collective-permute-start(bf16[2,2,64,256]{3,2,1,0:T(8,128)(2,1)S(1)} %get-tuple-element.43), channel_id=1, source_target_pairs={{0,8},{1,9},{2,10},{3,11},{4,12},{5,13},{6,14},{7,15},{8,16},{9,17... | collective-permute-start | bytes 393224 | tf_op jit(solution)/shard_map/ppermute | solution.py:339
  83.4 9.4 %collective-permute-start.13 = (bf16[2,2,64,256]{3,2,1,0:T(8,128)(2,1)S(1)}, bf16[2,2,64,256]{3,2,1,0:T(8,128)(2,1)S(1)}, u32[]{:S(2)}, u32[]{:S(2)}) collective-permute-start(bf16[2,2,64,256]{3,2,1,0:T(8,128)(2,1)S(1)} %get-tuple-element.44), channel_id=1, source_target_pairs={{8,0},{9,1},{10,2},{11,3},{12,4},{13,5},{14,6},{15,7},{16,8},{17,9... | collective-permute-start | bytes 393224 | tf_op jit(solution)/shard_map/ppermute | solution.py:339
where the time goes:
time: 95.1 us; the launch traced here: 94 us
  starting transfers between devices  47.8 us (50%)
  waiting for transfers between devices  32 us (34%)
  Pallas kernels  11.9 us (13%)
  local copies, waits for them, and re-layouts  2.23 us (2%)
    ppermute x6, starting transfers between devices, depth_shift(): lax.ppermute(x, 'depth', [(i, (i + by) % count) for i in range(count)])  19.7 us
    ppermute x4, starting transfers between devices, row_shift(): return lax.ppermute(x, 'tile', pairs)  16.6 us
    ppermute x6, waiting for transfers between devices, depth_shift(): lax.ppermute(x, 'depth', [(i, (i + by) % count) for i in range(count)])  15.7 us
    pallas_call x8, Pallas kernels, call(): pl.pallas_call(body, out_shape=out_shape, in_specs=specs or [VMEM] * len(...  11.9 us
    ppermute x4, starting transfers between devices, column_shift(): return lax.ppermute(x, 'tile', pairs)  11.4 us
    ppermute x4, waiting for transfers between devices, row_shift(): return lax.ppermute(x, 'tile', pairs)  10.1 us
    ppermute x4, waiting for transfers between devices, column_shift(): return lax.ppermute(x, 'tile', pairs)  6.23 us
    unnamed x16, local copies, waits for them, and re-layouts  2.13 us
  transfers between devices with their start and end apart: 14, of which 14 were waited for; matrix products, arithmetic and copies ran while one was open for 0% of the time, Pallas kernels for 1%

commit v1 on v0

v1 whole, which is shorter than its diff:
```python
import functools
import math

import jax
import jax.numpy as jnp
import numpy as np
from jax import lax
from jax.experimental import pallas as pl
from jax.experimental.pallas import tpu as pltpu
from jax.sharding import PartitionSpec as P

RIM = 64
LANES = 128
F32 = jnp.float32
BF16 = jnp.bfloat16
VMEM = pl.BlockSpec(memory_space=pltpu.VMEM)
SMEM = pl.BlockSpec(memory_space=pltpu.SMEM)
HBM = pl.BlockSpec(memory_space=pltpu.MemorySpace.HBM)


def call(body, out_shape, inputs, specs=None, outs=VMEM, scratch=(), flops=0, aliases=None, name=None):
    out_specs = jax.tree.map(lambda _: outs, out_shape)
    moved = sum(x.size * x.dtype.itemsize for x in inputs)
    moved += sum(x.size * x.dtype.itemsize for x in jax.tree.leaves(out_shape))
    return pl.pallas_call(
        body,
        out_shape=out_shape,
        in_specs=specs or [VMEM] * len(inputs),
        out_specs=out_specs,
        scratch_shapes=list(scratch),
        compiler_params=pltpu.CompilerParams(vmem_limit_bytes=24 << 20),
        input_output_aliases=aliases or {},
        cost_estimate=pl.CostEstimate(flops=flops, bytes_accessed=moved, transcendentals=0),
        name=name,
    )(*inputs)


def sds(*shape, dtype=BF16):
    return jax.ShapeDtypeStruct(shape, dtype)


def sincos(x):
    y = x * 0.5
    q = y * y
    sine = 1.0
    for n in (11, 9, 7, 5, 3):
        sine = 1.0 - q * sine * (1.0 / (n * (n - 1)))
    sine = sine * y
    cosine = 1.0
    for n in (12, 10, 8, 6, 4, 2):
        cosine = 1.0 - q * cosine * (1.0 / (n * (n - 1)))
    return 2.0 * sine * cosine, 1.0 - 2.0 * sine * sine


def dft_tables(points):
    products = np.outer(np.arange(points), np.arange(points)) % points
    angles = products * (-2.0 * math.pi / points)
    scale = 1.0 / math.sqrt(points)
    return (np.cos(angles) * scale).astype(np.float32), (np.sin(angles) * scale).astype(np.float32)


def odd_row(columns):
    return lax.rem(lax.axis_index("tile") // columns, 2) == 1


def odd_column():
    return lax.rem(lax.axis_index("tile"), 2) == 1


def rim_body(columns, amp_ref, phase_ref, first_ref, second_ref, held, sem):
    slices, size = amp_ref.shape[0], amp_ref.shape[-1]
    odd = odd_row(columns)
    copies = {}
    for block in range(2):
        top = odd if block == 0 else jnp.logical_not(odd)
        start = pl.multiple_of(jnp.where(top, 0, size - RIM), RIM)
        for s in range(slices):
            for i, ref in enumerate((phase_ref, amp_ref)):
                copy = pltpu.make_async_copy(
                    ref.at[s, pl.ds(start, RIM), :], held.at[block, s, i], sem.at[block, s, i]
                )
                copy.start()
                copies[block, s, i] = copy
    for block, out in enumerate((first_ref, second_ref)):
        for s in range(slices):
            copies[block, s, 0].wait()
            sine, cosine = sincos(held[block, s, 0])
            copies[block, s, 1].wait()
            amp = held[block, s, 1]
            out[s, 0] = (amp * cosine).astype(BF16)
            out[s, 1] = (amp * sine).astype(BF16)


def transmit_body(amp_ref, phase_ref, t_ref, held, sem):
    slices = amp_ref.shape[0]
    copies = []
    for s in range(slices):
        for i, ref in enumerate((phase_ref, amp_ref)):
            copies.append(pltpu.make_async_copy(ref.at[s], held.at[s, i], sem.at[s, i]))
            copies[-1].start()
    for s in range(slices):
        copies[2 * s].wait()
        copies[2 * s + 1].wait()
        sine, cosine = sincos(held[s, 0])
        amp = held[s, 1]
        t_ref[s, 0] = (amp * cosine).astype(BF16)
        t_ref[s, 1] = (amp * sine).astype(BF16)


def lane_halves(low, high):
    lane = lax.broadcasted_iota(jnp.int32, low.shape, 1)
    return jnp.where(lane < RIM, low, high)


def swap(x):
    return pltpu.roll(x, RIM, 1)


def column_body(columns, t_ref, row_first_ref, row_second_ref, first_ref, second_ref):
    size = t_ref.shape[-1]
    flip = odd_row(columns)
    odd = odd_column()
    for s in range(t_ref.shape[0]):
        for start, rows in ((0, RIM), (RIM, size), (RIM + size, RIM)):
            dst = pl.ds(start, rows)

            def load(part, lanes):
                if start == RIM:
                    return t_ref[s, part, :, lanes].astype(F32)
                first = row_first_ref[s, part, :, lanes].astype(F32)
                second = row_second_ref[s, part, :, lanes].astype(F32)
                return jnp.where(flip == (start == 0), first, second)

            low, high = slice(0, LANES), slice(size - LANES, size)
            left = lane_halves(load(0, low), swap(load(1, low)))
            right = lane_halves(swap(load(0, high)), load(1, high))
            first_ref[s, dst, :] = jnp.where(odd, right, left).astype(BF16)
            second_ref[s, dst, :] = jnp.where(odd, left, right).astype(BF16)


def extend_body(columns, t_ref, row_first_ref, row_second_ref, ext_ref):
    slices, size = t_ref.shape[0], t_ref.shape[-1]
    flip = odd_row(columns)
    for s in range(slices):
        for part in range(2):
            for tile in range(size // LANES):
                lanes = slice(tile * LANES, (tile + 1) * LANES)
                first = row_first_ref[s, part, :, lanes].astype(F32)
                second = row_second_ref[s, part, :, lanes].astype(F32)
                ext_ref[tile, s, part, :RIM] = jnp.where(flip, first, second)
                ext_ref[tile, s, part, RIM : RIM + size] = t_ref[s, part, :, lanes].astype(F32)
                ext_ref[tile, s, part, RIM + size :] = jnp.where(flip, second, first)


def lane_place(column, size):
    tiles = (size + 2 * RIM) // LANES
    place = jnp.where(column < 0, column + size + 2 * RIM, column)
    first = place // LANES
    second = jnp.where(first == tiles - 1, 0, first + 1)
    return first, second, place % LANES


def cut_body(count, size, pos_ref, rim_first_ref, rim_second_ref, ext_in, ext, *outs):
    del ext_in
    slices = ext.shape[1]
    odd = odd_column()
    for s in range(slices):
        first = rim_first_ref[s].astype(F32)
        second = rim_second_ref[s].astype(F32)
        left = jnp.where(odd, second, first)
        right = jnp.where(odd, first, second)
        ext[size // LANES, s, 0] = lane_halves(right, swap(left))
        ext[size // LANES, s, 1] = lane_halves(swap(right), left)
    depth = lax.axis_index("depth")
    for k in range(count):
        wave = depth ^ k
        row = pos_ref[wave, 0] + RIM
        first, second, shift = lane_place(pos_ref[wave, 1], size)
        turn = lax.rem(LANES - shift, LANES)
        lane = lax.broadcasted_iota(jnp.int32, (LANES, LANES), 1)
        for s in range(slices):
            for part in range(2):
                low = pltpu.roll(ext[first, s, part, pl.ds(row, LANES), :], turn, 1)
                high = pltpu.roll(ext[second, s, part, pl.ds(row, LANES), :], turn, 1)
                outs[k][s, part] = jnp.where(lane < LANES - shift, low, high).astype(BF16)


def operator_body(phase_ref, dft_real_ref, dft_imag_ref, fwd_ref, bwd_ref):
    fr = dft_real_ref[...]
    fi = dft_imag_ref[...]
    n = fr.shape[0]

    def dot(a, b):
        return jnp.dot(a, b, precision=lax.Precision.HIGHEST, preferred_element_type=F32)

    def put(index, real, imag, flip):
        rt, it = real.T, imag.T
        plain = ((real, imag), (-imag, real))
        turned = ((rt, -it), (it, rt))
        for i in range(2):
            for j in range(2):
                rows, cols = pl.ds(i * n, n), pl.ds(j * n, n)
                value = (turned if flip else plain)[i][j]
                high = value.astype(BF16)
                fwd_ref[index, 0, rows, cols] = high
                fwd_ref[index, 1, rows, cols] = (value - high.astype(F32)).astype(BF16)
                bwd_ref[index, rows, cols] = (plain if flip else turned)[i][j].astype(BF16)

    for axis in range(2):
        sine, cosine = sincos(phase_ref[axis : axis + 1, :])
        er = fr * cosine - fi * sine
        ei = fr * sine + fi * cosine
        real = dot(er, fr) + dot(ei, fi)
        imag = dot(ei, fr) - dot(er, fi)
        put(axis, real, imag, axis == 0)
        put(2 + axis, er, ei, axis == 0)


def split(x):
    high = x.astype(BF16)
    return high, (x - high.astype(F32)).astype(BF16)


def mm(a, b):
    return jnp.dot(a, b, preferred_element_type=F32)


def left_fine(fwd_ref, index, real, imag):
    n = real.shape[0]
    high, low = split(jnp.concatenate([real, imag], axis=0))
    both = mm(fwd_ref[index, 0], jnp.concatenate([high, low], axis=1))
    out = both[:, :n] + both[:, n:] + mm(fwd_ref[index, 1], high)
    return out[:n], out[n:]


def right_fine(fwd_ref, index, real, imag):
    n = real.shape[0]
    high, low = split(jnp.concatenate([real, imag], axis=1))
    both = mm(jnp.concatenate([high, low], axis=0), fwd_ref[index, 0])
    out = both[:n] + both[n:] + mm(high, fwd_ref[index, 1])
    return out[:, :n], out[:, n:]


def left_plain(bwd_ref, index, real, imag):
    n = real.shape[0]
    out = mm(bwd_ref[index], jnp.concatenate([real, imag], axis=0).astype(BF16))
    return out[:n], out[n:]


def right_plain(bwd_ref, index, real, imag):
    n = real.shape[0]
    out = mm(jnp.concatenate([real, imag], axis=1).astype(BF16), bwd_ref[index])
    return out[:, :n], out[:, n:]


def wave_body(count, fwd_ref, bwd_ref, probe_ref, measured_ref, *rest):
    windows, outs = rest[:count], rest[count : 2 * count]
    patch, waves, grads = rest[2 * count :]
    depth = lax.axis_index("depth")
    slices = windows[0].shape[0]
    total = slices * count
    for k in range(count):
        patch[depth ^ k] = windows[k][...]

    def patch_of(s):
        group, local = s // slices, s % slices
        return patch[group, local, 0].astype(F32), patch[group, local, 1].astype(F32)

    def mix(s, wr, wi):
        pr, pi = patch_of(s)
        waves[s, 0] = wr
        waves[s, 1] = wi
        return pr * wr - pi * wi, pr * wi + pi * wr

    def forward(s, wave):
        half = left_fine(fwd_ref, 0, *mix(s, *wave))
        return right_fine(fwd_ref, 1, *half)

    wave = lax.fori_loop(0, total - 1, forward, (probe_ref[0], probe_ref[1]))
    half = left_fine(fwd_ref, 2, *mix(total - 1, *wave))
    far_real, far_imag = right_fine(fwd_ref, 3, *half)
    misfit = far_real * far_real + far_imag * far_imag - measured_ref[depth]
    half = left_plain(bwd_ref, 2, misfit * far_real, misfit * far_imag)
    spread = right_plain(bwd_ref, 3, *half)

    def contribute(s, sr, si):
        wr, wi = waves[s, 0], waves[s, 1]
        group, local = s // slices, s % slices
        grads[group, local, 0] = (wr * sr + wi * si).astype(BF16)
        grads[group, local, 1] = (wr * si - wi * sr).astype(BF16)

    def backward(step, spread):
        s = total - 1 - step
        sr, si = spread
        contribute(s, sr, si)
        pr, pi = patch_of(s)
        half = left_plain(bwd_ref, 0, pr * sr + pi * si, pr * si - pi * sr)
        return right_plain(bwd_ref, 1, *half)

    spread = lax.fori_loop(0, total - 1, backward, spread)
    contribute(0, *spread)
    for k in range(count):
        outs[k][...] = grads[depth ^ k]


def deposit_body(count, size, pos_ref, *rest):
    grads = rest[:count]
    ext, first_ref, second_ref = rest[count:]
    tiles = ext.shape[0]
    slices = grads[0].shape[0]
    ext[...] = jnp.zeros_like(ext)
    depth = lax.axis_index("depth")
    odd = odd_column()
    for k in range(count):
        wave = depth ^ k
        row = pos_ref[wave, 0] + RIM
        first, second, shift = lane_place(pos_ref[wave, 1], size)
        lane = lax.broadcasted_iota(jnp.int32, (LANES, LANES), 1)
        rows = pl.ds(row, LANES)
        for s in range(slices):
            for part in range(2):
                moved = pltpu.roll(grads[k][s, part].astype(F32), shift, 1)
                low = jnp.where(lane >= shift, moved, 0.0)
                ext[first, s, part, rows, :] += low
                ext[second, s, part, rows, :] += moved - low
    for s in range(slices):
        real, imag = ext[tiles - 1, s, 0], ext[tiles - 1, s, 1]
        right = lane_halves(real, swap(imag))
        left = lane_halves(swap(real), imag)
        first_ref[s] = jnp.where(odd, right, left).astype(BF16)
        second_ref[s] = jnp.where(odd, left, right).astype(BF16)


def halves_added(odd, ext_ref, rim_first_ref, rim_second_ref, s, part, rows):
    first = rim_first_ref[s, rows, :].astype(F32)
    second = rim_second_ref[s, rows, :].astype(F32)
    left = jnp.where(odd, second, first)
    right = jnp.where(odd, first, second)
    if part == 0:
        right = swap(right)
    else:
        left = swap(left)
    last = ext_ref.shape[0] - 2
    zero = jnp.zeros_like(left)
    return (
        ext_ref[0, s, part, rows, :] + lane_halves(left, zero),
        ext_ref[last, s, part, rows, :] + lane_halves(zero, right),
    )


def row_body(columns, ext_ref, rim_first_ref, rim_second_ref, first_ref, second_ref):
    height = ext_ref.shape[-2]
    odd = odd_column()
    flip = odd_row(columns)
    for s in range(ext_ref.shape[1]):
        for part in range(2):
            refs = (odd, ext_ref, rim_first_ref, rim_second_ref, s, part)
            above = halves_added(*refs, pl.ds(0, RIM))
            below = halves_added(*refs, pl.ds(height - RIM, RIM))
            for tile in range(2):
                lanes = slice(tile * LANES, (tile + 1) * LANES)
                up, down = above[tile], below[tile]
                first_ref[s, part, :, lanes] = jnp.where(flip, up, down).astype(BF16)
                second_ref[s, part, :, lanes] = jnp.where(flip, down, up).astype(BF16)


def put_rows(out_ref, held, sem, blocks):
    copies = []
    for part in range(out_ref.shape[0]):
        for s in range(out_ref.shape[1]):
            at = 0
            for i, (start, rows) in enumerate(blocks):
                copy = pltpu.make_async_copy(
                    held.at[part, s, pl.ds(at, rows), :],
                    out_ref.at[part, s, pl.ds(start, rows), :],
                    sem.at[part, s, i],
                )
                copies.append(copy)
                at += rows
    return copies


def middle_body(ext_ref, rim_first_ref, rim_second_ref, out_ref, held, sem):
    size = out_ref.shape[-1]
    odd = odd_column()
    copies = put_rows(out_ref, held, sem, ((RIM, size - 2 * RIM),))
    for part in range(2):
        for s in range(ext_ref.shape[1]):
            rows = pl.ds(2 * RIM, size - 2 * RIM)
            pieces = halves_added(odd, ext_ref, rim_first_ref, rim_second_ref, s, part, rows)
            for tile, piece in enumerate(pieces):
                held[part, s, :, tile * LANES : (tile + 1) * LANES] = piece
    for copy in copies:
        copy.start()
    for copy in copies:
        copy.wait()


def edge_body(columns, ext_ref, rim_first_ref, rim_second_ref, *rest):
    row_first_ref, row_second_ref, out_in, out_ref, held, sem = rest
    del out_in
    size = out_ref.shape[-1]
    odd = odd_column()
    flip = odd_row(columns)
    blocks = ((0, RIM), (size - RIM, RIM))
    copies = put_rows(out_ref, held, sem, blocks)
    for part in range(2):
        for s in range(ext_ref.shape[1]):
            for i, (start, rows) in enumerate(blocks):
                refs = (odd, ext_ref, rim_first_ref, rim_second_ref, s, part)
                pieces = halves_added(*refs, pl.ds(RIM + start, rows))
                for tile, piece in enumerate(pieces):
                    lanes = slice(tile * LANES, (tile + 1) * LANES)
                    first = row_first_ref[s, part, :, lanes].astype(F32)
                    second = row_second_ref[s, part, :, lanes].astype(F32)
                    piece = piece + jnp.where(flip == (start == 0), first, second)
                    held[part, s, i * RIM : (i + 1) * RIM, lanes] = piece
                copies[(part * ext_ref.shape[1] + s) * 2 + i].start()
    for copy in copies:
        copy.wait()


def shards(amplitude, phase_map, probe_wave, propagator_phase, positions, measured):
    slices, size = amplitude.shape[0], amplitude.shape[-1]
    points = probe_wave.shape[-1]
    count = lax.axis_size("depth")
    tiles = lax.axis_size("tile")
    columns = max(2, tiles // 8)
    pos = positions[0]

    def row_swap(x, odd):
        low = [i for i in range(tiles - columns) if i // columns % 2 == odd]
        pairs = [(i, i + columns) for i in low] + [(i + columns, i) for i in low]
        return lax.ppermute(x, "tile", pairs)

    def column_swap(x, odd):
        low = [i for i in range(tiles) if i % 2 == odd and i % columns + 1 < columns]
        pairs = [(i, i + 1) for i in low] + [(i + 1, i) for i in low]
        return lax.ppermute(x, "tile", pairs)

    def depth_swap(x, by):
        return lax.ppermute(x, "depth", [(i, i ^ by) for i in range(count)])

    rim_rows = sds(slices, 2, RIM, size)
    rim_cols = sds(slices, size + 2 * RIM, LANES)
    window = sds(slices, 2, points, points)
    ext = sds((size + 2 * RIM) // LANES, slices, 2, size + 2 * RIM, LANES, dtype=F32)
    amplitude, phase_map = amplitude[:, 0], phase_map[:, 0]
    first, second = call(
        functools.partial(rim_body, columns),
        (rim_rows, rim_rows),
        (amplitude, phase_map),
        specs=[HBM, HBM],
        scratch=(
            pltpu.VMEM((2, slices, 2, RIM, size), F32),
            pltpu.SemaphoreType.DMA((2, slices, 2)),
        ),
        flops=40 * 4 * RIM * size,
        name="row_rims_out",
    )
    rows = row_swap(first, 0), row_swap(second, 1)
    trans = call(
        transmit_body,
        sds(slices, 2, size, size),
        (amplitude, phase_map),
        specs=[HBM, HBM],
        scratch=(pltpu.VMEM((slices, 2, size, size), F32), pltpu.SemaphoreType.DMA((slices, 2))),
        flops=40 * 2 * size * size,
        name="transmit",
    )
    dft_real, dft_imag = dft_tables(points)
    fwd, bwd = call(
        operator_body,
        (sds(4, 2, 2 * points, 2 * points), sds(4, 2 * points, 2 * points)),
        (propagator_phase, jnp.asarray(dft_real), jnp.asarray(dft_imag)),
        flops=8 * 6 * 2 * points**3,
        name="operators",
    )
    first, second = call(
        functools.partial(column_body, columns),
        (rim_cols, rim_cols),
        (trans, *rows),
        name="column_rims_out",
    )
    cols = column_swap(first, 1), column_swap(second, 0)
    extended = call(functools.partial(extend_body, columns), ext, (trans, *rows), name="extend")
    windows = call(
        functools.partial(cut_body, count, size),
        (ext,) + (window,) * count,
        (pos, *cols, extended),
        specs=[SMEM] + [VMEM] * 3,
        aliases={3: 0},
        name="cut",
    )[1:]
    arrived = [windows[0]] + [depth_swap(windows[k], k) for k in range(1, count)]
    total = slices * count
    grads = call(
        functools.partial(wave_body, count),
        (window,) * count,
        (fwd, bwd, probe_wave, measured[0], *arrived),
        scratch=(
            pltpu.VMEM((count, slices, 2, points, points), BF16),
            pltpu.VMEM((total, 2, points, points), F32),
            pltpu.VMEM((count, slices, 2, points, points), BF16),
        ),
        flops=36 * 8 * 2 * points**3,
        name="waves",
    )
    returned = [grads[0]] + [depth_swap(grads[k], k) for k in range(1, count)]
    summed, first, second = call(
        functools.partial(deposit_body, count, size),
        (ext, rim_cols, rim_cols),
        (pos, *returned),
        specs=[SMEM] + [VMEM] * count,
        name="deposit",
    )
    cols = column_swap(first, 1), column_swap(second, 0)
    first, second = call(
        functools.partial(row_body, columns),
        (rim_rows, rim_rows),
        (summed, *cols),
        name="row_rims_back",
    )
    rows = row_swap(first, 0), row_swap(second, 1)
    gradient = sds(2, slices, size, size, dtype=F32)
    middle = call(
        middle_body,
        gradient,
        (summed, *cols),
        outs=HBM,
        scratch=(
            pltpu.VMEM((2, slices, size - 2 * RIM, size), F32),
            pltpu.SemaphoreType.DMA((2, slices, 1)),
        ),
        name="middle_rows",
    )
    gradient = call(
        functools.partial(edge_body, columns),
        gradient,
        (summed, *cols, *rows, middle),
        specs=[VMEM] * 5 + [HBM],
        outs=HBM,
        scratch=(
            pltpu.VMEM((2, slices, 2 * RIM, size), F32),
            pltpu.SemaphoreType.DMA((2, slices, 2)),
        ),
        aliases={5: 0},
        name="edge_rows",
    )
    return gradient[:, :, None]


def solution(mesh):
    in_specs = (
        P("depth", "tile", None, None),
        P("depth", "tile", None, None),
        P(),
        P(),
        P("tile", None, None),
        P("tile", None, None, None),
    )
    out_specs = P(None, "depth", "tile", None, None)
    return jax.shard_map(shards, mesh=mesh, in_specs=in_specs, out_specs=out_specs, check_vma=False)
```

time: 95.1 us -> 90 us (0.946)
  starting transfers between devices: 47.8 us -> 28.7 us
  waiting for transfers between devices: 32 us -> 44.8 us
  Pallas kernels: 11.9 us -> 13.9 us
    ppermute x14, starting transfers between devices: 47.8 us -> 28.7 us  [the longest x6 14.5 us: depth_swap(): return lax.ppermute(x, 'depth', [(i, i ^ by) for i in range(count)])]
    ppermute x14, waiting for transfers between devices: 32 us -> 44.8 us  [the longest x6 22.2 us: depth_swap(): return lax.ppermute(x, 'depth', [(i, i ^ by) for i in range(count)])]
    pallas_call x8 -> x11, Pallas kernels: 11.9 us -> 13.9 us  [call(): pl.pallas_call(body, out_shape=out_shape, in_specs=specs or [VMEM] * len(...]
  transfers between devices with their start and end apart: 14 -> 14, of which waited for: 14 -> 12; matrix products, arithmetic and copies ran while one was open for 0% -> 0% of each run, Pallas kernels for 1% -> 3%
where the time goes in v1:
time: 90 us; the launch traced here: 89.7 us
  waiting for transfers between devices  44.8 us (50%)
  starting transfers between devices  28.7 us (32%)
  Pallas kernels  13.9 us (15%)
  local copies, waits for them, and re-layouts  2.22 us (2%)
    ppermute x6, waiting for transfers between devices, depth_swap(): return lax.ppermute(x, 'depth', [(i, i ^ by) for i in range(count)])  22.2 us
    ppermute x6, starting transfers between devices, depth_swap(): return lax.ppermute(x, 'depth', [(i, i ^ by) for i in range(count)])  14.5 us
    pallas_call x11, Pallas kernels, call(): pl.pallas_call(body, out_shape=out_shape, in_specs=specs or [VMEM] * len(...  13.9 us
    ppermute x4, waiting for transfers between devices, row_swap(): return lax.ppermute(x, 'tile', pairs)  13.2 us
    ppermute x4, starting transfers between devices, row_swap(): return lax.ppermute(x, 'tile', pairs)  9.9 us
    ppermute x4, waiting for transfers between devices, column_swap(): return lax.ppermute(x, 'tile', pairs)  9.36 us
    ppermute x4, starting transfers between devices, column_swap(): return lax.ppermute(x, 'tile', pairs)  4.36 us
    unnamed x16, local copies, waits for them, and re-layouts  2.12 us
  transfers between devices with their start and end apart: 14, of which 12 were waited for; matrix products, arithmetic and copies ran while one was open for 0% of the time, Pallas kernels for 3%

profile of v1, /device:TPU:34, one launch (start us, length us, event | category | flops | bytes accessed | tf_op | source)
XLA Modules:
  0.0 89.7 jit_solution(5937830018287121780)
XLA Ops:
  0.0 1.1 %copy-done = f32[2,1,256,256]{3,2,1,0:T(8,128)S(1)} copy-done((f32[2,1,256,256]{3,2,1,0:T(8,128)S(1)}, f32[2,1,256,256]{3,2,1,0:T(8,128)}, u32[]{:S(2)}) %copy-start) | copy-done | bytes 524312
  1.1 1.0 %copy-done.1 = f32[2,1,256,256]{3,2,1,0:T(8,128)S(1)} copy-done((f32[2,1,256,256]{3,2,1,0:T(8,128)S(1)}, f32[2,1,256,256]{3,2,1,0:T(8,128)}, u32[]{:S(2)}) %copy-start.1) | copy-done | bytes 524312
  2.1 1.1 %row_rims_out.1 = (bf16[2,2,64,256]{3,2,1,0:T(8,128)(2,1)S(1)}, bf16[2,2,64,256]{3,2,1,0:T(8,128)(2,1)S(1)}) custom-call(f32[2,256,256]{2,1,0:T(8,128)S(1)} %bitcast.7, f32[2,256,256]{2,1,0:T(8,128)S(1)} %bitcast.9), custom_call_target="tpu_custom_call" | custom-call | flops 2621440 | bytes 1310720 | tf_op jit(solution)/shard_map/row_rims_out/pallas_call | solution.py:25
  3.2 3.3 %collective-permute-start = (bf16[2,2,64,256]{3,2,1,0:T(8,128)(2,1)S(1)}, bf16[2,2,64,256]{3,2,1,0:T(8,128)(2,1)S(1)}, u32[]{:S(2)}, u32[]{:S(2)}) collective-permute-start(bf16[2,2,64,256]{3,2,1,0:T(8,128)(2,1)S(1)} %get-tuple-element.26), channel_id=1, source_target_pairs={{0,8},{1,9},{2,10},{3,11},{4,12},{5,13},{6,14},{7,15},{16,24},{17,... | collective-permute-start | bytes 393224 | tf_op jit(solution)/shard_map/ppermute | solution.py:434
  6.5 2.2 %collective-permute-start.1 = (bf16[2,2,64,256]{3,2,1,0:T(8,128)(2,1)S(1)}, bf16[2,2,64,256]{3,2,1,0:T(8,128)(2,1)S(1)}, u32[]{:S(2)}, u32[]{:S(2)}) collective-permute-start(bf16[2,2,64,256]{3,2,1,0:T(8,128)(2,1)S(1)} %get-tuple-element.27), channel_id=1, source_target_pairs={{8,16},{9,17},{10,18},{11,19},{12,20},{13,21},{14,22},{15,23},{24,... | collective-permute-start | bytes 393224 | tf_op jit(solution)/shard_map/ppermute | solution.py:434
  8.7 0.8 transmit.1.t_ref
  9.6 0.5 collective-permute-done.row_first_ref
  10.0 5.7 %collective-permute-done.1.row_second_ref = bf16[2,2,64,256]{3,2,1,0:T(8,128)(2,1)S(1)} collective-permute-done((bf16[2,2,64,256]{3,2,1,0:T(8,128)(2,1)S(1)}, bf16[2,2,64,256]{3,2,1,0:T(8,128)(2,1)S(1)}, u32[]{:S(2)}, u32[]{:S(2)}) %collective-permute-start.1) | collective-permute-done | bytes 131104 | tf_op jit(solution)/shard_map/ppermute | solution.py:434
  15.7 0.2 column_rims_out.1
  16.0 1.9 %collective-permute-start.2 = (bf16[2,384,128]{2,1,0:T(8,128)(2,1)S(1)}, bf16[2,384,128]{2,1,0:T(8,128)(2,1)S(1)}, u32[]{:S(2)}, u32[]{:S(2)}) collective-permute-start(bf16[2,384,128]{2,1,0:T(8,128)(2,1)S(1)} %get-tuple-element.28), channel_id=1, source_target_pairs={{1,2},{3,4},{5,6},{9,10},{11,12},{13,14},{17,18},{19,20},{21,22},{... | collective-permute-start | bytes 589832 | tf_op jit(solution)/shard_map/ppermute | solution.py:439
  17.9 0.4 collective-permute-start.3
  18.3 0.0 copy-done.7
  18.3 0.1 copy.12.pos_ref
  18.4 0.1 extend.1.ext_in
  18.5 0.0 copy-start.2
  18.5 0.0 copy-start.3
  18.5 4.4 %collective-permute-done.2.rim_first_ref = bf16[2,384,128]{2,1,0:T(8,128)(2,1)S(1)} collective-permute-done((bf16[2,384,128]{2,1,0:T(8,128)(2,1)S(1)}, bf16[2,384,128]{2,1,0:T(8,128)(2,1)S(1)}, u32[]{:S(2)}, u32[]{:S(2)}) %collective-permute-start.2) | collective-permute-done | bytes 196640 | tf_op jit(solution)/shard_map/ppermute | solution.py:439
  22.9 0.0 collective-permute-done.3.rim_second_ref
  22.9 1.1 %cut.1 = (f32[3,2,2,384,128]{4,3,2,1,0:T(8,128)S(1)}, bf16[2,2,128,128]{3,2,1,0:T(8,128)(2,1)S(1)}, bf16[2,2,128,128]{3,2,1,0:T(8,128)(2,1)S(1)}, bf16[2,2,128,1...) custom-call(s32[4,2]{1,0:T(4,128)S(1)} %copy.12.pos_ref, ...), custom_call_target="tpu_custom_call", output_to_operand_aliasing={{0}: (3, {})} | custom-call | bytes 5636128 | tf_op jit(solution)/shard_map/cut/pallas_call | solution.py:25
  24.0 3.4 %collective-permute-start.4 = (bf16[2,2,128,128]{3,2,1,0:T(8,128)(2,1)S(1)}, bf16[2,2,128,128]{3,2,1,0:T(8,128)(2,1)S(1)}, u32[]{:S(2)}, u32[]{:S(2)}) collective-permute-start(bf16[2,2,128,128]{3,2,1,0:T(8,128)(2,1)S(1)} %get-tuple-element.31), channel_id=1, source_target_pairs={{0,64},{64,0},{128,192},{192,128},{1,65},{65,1},{129,193},{193,129... | collective-permute-start | bytes 393224 | tf_op jit(solution)/shard_map/ppermute | solution.py:442
  27.4 4.5 %collective-permute-start.5 = (bf16[2,2,128,128]{3,2,1,0:T(8,128)(2,1)S(1)}, bf16[2,2,128,128]{3,2,1,0:T(8,128)(2,1)S(1)}, u32[]{:S(2)}, u32[]{:S(2)}) collective-permute-start(bf16[2,2,128,128]{3,2,1,0:T(8,128)(2,1)S(1)} %get-tuple-element.32), channel_id=1, source_target_pairs={{0,128},{64,192},{128,0},{192,64},{1,129},{65,193},{129,1},{193,65... | collective-permute-start | bytes 393224 | tf_op jit(solution)/shard_map/ppermute | solution.py:442
  31.9 0.0 collective-permute-start.6
  31.9 0.0 copy-done.4
  31.9 0.0 copy-done.5
  31.9 0.7 operators.1
  32.7 5.5 %collective-permute-done.4.rest_1_ = bf16[2,2,128,128]{3,2,1,0:T(8,128)(2,1)S(1)} collective-permute-done((bf16[2,2,128,128]{3,2,1,0:T(8,128)(2,1)S(1)}, bf16[2,2,128,128]{3,2,1,0:T(8,128)(2,1)S(1)}, u32[]{:S(2)}, u32[]{:S(2)}) %collective-permute-start.4) | collective-permute-done | bytes 131104 | tf_op jit(solution)/shard_map/ppermute | solution.py:442
  38.1 0.1 collective-permute-done.5.rest_2_
  38.2 4.3 %collective-permute-done.6.rest_3_ = bf16[2,2,128,128]{3,2,1,0:T(8,128)(2,1)S(1)} collective-permute-done((bf16[2,2,128,128]{3,2,1,0:T(8,128)(2,1)S(1)}, bf16[2,2,128,128]{3,2,1,0:T(8,128)(2,1)S(1)}, u32[]{:S(2)}, u32[]{:S(2)}) %collective-permute-start.6) | collective-permute-done | bytes 131104 | tf_op jit(solution)/shard_map/ppermute | solution.py:442
  42.5 0.0 copy-done.3
  42.5 6.5 %waves.1 = (bf16[2,2,128,128]{3,2,1,0:T(8,128)(2,1)S(1)}, bf16[2,2,128,128]{3,2,1,0:T(8,128)(2,1)S(1)}, bf16[2,2,128,128]{3,2,1,0:T(8,128)(2,1)S(1)}, bf16[2,2,128,128]{3,2,1,0:T(8,128)(2,1)S(1)}) custom-call(bf16[4,2,256,256]{3,2,1,0:T(8,128)(2,1)S(1)} %get-tuple-element.24.fwd_ref, bf16[4,256,256]{2,1,0:T(8,128)(2,1)S(1)} %get-tuple-element.25.bwd_ref, ...), custom_call_target="tpu_custom_call" | custom-call | flops 1207959552 | bytes 3014656 | tf_op jit(solution)/shard_map/waves/pallas_call | solution.py:25
  49.0 2.9 %collective-permute-start.7 = (bf16[2,2,128,128]{3,2,1,0:T(8,128)(2,1)S(1)}, bf16[2,2,128,128]{3,2,1,0:T(8,128)(2,1)S(1)}, u32[]{:S(2)}, u32[]{:S(2)}) collective-permute-start(bf16[2,2,128,128]{3,2,1,0:T(8,128)(2,1)S(1)} %get-tuple-element.35), channel_id=1, source_target_pairs={{0,64},{64,0},{128,192},{192,128},{1,65},{65,1},{129,193},{193,129... | collective-permute-start | bytes 393224 | tf_op jit(solution)/shard_map/ppermute | solution.py:442
  51.9 3.1 %collective-permute-start.8 = (bf16[2,2,128,128]{3,2,1,0:T(8,128)(2,1)S(1)}, bf16[2,2,128,128]{3,2,1,0:T(8,128)(2,1)S(1)}, u32[]{:S(2)}, u32[]{:S(2)}) collective-permute-start(bf16[2,2,128,128]{3,2,1,0:T(8,128)(2,1)S(1)} %get-tuple-element.36), channel_id=1, source_target_pairs={{0,128},{64,192},{128,0},{192,64},{1,129},{65,193},{129,1},{193,65... | collective-permute-start | bytes 393224 | tf_op jit(solution)/shard_map/ppermute | solution.py:442
  55.0 0.6 collective-permute-start.9
  55.6 6.9 %collective-permute-done.7.rest_1_ = bf16[2,2,128,128]{3,2,1,0:T(8,128)(2,1)S(1)} collective-permute-done((bf16[2,2,128,128]{3,2,1,0:T(8,128)(2,1)S(1)}, bf16[2,2,128,128]{3,2,1,0:T(8,128)(2,1)S(1)}, u32[]{:S(2)}, u32[]{:S(2)}) %collective-permute-start.7) | collective-permute-done | bytes 131104 | tf_op jit(solution)/shard_map/ppermute | solution.py:442
  62.5 1.6 %collective-permute-done.8.rest_2_ = bf16[2,2,128,128]{3,2,1,0:T(8,128)(2,1)S(1)} collective-permute-done((bf16[2,2,128,128]{3,2,1,0:T(8,128)(2,1)S(1)}, bf16[2,2,128,128]{3,2,1,0:T(8,128)(2,1)S(1)}, u32[]{:S(2)}, u32[]{:S(2)}) %collective-permute-start.8) | collective-permute-done | bytes 131104 | tf_op jit(solution)/shard_map/ppermute | solution.py:442
  64.1 4.0 %collective-permute-done.9.rest_3_ = bf16[2,2,128,128]{3,2,1,0:T(8,128)(2,1)S(1)} collective-permute-done((bf16[2,2,128,128]{3,2,1,0:T(8,128)(2,1)S(1)}, bf16[2,2,128,128]{3,2,1,0:T(8,128)(2,1)S(1)}, u32[]{:S(2)}, u32[]{:S(2)}) %collective-permute-start.9) | collective-permute-done | bytes 131104 | tf_op jit(solution)/shard_map/ppermute | solution.py:442
  68.0 1.2 %deposit.1 = (f32[3,2,2,384,128]{4,3,2,1,0:T(8,128)S(1)}, bf16[2,384,128]{2,1,0:T(8,128)(2,1)S(1)}, bf16[2,384,128]{2,1,0:T(8,128)(2,1)S(1)}) custom-call(s32[4,2]{1,0:T(4,128)S(1)} %copy.12.pos_ref, bf16[2,2,128,128]{3,2,1,0:T(8,128)(2,1)S(1)} %get-tuple-element.34.rest_0_, bf16[2,2,128,128]{3,2,1,0:T(8,128)(2,1)S(1)} %collective-permute-done.7.rest_1_, ...), custom_call_target="tpu_custom_call" | custom-call | bytes 3276832 | tf_op jit(solution)/shard_map/deposit/pallas_call | solution.py:25
  69.3 1.9 %collective-permute-start.10 = (bf16[2,384,128]{2,1,0:T(8,128)(2,1)S(1)}, bf16[2,384,128]{2,1,0:T(8,128)(2,1)S(1)}, u32[]{:S(2)}, u32[]{:S(2)}) collective-permute-start(bf16[2,384,128]{2,1,0:T(8,128)(2,1)S(1)} %get-tuple-element.39), channel_id=1, source_target_pairs={{1,2},{3,4},{5,6},{9,10},{11,12},{13,14},{17,18},{19,20},{21,22},{... | collective-permute-start | bytes 589832 | tf_op jit(solution)/shard_map/ppermute | solution.py:439
  71.2 0.1 collective-permute-start.11
  71.3 5.0 %collective-permute-done.10.rim_first_ref = bf16[2,384,128]{2,1,0:T(8,128)(2,1)S(1)} collective-permute-done((bf16[2,384,128]{2,1,0:T(8,128)(2,1)S(1)}, bf16[2,384,128]{2,1,0:T(8,128)(2,1)S(1)}, u32[]{:S(2)}, u32[]{:S(2)}) %collective-permute-start.10) | collective-permute-done | bytes 196640 | tf_op jit(solution)/shard_map/ppermute | solution.py:439
  76.2 0.0 collective-permute-done.11.rim_second_ref
  76.2 0.1 row_rims_back.1
  76.4 2.5 %collective-permute-start.12 = (bf16[2,2,64,256]{3,2,1,0:T(8,128)(2,1)S(1)}, bf16[2,2,64,256]{3,2,1,0:T(8,128)(2,1)S(1)}, u32[]{:S(2)}, u32[]{:S(2)}) collective-permute-start(bf16[2,2,64,256]{3,2,1,0:T(8,128)(2,1)S(1)} %get-tuple-element.41), channel_id=1, source_target_pairs={{0,8},{1,9},{2,10},{3,11},{4,12},{5,13},{6,14},{7,15},{16,24},{17,... | collective-permute-start | bytes 393224 | tf_op jit(solution)/shard_map/ppermute | solution.py:434
  78.9 1.9 %collective-permute-start.13 = (bf16[2,2,64,256]{3,2,1,0:T(8,128)(2,1)S(1)}, bf16[2,2,64,256]{3,2,1,0:T(8,128)(2,1)S(1)}, u32[]{:S(2)}, u32[]{:S(2)}) collective-permute-start(bf16[2,2,64,256]{3,2,1,0:T(8,128)(2,1)S(1)} %get-tuple-element.42), channel_id=1, source_target_pairs={{8,16},{9,17},{10,18},{11,19},{12,20},{13,21},{14,22},{15,23},{24,... | collective-permute-start | bytes 393224 | tf_op jit(solution)/shard_map/ppermute | solution.py:434
  80.8 1.0 %middle_rows.1.rest_2_ = f32[2,2,256,256]{3,2,1,0:T(8,128)} custom-call(f32[3,2,2,384,128]{4,3,2,1,0:T(8,128)S(1)} %get-tuple-element.38.ext_ref, bf16[2,384,128]{2,1,0:T(8,128)(2,1)S(1)} %collective-permute-done.10.rim_first_ref, bf16[2,384,128]{2,1,0:T(8,128)(2,1)S(1)} %collective-permute-done.11.rim_second_ref), custom_call_target="tpu_custom_call" | custom-call | bytes 3801088 | tf_op jit(solution)/shard_map/middle_rows/pallas_call | solution.py:25
  81.8 2.5 %collective-permute-done.12.rest_0_ = bf16[2,2,64,256]{3,2,1,0:T(8,128)(2,1)S(1)} collective-permute-done((bf16[2,2,64,256]{3,2,1,0:T(8,128)(2,1)S(1)}, bf16[2,2,64,256]{3,2,1,0:T(8,128)(2,1)S(1)}, u32[]{:S(2)}, u32[]{:S(2)}) %collective-permute-start.12) | collective-permute-done | bytes 131104 | tf_op jit(solution)/shard_map/ppermute | solution.py:434
  84.3 4.5 %collective-permute-done.13.rest_1_ = bf16[2,2,64,256]{3,2,1,0:T(8,128)(2,1)S(1)} collective-permute-done((bf16[2,2,64,256]{3,2,1,0:T(8,128)(2,1)S(1)}, bf16[2,2,64,256]{3,2,1,0:T(8,128)(2,1)S(1)}, u32[]{:S(2)}, u32[]{:S(2)}) %collective-permute-start.13) | collective-permute-done | bytes 131104 | tf_op jit(solution)/shard_map/ppermute | solution.py:434
  88.8 0.9 %edge_rows.1 = f32[2,2,256,256]{3,2,1,0:T(8,128)} custom-call(f32[3,2,2,384,128]{4,3,2,1,0:T(8,128)S(1)} %get-tuple-element.38.ext_ref, bf16[2,384,128]{2,1,0:T(8,128)(2,1)S(1)} %collective-permute-done.10.rim_first_ref, bf16[2,384,128]{2,1,0:T(8,128)(2,1)S(1)} %collective-permute-done.11.rim_second_ref, ...), custom_call_target="tpu_custom_call", output_to_operand_aliasing={{}: (5, {})} | custom-call | bytes 5111808 | tf_op jit(solution)/shard_map/edge_rows/pallas_call | solution.py:25
  (8 shorter events, 0.0 us)
Async XLA Ops:
  0.0 18.3 %copy-start.7 = (s32[1,4,2]{1,2,0:T(2,128)S(1)}, s32[1,4,2]{1,2,0:T(2,128)}, u32[]{:S(2)}) copy-start(s32[1,4,2]{1,2,0:T(2,128)} %param.12) | copy-start | bytes 100
  0.0 1.1 %copy-start = (f32[2,1,256,256]{3,2,1,0:T(8,128)S(1)}, f32[2,1,256,256]{3,2,1,0:T(8,128)}, u32[]{:S(2)}) copy-start(f32[2,1,256,256]{3,2,1,0:T(8,128)} %param.8) | copy-start | bytes 1572868
  1.1 1.0 %copy-start.1 = (f32[2,1,256,256]{3,2,1,0:T(8,128)S(1)}, f32[2,1,256,256]{3,2,1,0:T(8,128)}, u32[]{:S(2)}) copy-start(f32[2,1,256,256]{3,2,1,0:T(8,128)} %param.9) | copy-start | bytes 1572868
  3.2 6.8 %collective-permute-start = (bf16[2,2,64,256]{3,2,1,0:T(8,128)(2,1)S(1)}, bf16[2,2,64,256]{3,2,1,0:T(8,128)(2,1)S(1)}, u32[]{:S(2)}, u32[]{:S(2)}) collective-permute-start(bf16[2,2,64,256]{3,2,1,0:T(8,128)(2,1)S(1)} %get-tuple-element.26), channel_id=1, source_target_pairs={{0,8},{1,9},{2,10},{3,11},{4,12},{5,13},{6,14},{7,15},{16,24},{17,... | collective-permute-start | bytes 393224 | tf_op jit(solution)/shard_map/ppermute | solution.py:434
  6.5 9.3 %collective-permute-start.1 = (bf16[2,2,64,256]{3,2,1,0:T(8,128)(2,1)S(1)}, bf16[2,2,64,256]{3,2,1,0:T(8,128)(2,1)S(1)}, u32[]{:S(2)}, u32[]{:S(2)}) collective-permute-start(bf16[2,2,64,256]{3,2,1,0:T(8,128)(2,1)S(1)} %get-tuple-element.27), channel_id=1, source_target_pairs={{8,16},{9,17},{10,18},{11,19},{12,20},{13,21},{14,22},{15,23},{24,... | collective-permute-start | bytes 393224 | tf_op jit(solution)/shard_map/ppermute | solution.py:434
  16.0 7.0 %collective-permute-start.2 = (bf16[2,384,128]{2,1,0:T(8,128)(2,1)S(1)}, bf16[2,384,128]{2,1,0:T(8,128)(2,1)S(1)}, u32[]{:S(2)}, u32[]{:S(2)}) collective-permute-start(bf16[2,384,128]{2,1,0:T(8,128)(2,1)S(1)} %get-tuple-element.28), channel_id=1, source_target_pairs={{1,2},{3,4},{5,6},{9,10},{11,12},{13,14},{17,18},{19,20},{21,22},{... | collective-permute-start | bytes 589832 | tf_op jit(solution)/shard_map/ppermute | solution.py:439
  17.9 5.1 %collective-permute-start.3 = (bf16[2,384,128]{2,1,0:T(8,128)(2,1)S(1)}, bf16[2,384,128]{2,1,0:T(8,128)(2,1)S(1)}, u32[]{:S(2)}, u32[]{:S(2)}) collective-permute-start(bf16[2,384,128]{2,1,0:T(8,128)(2,1)S(1)} %get-tuple-element.29), channel_id=1, source_target_pairs={{0,1},{2,3},{4,5},{6,7},{8,9},{10,11},{12,13},{14,15},{16,17},{18,... | collective-permute-start | bytes 589832 | tf_op jit(solution)/shard_map/ppermute | solution.py:439
  18.4 13.5 %copy-start.4 = (f32[2,128]{1,0:T(2,128)S(1)}, f32[2,128]{1,0:T(2,128)}, u32[]{:S(2)}) copy-start(f32[2,128]{1,0:T(2,128)} %phase_ref.1) | copy-start | bytes 3076
  18.4 13.5 %copy-start.5 = (f32[128,128]{1,0:T(8,128)S(1)}, f32[128,128]{1,0:T(8,128)}, u32[]{:S(2)}) copy-start(f32[128,128]{1,0:T(8,128)} %constant.5.clone.dft_imag_ref) | copy-start | bytes 196612
  18.4 13.5 %copy-start.6 = (f32[128,128]{1,0:T(8,128)S(1)}, f32[128,128]{1,0:T(8,128)}, u32[]{:S(2)}) copy-start(f32[128,128]{1,0:T(8,128)} %constant.4.clone.dft_real_ref) | copy-start | bytes 196612
  18.5 24.0 %copy-start.2 = (f32[1,4,128,128]{3,2,1,0:T(8,128)S(1)}, f32[1,4,128,128]{3,2,1,0:T(8,128)}, u32[]{:S(2)}) copy-start(f32[1,4,128,128]{3,2,1,0:T(8,128)} %param.13) | copy-start | bytes 786436
  18.5 23.9 %copy-start.3 = (f32[2,128,128]{2,1,0:T(8,128)S(1)}, f32[2,128,128]{2,1,0:T(8,128)}, u32[]{:S(2)}) copy-start(f32[2,128,128]{2,1,0:T(8,128)} %probe_ref.1) | copy-start | bytes 393220
  24.0 14.1 %collective-permute-start.4 = (bf16[2,2,128,128]{3,2,1,0:T(8,128)(2,1)S(1)}, bf16[2,2,128,128]{3,2,1,0:T(8,128)(2,1)S(1)}, u32[]{:S(2)}, u32[]{:S(2)}) collective-permute-start(bf16[2,2,128,128]{3,2,1,0:T(8,128)(2,1)S(1)} %get-tuple-element.31), channel_id=1, source_target_pairs={{0,64},{64,0},{128,192},{192,128},{1,65},{65,1},{129,193},{193,129... | collective-permute-start | bytes 393224 | tf_op jit(solution)/shard_map/ppermute | solution.py:442
  27.4 10.8 %collective-permute-start.5 = (bf16[2,2,128,128]{3,2,1,0:T(8,128)(2,1)S(1)}, bf16[2,2,128,128]{3,2,1,0:T(8,128)(2,1)S(1)}, u32[]{:S(2)}, u32[]{:S(2)}) collective-permute-start(bf16[2,2,128,128]{3,2,1,0:T(8,128)(2,1)S(1)} %get-tuple-element.32), channel_id=1, source_target_pairs={{0,128},{64,192},{128,0},{192,64},{1,129},{65,193},{129,1},{193,65... | collective-permute-start | bytes 393224 | tf_op jit(solution)/shard_map/ppermute | solution.py:442
  31.9 10.6 %collective-permute-start.6 = (bf16[2,2,128,128]{3,2,1,0:T(8,128)(2,1)S(1)}, bf16[2,2,128,128]{3,2,1,0:T(8,128)(2,1)S(1)}, u32[]{:S(2)}, u32[]{:S(2)}) collective-permute-start(bf16[2,2,128,128]{3,2,1,0:T(8,128)(2,1)S(1)} %get-tuple-element.33), channel_id=1, source_target_pairs={{0,192},{64,128},{128,64},{192,0},{1,193},{65,129},{129,65},{193,1... | collective-permute-start | bytes 393224 | tf_op jit(solution)/shard_map/ppermute | solution.py:442
  49.0 13.5 %collective-permute-start.7 = (bf16[2,2,128,128]{3,2,1,0:T(8,128)(2,1)S(1)}, bf16[2,2,128,128]{3,2,1,0:T(8,128)(2,1)S(1)}, u32[]{:S(2)}, u32[]{:S(2)}) collective-permute-start(bf16[2,2,128,128]{3,2,1,0:T(8,128)(2,1)S(1)} %get-tuple-element.35), channel_id=1, source_target_pairs={{0,64},{64,0},{128,192},{192,128},{1,65},{65,1},{129,193},{193,129... | collective-permute-start | bytes 393224 | tf_op jit(solution)/shard_map/ppermute | solution.py:442
  51.9 12.1 %collective-permute-start.8 = (bf16[2,2,128,128]{3,2,1,0:T(8,128)(2,1)S(1)}, bf16[2,2,128,128]{3,2,1,0:T(8,128)(2,1)S(1)}, u32[]{:S(2)}, u32[]{:S(2)}) collective-permute-start(bf16[2,2,128,128]{3,2,1,0:T(8,128)(2,1)S(1)} %get-tuple-element.36), channel_id=1, source_target_pairs={{0,128},{64,192},{128,0},{192,64},{1,129},{65,193},{129,1},{193,65... | collective-permute-start | bytes 393224 | tf_op jit(solution)/shard_map/ppermute | solution.py:442
  55.0 13.0 %collective-permute-start.9 = (bf16[2,2,128,128]{3,2,1,0:T(8,128)(2,1)S(1)}, bf16[2,2,128,128]{3,2,1,0:T(8,128)(2,1)S(1)}, u32[]{:S(2)}, u32[]{:S(2)}) collective-permute-start(bf16[2,2,128,128]{3,2,1,0:T(8,128)(2,1)S(1)} %get-tuple-element.37), channel_id=1, source_target_pairs={{0,192},{64,128},{128,64},{192,0},{1,193},{65,129},{129,65},{193,1... | collective-permute-start | bytes 393224 | tf_op jit(solution)/shard_map/ppermute | solution.py:442
  69.3 7.0 %collective-permute-start.10 = (bf16[2,384,128]{2,1,0:T(8,128)(2,1)S(1)}, bf16[2,384,128]{2,1,0:T(8,128)(2,1)S(1)}, u32[]{:S(2)}, u32[]{:S(2)}) collective-permute-start(bf16[2,384,128]{2,1,0:T(8,128)(2,1)S(1)} %get-tuple-element.39), channel_id=1, source_target_pairs={{1,2},{3,4},{5,6},{9,10},{11,12},{13,14},{17,18},{19,20},{21,22},{... | collective-permute-start | bytes 589832 | tf_op jit(solution)/shard_map/ppermute | solution.py:439
  71.2 5.1 %collective-permute-start.11 = (bf16[2,384,128]{2,1,0:T(8,128)(2,1)S(1)}, bf16[2,384,128]{2,1,0:T(8,128)(2,1)S(1)}, u32[]{:S(2)}, u32[]{:S(2)}) collective-permute-start(bf16[2,384,128]{2,1,0:T(8,128)(2,1)S(1)} %get-tuple-element.40), channel_id=1, source_target_pairs={{0,1},{2,3},{4,5},{6,7},{8,9},{10,11},{12,13},{14,15},{16,17},{18,... | collective-permute-start | bytes 589832 | tf_op jit(solution)/shard_map/ppermute | solution.py:439
  76.4 7.9 %collective-permute-start.12 = (bf16[2,2,64,256]{3,2,1,0:T(8,128)(2,1)S(1)}, bf16[2,2,64,256]{3,2,1,0:T(8,128)(2,1)S(1)}, u32[]{:S(2)}, u32[]{:S(2)}) collective-permute-start(bf16[2,2,64,256]{3,2,1,0:T(8,128)(2,1)S(1)} %get-tuple-element.41), channel_id=1, source_target_pairs={{0,8},{1,9},{2,10},{3,11},{4,12},{5,13},{6,14},{7,15},{16,24},{17,... | collective-permute-start | bytes 393224 | tf_op jit(solution)/shard_map/ppermute | solution.py:434
  78.9 9.9 %collective-permute-start.13 = (bf16[2,2,64,256]{3,2,1,0:T(8,128)(2,1)S(1)}, bf16[2,2,64,256]{3,2,1,0:T(8,128)(2,1)S(1)}, u32[]{:S(2)}, u32[]{:S(2)}) collective-permute-start(bf16[2,2,64,256]{3,2,1,0:T(8,128)(2,1)S(1)} %get-tuple-element.42), channel_id=1, source_target_pairs={{8,16},{9,17},{10,18},{11,19},{12,20},{13,21},{14,22},{15,23},{24,... | collective-permute-start | bytes 393224 | tf_op jit(solution)/shard_map/ppermute | solution.py:434

commit v2 on v1

--- a/solution.py
+++ b/solution.py
@@ -445,7 +445,10 @@
     rim_cols = sds(slices, size + 2 * RIM, LANES)
     window = sds(slices, 2, points, points)
     ext = sds((size + 2 * RIM) // LANES, slices, 2, size + 2 * RIM, LANES, dtype=F32)
-    amplitude, phase_map = amplitude[:, 0], phase_map[:, 0]
+    amplitude, phase_map = (
+        pltpu.with_memory_space_constraint(x[:, 0], pltpu.MemorySpace.HBM)
+        for x in (amplitude, phase_map)
+    )
     first, second = call(
         functools.partial(rim_body, columns),
         (rim_rows, rim_rows),

time: 90 us -> 88.1 us (0.979)
  local copies, waits for them, and re-layouts: 2.22 us -> 0.12 us
  waiting for transfers between devices: 44.8 us -> 43.3 us
  Pallas kernels: 13.9 us -> 15 us
    unnamed x16 -> x12, local copies, waits for them, and re-layouts: 2.12 us -> 0.03 us
    pallas_call x11, Pallas kernels: 13.9 us -> 15 us  [call(): pl.pallas_call(body, out_shape=out_shape, in_specs=specs or [VMEM] * len(...]
    ppermute x4, waiting for transfers between devices: 13.2 us -> 12.3 us  [row_swap(): return lax.ppermute(x, 'tile', pairs)]
  transfers between devices with their start and end apart: 14 -> 14, of which waited for: 12 -> 11; matrix products, arithmetic and copies ran while one was open for 0% -> 0% of each run, Pallas kernels for 3% -> 4%
where the time goes in v2:
time: 88.1 us; the launch traced here: 87.9 us
  waiting for transfers between devices  43.3 us (49%)
  starting transfers between devices  29.2 us (33%)
  Pallas kernels  15 us (17%)
    ppermute x6, waiting for transfers between devices, depth_swap(): return lax.ppermute(x, 'depth', [(i, i ^ by) for i in range(count)])  21.7 us
    pallas_call x11, Pallas kernels, call(): pl.pallas_call(body, out_shape=out_shape, in_specs=specs or [VMEM] * len(...  15 us
    ppermute x6, starting transfers between devices, depth_swap(): return lax.ppermute(x, 'depth', [(i, i ^ by) for i in range(count)])  14.9 us
    ppermute x4, waiting for transfers between devices, row_swap(): return lax.ppermute(x, 'tile', pairs)  12.3 us
    ppermute x4, starting transfers between devices, row_swap(): return lax.ppermute(x, 'tile', pairs)  9.92 us
    ppermute x4, waiting for transfers between devices, column_swap(): return lax.ppermute(x, 'tile', pairs)  9.36 us
    ppermute x4, starting transfers between devices, column_swap(): return lax.ppermute(x, 'tile', pairs)  4.36 us
  transfers between devices with their start and end apart: 14, of which 11 were waited for; matrix products, arithmetic and copies ran while one was open for 0% of the time, Pallas kernels for 4%

profile of v2, /device:TPU:34, one launch (start us, length us, event | category | flops | bytes accessed | tf_op | source)
XLA Modules:
  0.0 87.9 jit_solution(574113003208145597)
XLA Ops:
  0.0 1.3 %row_rims_out.1 = (bf16[2,2,64,256]{3,2,1,0:T(8,128)(2,1)S(1)}, bf16[2,2,64,256]{3,2,1,0:T(8,128)(2,1)S(1)}) custom-call(f32[2,256,256]{2,1,0:T(8,128)} %bitcast.8, f32[2,256,256]{2,1,0:T(8,128)} %bitcast.10), custom_call_target="tpu_custom_call" | custom-call | flops 2621440 | bytes 1310720 | tf_op jit(solution)/shard_map/row_rims_out/pallas_call | solution.py:25
  1.3 3.3 %collective-permute-start = (bf16[2,2,64,256]{3,2,1,0:T(8,128)(2,1)S(1)}, bf16[2,2,64,256]{3,2,1,0:T(8,128)(2,1)S(1)}, u32[]{:S(2)}, u32[]{:S(2)}) collective-permute-start(bf16[2,2,64,256]{3,2,1,0:T(8,128)(2,1)S(1)} %get-tuple-element.26), channel_id=1, source_target_pairs={{0,8},{1,9},{2,10},{3,11},{4,12},{5,13},{6,14},{7,15},{16,24},{17,... | collective-permute-start | bytes 393224 | tf_op jit(solution)/shard_map/ppermute | solution.py:434
  4.6 2.2 %collective-permute-start.1 = (bf16[2,2,64,256]{3,2,1,0:T(8,128)(2,1)S(1)}, bf16[2,2,64,256]{3,2,1,0:T(8,128)(2,1)S(1)}, u32[]{:S(2)}, u32[]{:S(2)}) collective-permute-start(bf16[2,2,64,256]{3,2,1,0:T(8,128)(2,1)S(1)} %get-tuple-element.27), channel_id=1, source_target_pairs={{8,16},{9,17},{10,18},{11,19},{12,20},{13,21},{14,22},{15,23},{24,... | collective-permute-start | bytes 393224 | tf_op jit(solution)/shard_map/ppermute | solution.py:434
  6.8 1.8 %transmit.1.t_ref = bf16[2,2,256,256]{3,2,1,0:T(8,128)(2,1)S(1)} custom-call(f32[2,256,256]{2,1,0:T(8,128)} %bitcast.9, f32[2,256,256]{2,1,0:T(8,128)} %bitcast.11), custom_call_target="tpu_custom_call" | custom-call | flops 5242880 | bytes 1572864 | tf_op jit(solution)/shard_map/transmit/pallas_call | solution.py:25
  8.6 0.0 collective-permute-done.row_first_ref
  8.6 5.2 %collective-permute-done.1.row_second_ref = bf16[2,2,64,256]{3,2,1,0:T(8,128)(2,1)S(1)} collective-permute-done((bf16[2,2,64,256]{3,2,1,0:T(8,128)(2,1)S(1)}, bf16[2,2,64,256]{3,2,1,0:T(8,128)(2,1)S(1)}, u32[]{:S(2)}, u32[]{:S(2)}) %collective-permute-start.1) | collective-permute-done | bytes 131104 | tf_op jit(solution)/shard_map/ppermute | solution.py:434
  13.8 0.2 column_rims_out.1
  14.1 1.9 %collective-permute-start.2 = (bf16[2,384,128]{2,1,0:T(8,128)(2,1)S(1)}, bf16[2,384,128]{2,1,0:T(8,128)(2,1)S(1)}, u32[]{:S(2)}, u32[]{:S(2)}) collective-permute-start(bf16[2,384,128]{2,1,0:T(8,128)(2,1)S(1)} %get-tuple-element.28), channel_id=1, source_target_pairs={{1,2},{3,4},{5,6},{9,10},{11,12},{13,14},{17,18},{19,20},{21,22},{... | collective-permute-start | bytes 589832 | tf_op jit(solution)/shard_map/ppermute | solution.py:439
  16.0 0.4 collective-permute-start.3
  16.4 0.0 copy-done.5
  16.4 0.1 copy.12.pos_ref
  16.5 0.1 extend.1.ext_in
  16.6 0.0 copy-start
  16.6 0.0 copy-start.1
  16.6 4.4 %collective-permute-done.2.rim_first_ref = bf16[2,384,128]{2,1,0:T(8,128)(2,1)S(1)} collective-permute-done((bf16[2,384,128]{2,1,0:T(8,128)(2,1)S(1)}, bf16[2,384,128]{2,1,0:T(8,128)(2,1)S(1)}, u32[]{:S(2)}, u32[]{:S(2)}) %collective-permute-start.2) | collective-permute-done | bytes 196640 | tf_op jit(solution)/shard_map/ppermute | solution.py:439
  21.0 0.0 collective-permute-done.3.rim_second_ref
  21.1 1.1 %cut.1 = (f32[3,2,2,384,128]{4,3,2,1,0:T(8,128)S(1)}, bf16[2,2,128,128]{3,2,1,0:T(8,128)(2,1)S(1)}, bf16[2,2,128,128]{3,2,1,0:T(8,128)(2,1)S(1)}, bf16[2,2,128,1...) custom-call(s32[4,2]{1,0:T(4,128)S(1)} %copy.12.pos_ref, ...), custom_call_target="tpu_custom_call", output_to_operand_aliasing={{0}: (3, {})} | custom-call | bytes 5636128 | tf_op jit(solution)/shard_map/cut/pallas_call | solution.py:25
  22.2 3.4 %collective-permute-start.4 = (bf16[2,2,128,128]{3,2,1,0:T(8,128)(2,1)S(1)}, bf16[2,2,128,128]{3,2,1,0:T(8,128)(2,1)S(1)}, u32[]{:S(2)}, u32[]{:S(2)}) collective-permute-start(bf16[2,2,128,128]{3,2,1,0:T(8,128)(2,1)S(1)} %get-tuple-element.31), channel_id=1, source_target_pairs={{0,64},{64,0},{128,192},{192,128},{1,65},{65,1},{129,193},{193,129... | collective-permute-start | bytes 393224 | tf_op jit(solution)/shard_map/ppermute | solution.py:442
  25.5 4.5 %collective-permute-start.5 = (bf16[2,2,128,128]{3,2,1,0:T(8,128)(2,1)S(1)}, bf16[2,2,128,128]{3,2,1,0:T(8,128)(2,1)S(1)}, u32[]{:S(2)}, u32[]{:S(2)}) collective-permute-start(bf16[2,2,128,128]{3,2,1,0:T(8,128)(2,1)S(1)} %get-tuple-element.32), channel_id=1, source_target_pairs={{0,128},{64,192},{128,0},{192,64},{1,129},{65,193},{129,1},{193,65... | collective-permute-start | bytes 393224 | tf_op jit(solution)/shard_map/ppermute | solution.py:442
  30.0 0.0 collective-permute-start.6
  30.0 0.0 copy-done.2
  30.0 0.0 copy-done.3
  30.0 0.0 copy-done.4
  30.0 0.7 operators.1
  30.8 5.5 %collective-permute-done.4.rest_1_ = bf16[2,2,128,128]{3,2,1,0:T(8,128)(2,1)S(1)} collective-permute-done((bf16[2,2,128,128]{3,2,1,0:T(8,128)(2,1)S(1)}, bf16[2,2,128,128]{3,2,1,0:T(8,128)(2,1)S(1)}, u32[]{:S(2)}, u32[]{:S(2)}) %collective-permute-start.4) | collective-permute-done | bytes 131104 | tf_op jit(solution)/shard_map/ppermute | solution.py:442
  36.2 0.1 collective-permute-done.5.rest_2_
  36.3 3.8 %collective-permute-done.6.rest_3_ = bf16[2,2,128,128]{3,2,1,0:T(8,128)(2,1)S(1)} collective-permute-done((bf16[2,2,128,128]{3,2,1,0:T(8,128)(2,1)S(1)}, bf16[2,2,128,128]{3,2,1,0:T(8,128)(2,1)S(1)}, u32[]{:S(2)}, u32[]{:S(2)}) %collective-permute-start.6) | collective-permute-done | bytes 131104 | tf_op jit(solution)/shard_map/ppermute | solution.py:442
  40.1 0.0 copy-done
  40.1 0.0 copy-done.1
  40.1 6.5 %waves.1 = (bf16[2,2,128,128]{3,2,1,0:T(8,128)(2,1)S(1)}, bf16[2,2,128,128]{3,2,1,0:T(8,128)(2,1)S(1)}, bf16[2,2,128,128]{3,2,1,0:T(8,128)(2,1)S(1)}, bf16[2,2,128,128]{3,2,1,0:T(8,128)(2,1)S(1)}) custom-call(bf16[4,2,256,256]{3,2,1,0:T(8,128)(2,1)S(1)} %get-tuple-element.24.fwd_ref, bf16[4,256,256]{2,1,0:T(8,128)(2,1)S(1)} %get-tuple-element.25.bwd_ref, ...), custom_call_target="tpu_custom_call" | custom-call | flops 1207959552 | bytes 3014656 | tf_op jit(solution)/shard_map/waves/pallas_call | solution.py:25
  46.6 3.4 %collective-permute-start.7 = (bf16[2,2,128,128]{3,2,1,0:T(8,128)(2,1)S(1)}, bf16[2,2,128,128]{3,2,1,0:T(8,128)(2,1)S(1)}, u32[]{:S(2)}, u32[]{:S(2)}) collective-permute-start(bf16[2,2,128,128]{3,2,1,0:T(8,128)(2,1)S(1)} %get-tuple-element.35), channel_id=1, source_target_pairs={{0,64},{64,0},{128,192},{192,128},{1,65},{65,1},{129,193},{193,129... | collective-permute-start | bytes 393224 | tf_op jit(solution)/shard_map/ppermute | solution.py:442
  50.0 3.1 %collective-permute-start.8 = (bf16[2,2,128,128]{3,2,1,0:T(8,128)(2,1)S(1)}, bf16[2,2,128,128]{3,2,1,0:T(8,128)(2,1)S(1)}, u32[]{:S(2)}, u32[]{:S(2)}) collective-permute-start(bf16[2,2,128,128]{3,2,1,0:T(8,128)(2,1)S(1)} %get-tuple-element.36), channel_id=1, source_target_pairs={{0,128},{64,192},{128,0},{192,64},{1,129},{65,193},{129,1},{193,65... | collective-permute-start | bytes 393224 | tf_op jit(solution)/shard_map/ppermute | solution.py:442
  53.1 0.6 collective-permute-start.9
  53.7 6.9 %collective-permute-done.7.rest_1_ = bf16[2,2,128,128]{3,2,1,0:T(8,128)(2,1)S(1)} collective-permute-done((bf16[2,2,128,128]{3,2,1,0:T(8,128)(2,1)S(1)}, bf16[2,2,128,128]{3,2,1,0:T(8,128)(2,1)S(1)}, u32[]{:S(2)}, u32[]{:S(2)}) %collective-permute-start.7) | collective-permute-done | bytes 131104 | tf_op jit(solution)/shard_map/ppermute | solution.py:442
  60.6 1.6 %collective-permute-done.8.rest_2_ = bf16[2,2,128,128]{3,2,1,0:T(8,128)(2,1)S(1)} collective-permute-done((bf16[2,2,128,128]{3,2,1,0:T(8,128)(2,1)S(1)}, bf16[2,2,128,128]{3,2,1,0:T(8,128)(2,1)S(1)}, u32[]{:S(2)}, u32[]{:S(2)}) %collective-permute-start.8) | collective-permute-done | bytes 131104 | tf_op jit(solution)/shard_map/ppermute | solution.py:442
  62.2 4.0 %collective-permute-done.9.rest_3_ = bf16[2,2,128,128]{3,2,1,0:T(8,128)(2,1)S(1)} collective-permute-done((bf16[2,2,128,128]{3,2,1,0:T(8,128)(2,1)S(1)}, bf16[2,2,128,128]{3,2,1,0:T(8,128)(2,1)S(1)}, u32[]{:S(2)}, u32[]{:S(2)}) %collective-permute-start.9) | collective-permute-done | bytes 131104 | tf_op jit(solution)/shard_map/ppermute | solution.py:442
  66.1 1.2 %deposit.1 = (f32[3,2,2,384,128]{4,3,2,1,0:T(8,128)S(1)}, bf16[2,384,128]{2,1,0:T(8,128)(2,1)S(1)}, bf16[2,384,128]{2,1,0:T(8,128)(2,1)S(1)}) custom-call(s32[4,2]{1,0:T(4,128)S(1)} %copy.12.pos_ref, bf16[2,2,128,128]{3,2,1,0:T(8,128)(2,1)S(1)} %get-tuple-element.34.rest_0_, bf16[2,2,128,128]{3,2,1,0:T(8,128)(2,1)S(1)} %collective-permute-done.7.rest_1_, ...), custom_call_target="tpu_custom_call" | custom-call | bytes 3276832 | tf_op jit(solution)/shard_map/deposit/pallas_call | solution.py:25
  67.3 1.9 %collective-permute-start.10 = (bf16[2,384,128]{2,1,0:T(8,128)(2,1)S(1)}, bf16[2,384,128]{2,1,0:T(8,128)(2,1)S(1)}, u32[]{:S(2)}, u32[]{:S(2)}) collective-permute-start(bf16[2,384,128]{2,1,0:T(8,128)(2,1)S(1)} %get-tuple-element.39), channel_id=1, source_target_pairs={{1,2},{3,4},{5,6},{9,10},{11,12},{13,14},{17,18},{19,20},{21,22},{... | collective-permute-start | bytes 589832 | tf_op jit(solution)/shard_map/ppermute | solution.py:439
  69.3 0.1 collective-permute-start.11
  69.4 5.0 %collective-permute-done.10.rim_first_ref = bf16[2,384,128]{2,1,0:T(8,128)(2,1)S(1)} collective-permute-done((bf16[2,384,128]{2,1,0:T(8,128)(2,1)S(1)}, bf16[2,384,128]{2,1,0:T(8,128)(2,1)S(1)}, u32[]{:S(2)}, u32[]{:S(2)}) %collective-permute-start.10) | collective-permute-done | bytes 196640 | tf_op jit(solution)/shard_map/ppermute | solution.py:439
  74.3 0.0 collective-permute-done.11.rim_second_ref
  74.3 0.1 row_rims_back.1
  74.5 2.5 %collective-permute-start.12 = (bf16[2,2,64,256]{3,2,1,0:T(8,128)(2,1)S(1)}, bf16[2,2,64,256]{3,2,1,0:T(8,128)(2,1)S(1)}, u32[]{:S(2)}, u32[]{:S(2)}) collective-permute-start(bf16[2,2,64,256]{3,2,1,0:T(8,128)(2,1)S(1)} %get-tuple-element.41), channel_id=1, source_target_pairs={{0,8},{1,9},{2,10},{3,11},{4,12},{5,13},{6,14},{7,15},{16,24},{17,... | collective-permute-start | bytes 393224 | tf_op jit(solution)/shard_map/ppermute | solution.py:434
  77.0 1.9 %collective-permute-start.13 = (bf16[2,2,64,256]{3,2,1,0:T(8,128)(2,1)S(1)}, bf16[2,2,64,256]{3,2,1,0:T(8,128)(2,1)S(1)}, u32[]{:S(2)}, u32[]{:S(2)}) collective-permute-start(bf16[2,2,64,256]{3,2,1,0:T(8,128)(2,1)S(1)} %get-tuple-element.42), channel_id=1, source_target_pairs={{8,16},{9,17},{10,18},{11,19},{12,20},{13,21},{14,22},{15,23},{24,... | collective-permute-start | bytes 393224 | tf_op jit(solution)/shard_map/ppermute | solution.py:434
  78.9 1.0 %middle_rows.1.rest_2_ = f32[2,2,256,256]{3,2,1,0:T(8,128)} custom-call(f32[3,2,2,384,128]{4,3,2,1,0:T(8,128)S(1)} %get-tuple-element.38.ext_ref, bf16[2,384,128]{2,1,0:T(8,128)(2,1)S(1)} %collective-permute-done.10.rim_first_ref, bf16[2,384,128]{2,1,0:T(8,128)(2,1)S(1)} %collective-permute-done.11.rim_second_ref), custom_call_target="tpu_custom_call" | custom-call | bytes 3801088 | tf_op jit(solution)/shard_map/middle_rows/pallas_call | solution.py:25
  79.9 2.5 %collective-permute-done.12.rest_0_ = bf16[2,2,64,256]{3,2,1,0:T(8,128)(2,1)S(1)} collective-permute-done((bf16[2,2,64,256]{3,2,1,0:T(8,128)(2,1)S(1)}, bf16[2,2,64,256]{3,2,1,0:T(8,128)(2,1)S(1)}, u32[]{:S(2)}, u32[]{:S(2)}) %collective-permute-start.12) | collective-permute-done | bytes 131104 | tf_op jit(solution)/shard_map/ppermute | solution.py:434
  82.4 4.5 %collective-permute-done.13.rest_1_ = bf16[2,2,64,256]{3,2,1,0:T(8,128)(2,1)S(1)} collective-permute-done((bf16[2,2,64,256]{3,2,1,0:T(8,128)(2,1)S(1)}, bf16[2,2,64,256]{3,2,1,0:T(8,128)(2,1)S(1)}, u32[]{:S(2)}, u32[]{:S(2)}) %collective-permute-start.13) | collective-permute-done | bytes 131104 | tf_op jit(solution)/shard_map/ppermute | solution.py:434
  86.9 0.9 %edge_rows.1 = f32[2,2,256,256]{3,2,1,0:T(8,128)} custom-call(f32[3,2,2,384,128]{4,3,2,1,0:T(8,128)S(1)} %get-tuple-element.38.ext_ref, bf16[2,384,128]{2,1,0:T(8,128)(2,1)S(1)} %collective-permute-done.10.rim_first_ref, bf16[2,384,128]{2,1,0:T(8,128)(2,1)S(1)} %collective-permute-done.11.rim_second_ref, ...), custom_call_target="tpu_custom_call", output_to_operand_aliasing={{}: (5, {})} | custom-call | bytes 5111808 | tf_op jit(solution)/shard_map/edge_rows/pallas_call | solution.py:25
  (4 shorter events, 0.0 us)
Async XLA Ops:
  0.0 16.4 %copy-start.5 = (s32[1,4,2]{1,2,0:T(2,128)S(1)}, s32[1,4,2]{1,2,0:T(2,128)}, u32[]{:S(2)}) copy-start(s32[1,4,2]{1,2,0:T(2,128)} %param.12) | copy-start | bytes 100
  1.3 7.3 %collective-permute-start = (bf16[2,2,64,256]{3,2,1,0:T(8,128)(2,1)S(1)}, bf16[2,2,64,256]{3,2,1,0:T(8,128)(2,1)S(1)}, u32[]{:S(2)}, u32[]{:S(2)}) collective-permute-start(bf16[2,2,64,256]{3,2,1,0:T(8,128)(2,1)S(1)} %get-tuple-element.26), channel_id=1, source_target_pairs={{0,8},{1,9},{2,10},{3,11},{4,12},{5,13},{6,14},{7,15},{16,24},{17,... | collective-permute-start | bytes 393224 | tf_op jit(solution)/shard_map/ppermute | solution.py:434
  4.6 9.3 %collective-permute-start.1 = (bf16[2,2,64,256]{3,2,1,0:T(8,128)(2,1)S(1)}, bf16[2,2,64,256]{3,2,1,0:T(8,128)(2,1)S(1)}, u32[]{:S(2)}, u32[]{:S(2)}) collective-permute-start(bf16[2,2,64,256]{3,2,1,0:T(8,128)(2,1)S(1)} %get-tuple-element.27), channel_id=1, source_target_pairs={{8,16},{9,17},{10,18},{11,19},{12,20},{13,21},{14,22},{15,23},{24,... | collective-permute-start | bytes 393224 | tf_op jit(solution)/shard_map/ppermute | solution.py:434
  14.1 7.0 %collective-permute-start.2 = (bf16[2,384,128]{2,1,0:T(8,128)(2,1)S(1)}, bf16[2,384,128]{2,1,0:T(8,128)(2,1)S(1)}, u32[]{:S(2)}, u32[]{:S(2)}) collective-permute-start(bf16[2,384,128]{2,1,0:T(8,128)(2,1)S(1)} %get-tuple-element.28), channel_id=1, source_target_pairs={{1,2},{3,4},{5,6},{9,10},{11,12},{13,14},{17,18},{19,20},{21,22},{... | collective-permute-start | bytes 589832 | tf_op jit(solution)/shard_map/ppermute | solution.py:439
  16.0 5.1 %collective-permute-start.3 = (bf16[2,384,128]{2,1,0:T(8,128)(2,1)S(1)}, bf16[2,384,128]{2,1,0:T(8,128)(2,1)S(1)}, u32[]{:S(2)}, u32[]{:S(2)}) collective-permute-start(bf16[2,384,128]{2,1,0:T(8,128)(2,1)S(1)} %get-tuple-element.29), channel_id=1, source_target_pairs={{0,1},{2,3},{4,5},{6,7},{8,9},{10,11},{12,13},{14,15},{16,17},{18,... | collective-permute-start | bytes 589832 | tf_op jit(solution)/shard_map/ppermute | solution.py:439
  16.5 13.5 %copy-start.2 = (f32[2,128]{1,0:T(2,128)S(1)}, f32[2,128]{1,0:T(2,128)}, u32[]{:S(2)}) copy-start(f32[2,128]{1,0:T(2,128)} %phase_ref.1) | copy-start | bytes 3076
  16.5 13.5 %copy-start.3 = (f32[128,128]{1,0:T(8,128)S(1)}, f32[128,128]{1,0:T(8,128)}, u32[]{:S(2)}) copy-start(f32[128,128]{1,0:T(8,128)} %constant.5.clone.dft_imag_ref) | copy-start | bytes 196612
  16.5 13.5 %copy-start.4 = (f32[128,128]{1,0:T(8,128)S(1)}, f32[128,128]{1,0:T(8,128)}, u32[]{:S(2)}) copy-start(f32[128,128]{1,0:T(8,128)} %constant.4.clone.dft_real_ref) | copy-start | bytes 196612
  16.6 23.5 %copy-start = (f32[1,4,128,128]{3,2,1,0:T(8,128)S(1)}, f32[1,4,128,128]{3,2,1,0:T(8,128)}, u32[]{:S(2)}) copy-start(f32[1,4,128,128]{3,2,1,0:T(8,128)} %param.13) | copy-start | bytes 786436
  16.6 23.5 %copy-start.1 = (f32[2,128,128]{2,1,0:T(8,128)S(1)}, f32[2,128,128]{2,1,0:T(8,128)}, u32[]{:S(2)}) copy-start(f32[2,128,128]{2,1,0:T(8,128)} %probe_ref.1) | copy-start | bytes 393220
  22.2 14.1 %collective-permute-start.4 = (bf16[2,2,128,128]{3,2,1,0:T(8,128)(2,1)S(1)}, bf16[2,2,128,128]{3,2,1,0:T(8,128)(2,1)S(1)}, u32[]{:S(2)}, u32[]{:S(2)}) collective-permute-start(bf16[2,2,128,128]{3,2,1,0:T(8,128)(2,1)S(1)} %get-tuple-element.31), channel_id=1, source_target_pairs={{0,64},{64,0},{128,192},{192,128},{1,65},{65,1},{129,193},{193,129... | collective-permute-start | bytes 393224 | tf_op jit(solution)/shard_map/ppermute | solution.py:442
  25.5 10.8 %collective-permute-start.5 = (bf16[2,2,128,128]{3,2,1,0:T(8,128)(2,1)S(1)}, bf16[2,2,128,128]{3,2,1,0:T(8,128)(2,1)S(1)}, u32[]{:S(2)}, u32[]{:S(2)}) collective-permute-start(bf16[2,2,128,128]{3,2,1,0:T(8,128)(2,1)S(1)} %get-tuple-element.32), channel_id=1, source_target_pairs={{0,128},{64,192},{128,0},{192,64},{1,129},{65,193},{129,1},{193,65... | collective-permute-start | bytes 393224 | tf_op jit(solution)/shard_map/ppermute | solution.py:442
  30.0 10.1 %collective-permute-start.6 = (bf16[2,2,128,128]{3,2,1,0:T(8,128)(2,1)S(1)}, bf16[2,2,128,128]{3,2,1,0:T(8,128)(2,1)S(1)}, u32[]{:S(2)}, u32[]{:S(2)}) collective-permute-start(bf16[2,2,128,128]{3,2,1,0:T(8,128)(2,1)S(1)} %get-tuple-element.33), channel_id=1, source_target_pairs={{0,192},{64,128},{128,64},{192,0},{1,193},{65,129},{129,65},{193,1... | collective-permute-start | bytes 393224 | tf_op jit(solution)/shard_map/ppermute | solution.py:442
  46.6 13.9 %collective-permute-start.7 = (bf16[2,2,128,128]{3,2,1,0:T(8,128)(2,1)S(1)}, bf16[2,2,128,128]{3,2,1,0:T(8,128)(2,1)S(1)}, u32[]{:S(2)}, u32[]{:S(2)}) collective-permute-start(bf16[2,2,128,128]{3,2,1,0:T(8,128)(2,1)S(1)} %get-tuple-element.35), channel_id=1, source_target_pairs={{0,64},{64,0},{128,192},{192,128},{1,65},{65,1},{129,193},{193,129... | collective-permute-start | bytes 393224 | tf_op jit(solution)/shard_map/ppermute | solution.py:442
  50.0 12.1 %collective-permute-start.8 = (bf16[2,2,128,128]{3,2,1,0:T(8,128)(2,1)S(1)}, bf16[2,2,128,128]{3,2,1,0:T(8,128)(2,1)S(1)}, u32[]{:S(2)}, u32[]{:S(2)}) collective-permute-start(bf16[2,2,128,128]{3,2,1,0:T(8,128)(2,1)S(1)} %get-tuple-element.36), channel_id=1, source_target_pairs={{0,128},{64,192},{128,0},{192,64},{1,129},{65,193},{129,1},{193,65... | collective-permute-start | bytes 393224 | tf_op jit(solution)/shard_map/ppermute | solution.py:442
  53.1 13.0 %collective-permute-start.9 = (bf16[2,2,128,128]{3,2,1,0:T(8,128)(2,1)S(1)}, bf16[2,2,128,128]{3,2,1,0:T(8,128)(2,1)S(1)}, u32[]{:S(2)}, u32[]{:S(2)}) collective-permute-start(bf16[2,2,128,128]{3,2,1,0:T(8,128)(2,1)S(1)} %get-tuple-element.37), channel_id=1, source_target_pairs={{0,192},{64,128},{128,64},{192,0},{1,193},{65,129},{129,65},{193,1... | collective-permute-start | bytes 393224 | tf_op jit(solution)/shard_map/ppermute | solution.py:442
  67.3 7.0 %collective-permute-start.10 = (bf16[2,384,128]{2,1,0:T(8,128)(2,1)S(1)}, bf16[2,384,128]{2,1,0:T(8,128)(2,1)S(1)}, u32[]{:S(2)}, u32[]{:S(2)}) collective-permute-start(bf16[2,384,128]{2,1,0:T(8,128)(2,1)S(1)} %get-tuple-element.39), channel_id=1, source_target_pairs={{1,2},{3,4},{5,6},{9,10},{11,12},{13,14},{17,18},{19,20},{21,22},{... | collective-permute-start | bytes 589832 | tf_op jit(solution)/shard_map/ppermute | solution.py:439
  69.3 5.1 %collective-permute-start.11 = (bf16[2,384,128]{2,1,0:T(8,128)(2,1)S(1)}, bf16[2,384,128]{2,1,0:T(8,128)(2,1)S(1)}, u32[]{:S(2)}, u32[]{:S(2)}) collective-permute-start(bf16[2,384,128]{2,1,0:T(8,128)(2,1)S(1)} %get-tuple-element.40), channel_id=1, source_target_pairs={{0,1},{2,3},{4,5},{6,7},{8,9},{10,11},{12,13},{14,15},{16,17},{18,... | collective-permute-start | bytes 589832 | tf_op jit(solution)/shard_map/ppermute | solution.py:439
  74.5 7.9 %collective-permute-start.12 = (bf16[2,2,64,256]{3,2,1,0:T(8,128)(2,1)S(1)}, bf16[2,2,64,256]{3,2,1,0:T(8,128)(2,1)S(1)}, u32[]{:S(2)}, u32[]{:S(2)}) collective-permute-start(bf16[2,2,64,256]{3,2,1,0:T(8,128)(2,1)S(1)} %get-tuple-element.41), channel_id=1, source_target_pairs={{0,8},{1,9},{2,10},{3,11},{4,12},{5,13},{6,14},{7,15},{16,24},{17,... | collective-permute-start | bytes 393224 | tf_op jit(solution)/shard_map/ppermute | solution.py:434
  77.0 9.9 %collective-permute-start.13 = (bf16[2,2,64,256]{3,2,1,0:T(8,128)(2,1)S(1)}, bf16[2,2,64,256]{3,2,1,0:T(8,128)(2,1)S(1)}, u32[]{:S(2)}, u32[]{:S(2)}) collective-permute-start(bf16[2,2,64,256]{3,2,1,0:T(8,128)(2,1)S(1)} %get-tuple-element.42), channel_id=1, source_target_pairs={{8,16},{9,17},{10,18},{11,19},{12,20},{13,21},{14,22},{15,23},{24,... | collective-permute-start | bytes 393224 | tf_op jit(solution)/shard_map/ppermute | solution.py:434

commit v3 on v2

--- a/solution.py
+++ b/solution.py
@@ -180,9 +180,10 @@
         lane = lax.broadcasted_iota(jnp.int32, (LANES, LANES), 1)
         for s in range(slices):
             for part in range(2):
-                low = pltpu.roll(ext[first, s, part, pl.ds(row, LANES), :], turn, 1)
-                high = pltpu.roll(ext[second, s, part, pl.ds(row, LANES), :], turn, 1)
-                outs[k][s, part] = jnp.where(lane < LANES - shift, low, high).astype(BF16)
+                low = ext[first, s, part, pl.ds(row, LANES), :]
+                high = ext[second, s, part, pl.ds(row, LANES), :]
+                mixed = jnp.where(lane >= shift, low, high)
+                outs[k][s, part] = pltpu.roll(mixed.astype(BF16), turn, 1)
 
 
 def operator_body(phase_ref, dft_real_ref, dft_imag_ref, fwd_ref, bwd_ref):
@@ -276,7 +277,7 @@
         half = left_fine(fwd_ref, 0, *mix(s, *wave))
         return right_fine(fwd_ref, 1, *half)
 
-    wave = lax.fori_loop(0, total - 1, forward, (probe_ref[0], probe_ref[1]))
+    wave = lax.fori_loop(0, total - 1, forward, (probe_ref[0], probe_ref[1]), unroll=True)
     half = left_fine(fwd_ref, 2, *mix(total - 1, *wave))
     far_real, far_imag = right_fine(fwd_ref, 3, *half)
     misfit = far_real * far_real + far_imag * far_imag - measured_ref[depth]
@@ -297,7 +298,7 @@
         half = left_plain(bwd_ref, 0, pr * sr + pi * si, pr * si - pi * sr)
         return right_plain(bwd_ref, 1, *half)
 
-    spread = lax.fori_loop(0, total - 1, backward, spread)
+    spread = lax.fori_loop(0, total - 1, backward, spread, unroll=True)
     contribute(0, *spread)
     for k in range(count):
         outs[k][...] = grads[depth ^ k]
@@ -319,7 +320,7 @@
         rows = pl.ds(row, LANES)
         for s in range(slices):
             for part in range(2):
-                moved = pltpu.roll(grads[k][s, part].astype(F32), shift, 1)
+                moved = pltpu.roll(grads[k][s, part], shift, 1).astype(F32)
                 low = jnp.where(lane >= shift, moved, 0.0)
                 ext[first, s, part, rows, :] += low
                 ext[second, s, part, rows, :] += moved - low

time: 88.1 us -> 87.3 us (level)
  no operation moved by 1% of the time
where the time goes in v3:
time: 87.3 us; the launch traced here: 87 us
  waiting for transfers between devices  43.8 us (50%)
  starting transfers between devices  28.8 us (33%)
  Pallas kernels  14.2 us (16%)
    ppermute x6, waiting for transfers between devices, depth_swap(): return lax.ppermute(x, 'depth', [(i, i ^ by) for i in range(count)])  22.2 us
    ppermute x6, starting transfers between devices, depth_swap(): return lax.ppermute(x, 'depth', [(i, i ^ by) for i in range(count)])  14.5 us
    pallas_call x11, Pallas kernels, call(): pl.pallas_call(body, out_shape=out_shape, in_specs=specs or [VMEM] * len(...  14.2 us
    ppermute x4, waiting for transfers between devices, row_swap(): return lax.ppermute(x, 'tile', pairs)  12.3 us
    ppermute x4, starting transfers between devices, row_swap(): return lax.ppermute(x, 'tile', pairs)  9.95 us
    ppermute x4, waiting for transfers between devices, column_swap(): return lax.ppermute(x, 'tile', pairs)  9.37 us
    ppermute x4, starting transfers between devices, column_swap(): return lax.ppermute(x, 'tile', pairs)  4.35 us
  transfers between devices with their start and end apart: 14, of which 11 were waited for; matrix products, arithmetic and copies ran while one was open for 0% of the time, Pallas kernels for 4%

profile of v3, /device:TPU:34, one launch (start us, length us, event | category | flops | bytes accessed | tf_op | source)
XLA Modules:
  0.0 87.0 jit_solution(2644783972692475391)
XLA Ops:
  0.0 1.3 %row_rims_out.1 = (bf16[2,2,64,256]{3,2,1,0:T(8,128)(2,1)S(1)}, bf16[2,2,64,256]{3,2,1,0:T(8,128)(2,1)S(1)}) custom-call(f32[2,256,256]{2,1,0:T(8,128)} %bitcast.8, f32[2,256,256]{2,1,0:T(8,128)} %bitcast.10), custom_call_target="tpu_custom_call" | custom-call | flops 2621440 | bytes 1310720 | tf_op jit(solution)/shard_map/row_rims_out/pallas_call | solution.py:25
  1.3 3.3 %collective-permute-start = (bf16[2,2,64,256]{3,2,1,0:T(8,128)(2,1)S(1)}, bf16[2,2,64,256]{3,2,1,0:T(8,128)(2,1)S(1)}, u32[]{:S(2)}, u32[]{:S(2)}) collective-permute-start(bf16[2,2,64,256]{3,2,1,0:T(8,128)(2,1)S(1)} %get-tuple-element.26), channel_id=1, source_target_pairs={{0,8},{1,9},{2,10},{3,11},{4,12},{5,13},{6,14},{7,15},{16,24},{17,... | collective-permute-start | bytes 393224 | tf_op jit(solution)/shard_map/ppermute | solution.py:435
  4.6 2.2 %collective-permute-start.1 = (bf16[2,2,64,256]{3,2,1,0:T(8,128)(2,1)S(1)}, bf16[2,2,64,256]{3,2,1,0:T(8,128)(2,1)S(1)}, u32[]{:S(2)}, u32[]{:S(2)}) collective-permute-start(bf16[2,2,64,256]{3,2,1,0:T(8,128)(2,1)S(1)} %get-tuple-element.27), channel_id=1, source_target_pairs={{8,16},{9,17},{10,18},{11,19},{12,20},{13,21},{14,22},{15,23},{24,... | collective-permute-start | bytes 393224 | tf_op jit(solution)/shard_map/ppermute | solution.py:435
  6.8 1.8 %transmit.1.t_ref = bf16[2,2,256,256]{3,2,1,0:T(8,128)(2,1)S(1)} custom-call(f32[2,256,256]{2,1,0:T(8,128)} %bitcast.9, f32[2,256,256]{2,1,0:T(8,128)} %bitcast.11), custom_call_target="tpu_custom_call" | custom-call | flops 5242880 | bytes 1572864 | tf_op jit(solution)/shard_map/transmit/pallas_call | solution.py:25
  8.6 0.0 collective-permute-done.row_first_ref
  8.6 5.2 %collective-permute-done.1.row_second_ref = bf16[2,2,64,256]{3,2,1,0:T(8,128)(2,1)S(1)} collective-permute-done((bf16[2,2,64,256]{3,2,1,0:T(8,128)(2,1)S(1)}, bf16[2,2,64,256]{3,2,1,0:T(8,128)(2,1)S(1)}, u32[]{:S(2)}, u32[]{:S(2)}) %collective-permute-start.1) | collective-permute-done | bytes 131104 | tf_op jit(solution)/shard_map/ppermute | solution.py:435
  13.8 0.2 column_rims_out.1
  14.1 1.9 %collective-permute-start.2 = (bf16[2,384,128]{2,1,0:T(8,128)(2,1)S(1)}, bf16[2,384,128]{2,1,0:T(8,128)(2,1)S(1)}, u32[]{:S(2)}, u32[]{:S(2)}) collective-permute-start(bf16[2,384,128]{2,1,0:T(8,128)(2,1)S(1)} %get-tuple-element.28), channel_id=1, source_target_pairs={{1,2},{3,4},{5,6},{9,10},{11,12},{13,14},{17,18},{19,20},{21,22},{... | collective-permute-start | bytes 589832 | tf_op jit(solution)/shard_map/ppermute | solution.py:440
  16.0 0.4 collective-permute-start.3
  16.4 0.0 copy-done.5
  16.4 0.1 copy.12.pos_ref
  16.5 0.1 extend.1.ext_in
  16.6 0.0 copy-start
  16.6 0.0 copy-start.1
  16.6 4.4 %collective-permute-done.2.rim_first_ref = bf16[2,384,128]{2,1,0:T(8,128)(2,1)S(1)} collective-permute-done((bf16[2,384,128]{2,1,0:T(8,128)(2,1)S(1)}, bf16[2,384,128]{2,1,0:T(8,128)(2,1)S(1)}, u32[]{:S(2)}, u32[]{:S(2)}) %collective-permute-start.2) | collective-permute-done | bytes 196640 | tf_op jit(solution)/shard_map/ppermute | solution.py:440
  21.0 0.0 collective-permute-done.3.rim_second_ref
  21.1 1.0 %cut.1 = (f32[3,2,2,384,128]{4,3,2,1,0:T(8,128)S(1)}, bf16[2,2,128,128]{3,2,1,0:T(8,128)(2,1)S(1)}, bf16[2,2,128,128]{3,2,1,0:T(8,128)(2,1)S(1)}, bf16[2,2,128,1...) custom-call(s32[4,2]{1,0:T(4,128)S(1)} %copy.12.pos_ref, ...), custom_call_target="tpu_custom_call", output_to_operand_aliasing={{0}: (3, {})} | custom-call | bytes 5636128 | tf_op jit(solution)/shard_map/cut/pallas_call | solution.py:25
  22.0 3.4 %collective-permute-start.4 = (bf16[2,2,128,128]{3,2,1,0:T(8,128)(2,1)S(1)}, bf16[2,2,128,128]{3,2,1,0:T(8,128)(2,1)S(1)}, u32[]{:S(2)}, u32[]{:S(2)}) collective-permute-start(bf16[2,2,128,128]{3,2,1,0:T(8,128)(2,1)S(1)} %get-tuple-element.31), channel_id=1, source_target_pairs={{0,64},{64,0},{128,192},{192,128},{1,65},{65,1},{129,193},{193,129... | collective-permute-start | bytes 393224 | tf_op jit(solution)/shard_map/ppermute | solution.py:443
  25.4 4.5 %collective-permute-start.5 = (bf16[2,2,128,128]{3,2,1,0:T(8,128)(2,1)S(1)}, bf16[2,2,128,128]{3,2,1,0:T(8,128)(2,1)S(1)}, u32[]{:S(2)}, u32[]{:S(2)}) collective-permute-start(bf16[2,2,128,128]{3,2,1,0:T(8,128)(2,1)S(1)} %get-tuple-element.32), channel_id=1, source_target_pairs={{0,128},{64,192},{128,0},{192,64},{1,129},{65,193},{129,1},{193,65... | collective-permute-start | bytes 393224 | tf_op jit(solution)/shard_map/ppermute | solution.py:443
  29.9 0.0 collective-permute-start.6
  29.9 0.0 copy-done.2
  29.9 0.0 copy-done.3
  29.9 0.0 copy-done.4
  29.9 0.7 operators.1
  30.6 5.5 %collective-permute-done.4.rest_1_ = bf16[2,2,128,128]{3,2,1,0:T(8,128)(2,1)S(1)} collective-permute-done((bf16[2,2,128,128]{3,2,1,0:T(8,128)(2,1)S(1)}, bf16[2,2,128,128]{3,2,1,0:T(8,128)(2,1)S(1)}, u32[]{:S(2)}, u32[]{:S(2)}) %collective-permute-start.4) | collective-permute-done | bytes 131104 | tf_op jit(solution)/shard_map/ppermute | solution.py:443
  36.1 0.1 collective-permute-done.5.rest_2_
  36.2 4.3 %collective-permute-done.6.rest_3_ = bf16[2,2,128,128]{3,2,1,0:T(8,128)(2,1)S(1)} collective-permute-done((bf16[2,2,128,128]{3,2,1,0:T(8,128)(2,1)S(1)}, bf16[2,2,128,128]{3,2,1,0:T(8,128)(2,1)S(1)}, u32[]{:S(2)}, u32[]{:S(2)}) %collective-permute-start.6) | collective-permute-done | bytes 131104 | tf_op jit(solution)/shard_map/ppermute | solution.py:443
  40.4 0.0 copy-done
  40.4 0.0 copy-done.1
  40.4 5.9 %waves.1 = (bf16[2,2,128,128]{3,2,1,0:T(8,128)(2,1)S(1)}, bf16[2,2,128,128]{3,2,1,0:T(8,128)(2,1)S(1)}, bf16[2,2,128,128]{3,2,1,0:T(8,128)(2,1)S(1)}, bf16[2,2,128,128]{3,2,1,0:T(8,128)(2,1)S(1)}) custom-call(bf16[4,2,256,256]{3,2,1,0:T(8,128)(2,1)S(1)} %get-tuple-element.24.fwd_ref, bf16[4,256,256]{2,1,0:T(8,128)(2,1)S(1)} %get-tuple-element.25.bwd_ref, ...), custom_call_target="tpu_custom_call" | custom-call | flops 1207959552 | bytes 3014656 | tf_op jit(solution)/shard_map/waves/pallas_call | solution.py:25
  46.3 3.0 %collective-permute-start.7 = (bf16[2,2,128,128]{3,2,1,0:T(8,128)(2,1)S(1)}, bf16[2,2,128,128]{3,2,1,0:T(8,128)(2,1)S(1)}, u32[]{:S(2)}, u32[]{:S(2)}) collective-permute-start(bf16[2,2,128,128]{3,2,1,0:T(8,128)(2,1)S(1)} %get-tuple-element.35), channel_id=1, source_target_pairs={{0,64},{64,0},{128,192},{192,128},{1,65},{65,1},{129,193},{193,129... | collective-permute-start | bytes 393224 | tf_op jit(solution)/shard_map/ppermute | solution.py:443
  49.3 3.1 %collective-permute-start.8 = (bf16[2,2,128,128]{3,2,1,0:T(8,128)(2,1)S(1)}, bf16[2,2,128,128]{3,2,1,0:T(8,128)(2,1)S(1)}, u32[]{:S(2)}, u32[]{:S(2)}) collective-permute-start(bf16[2,2,128,128]{3,2,1,0:T(8,128)(2,1)S(1)} %get-tuple-element.36), channel_id=1, source_target_pairs={{0,128},{64,192},{128,0},{192,64},{1,129},{65,193},{129,1},{193,65... | collective-permute-start | bytes 393224 | tf_op jit(solution)/shard_map/ppermute | solution.py:443
  52.3 0.6 collective-permute-start.9
  53.0 6.8 %collective-permute-done.7.rest_1_ = bf16[2,2,128,128]{3,2,1,0:T(8,128)(2,1)S(1)} collective-permute-done((bf16[2,2,128,128]{3,2,1,0:T(8,128)(2,1)S(1)}, bf16[2,2,128,128]{3,2,1,0:T(8,128)(2,1)S(1)}, u32[]{:S(2)}, u32[]{:S(2)}) %collective-permute-start.7) | collective-permute-done | bytes 131104 | tf_op jit(solution)/shard_map/ppermute | solution.py:443
  59.8 1.6 %collective-permute-done.8.rest_2_ = bf16[2,2,128,128]{3,2,1,0:T(8,128)(2,1)S(1)} collective-permute-done((bf16[2,2,128,128]{3,2,1,0:T(8,128)(2,1)S(1)}, bf16[2,2,128,128]{3,2,1,0:T(8,128)(2,1)S(1)}, u32[]{:S(2)}, u32[]{:S(2)}) %collective-permute-start.8) | collective-permute-done | bytes 131104 | tf_op jit(solution)/shard_map/ppermute | solution.py:443
  61.4 3.9 %collective-permute-done.9.rest_3_ = bf16[2,2,128,128]{3,2,1,0:T(8,128)(2,1)S(1)} collective-permute-done((bf16[2,2,128,128]{3,2,1,0:T(8,128)(2,1)S(1)}, bf16[2,2,128,128]{3,2,1,0:T(8,128)(2,1)S(1)}, u32[]{:S(2)}, u32[]{:S(2)}) %collective-permute-start.9) | collective-permute-done | bytes 131104 | tf_op jit(solution)/shard_map/ppermute | solution.py:443
  65.3 1.2 %deposit.1 = (f32[3,2,2,384,128]{4,3,2,1,0:T(8,128)S(1)}, bf16[2,384,128]{2,1,0:T(8,128)(2,1)S(1)}, bf16[2,384,128]{2,1,0:T(8,128)(2,1)S(1)}) custom-call(s32[4,2]{1,0:T(4,128)S(1)} %copy.12.pos_ref, bf16[2,2,128,128]{3,2,1,0:T(8,128)(2,1)S(1)} %get-tuple-element.34.rest_0_, bf16[2,2,128,128]{3,2,1,0:T(8,128)(2,1)S(1)} %collective-permute-done.7.rest_1_, ...), custom_call_target="tpu_custom_call" | custom-call | bytes 3276832 | tf_op jit(solution)/shard_map/deposit/pallas_call | solution.py:25
  66.5 1.9 %collective-permute-start.10 = (bf16[2,384,128]{2,1,0:T(8,128)(2,1)S(1)}, bf16[2,384,128]{2,1,0:T(8,128)(2,1)S(1)}, u32[]{:S(2)}, u32[]{:S(2)}) collective-permute-start(bf16[2,384,128]{2,1,0:T(8,128)(2,1)S(1)} %get-tuple-element.39), channel_id=1, source_target_pairs={{1,2},{3,4},{5,6},{9,10},{11,12},{13,14},{17,18},{19,20},{21,22},{... | collective-permute-start | bytes 589832 | tf_op jit(solution)/shard_map/ppermute | solution.py:440
  68.4 0.1 collective-permute-start.11
  68.5 5.0 %collective-permute-done.10.rim_first_ref = bf16[2,384,128]{2,1,0:T(8,128)(2,1)S(1)} collective-permute-done((bf16[2,384,128]{2,1,0:T(8,128)(2,1)S(1)}, bf16[2,384,128]{2,1,0:T(8,128)(2,1)S(1)}, u32[]{:S(2)}, u32[]{:S(2)}) %collective-permute-start.10) | collective-permute-done | bytes 196640 | tf_op jit(solution)/shard_map/ppermute | solution.py:440
  73.5 0.0 collective-permute-done.11.rim_second_ref
  73.5 0.1 row_rims_back.1
  73.6 2.6 %collective-permute-start.12 = (bf16[2,2,64,256]{3,2,1,0:T(8,128)(2,1)S(1)}, bf16[2,2,64,256]{3,2,1,0:T(8,128)(2,1)S(1)}, u32[]{:S(2)}, u32[]{:S(2)}) collective-permute-start(bf16[2,2,64,256]{3,2,1,0:T(8,128)(2,1)S(1)} %get-tuple-element.41), channel_id=1, source_target_pairs={{0,8},{1,9},{2,10},{3,11},{4,12},{5,13},{6,14},{7,15},{16,24},{17,... | collective-permute-start | bytes 393224 | tf_op jit(solution)/shard_map/ppermute | solution.py:435
  76.2 1.9 %collective-permute-start.13 = (bf16[2,2,64,256]{3,2,1,0:T(8,128)(2,1)S(1)}, bf16[2,2,64,256]{3,2,1,0:T(8,128)(2,1)S(1)}, u32[]{:S(2)}, u32[]{:S(2)}) collective-permute-start(bf16[2,2,64,256]{3,2,1,0:T(8,128)(2,1)S(1)} %get-tuple-element.42), channel_id=1, source_target_pairs={{8,16},{9,17},{10,18},{11,19},{12,20},{13,21},{14,22},{15,23},{24,... | collective-permute-start | bytes 393224 | tf_op jit(solution)/shard_map/ppermute | solution.py:435
  78.1 1.0 %middle_rows.1.rest_2_ = f32[2,2,256,256]{3,2,1,0:T(8,128)} custom-call(f32[3,2,2,384,128]{4,3,2,1,0:T(8,128)S(1)} %get-tuple-element.38.ext_ref, bf16[2,384,128]{2,1,0:T(8,128)(2,1)S(1)} %collective-permute-done.10.rim_first_ref, bf16[2,384,128]{2,1,0:T(8,128)(2,1)S(1)} %collective-permute-done.11.rim_second_ref), custom_call_target="tpu_custom_call" | custom-call | bytes 3801088 | tf_op jit(solution)/shard_map/middle_rows/pallas_call | solution.py:25
  79.1 2.5 %collective-permute-done.12.rest_0_ = bf16[2,2,64,256]{3,2,1,0:T(8,128)(2,1)S(1)} collective-permute-done((bf16[2,2,64,256]{3,2,1,0:T(8,128)(2,1)S(1)}, bf16[2,2,64,256]{3,2,1,0:T(8,128)(2,1)S(1)}, u32[]{:S(2)}, u32[]{:S(2)}) %collective-permute-start.12) | collective-permute-done | bytes 131104 | tf_op jit(solution)/shard_map/ppermute | solution.py:435
  81.5 4.5 %collective-permute-done.13.rest_1_ = bf16[2,2,64,256]{3,2,1,0:T(8,128)(2,1)S(1)} collective-permute-done((bf16[2,2,64,256]{3,2,1,0:T(8,128)(2,1)S(1)}, bf16[2,2,64,256]{3,2,1,0:T(8,128)(2,1)S(1)}, u32[]{:S(2)}, u32[]{:S(2)}) %collective-permute-start.13) | collective-permute-done | bytes 131104 | tf_op jit(solution)/shard_map/ppermute | solution.py:435
  86.1 0.9 %edge_rows.1 = f32[2,2,256,256]{3,2,1,0:T(8,128)} custom-call(f32[3,2,2,384,128]{4,3,2,1,0:T(8,128)S(1)} %get-tuple-element.38.ext_ref, bf16[2,384,128]{2,1,0:T(8,128)(2,1)S(1)} %collective-permute-done.10.rim_first_ref, bf16[2,384,128]{2,1,0:T(8,128)(2,1)S(1)} %collective-permute-done.11.rim_second_ref, ...), custom_call_target="tpu_custom_call", output_to_operand_aliasing={{}: (5, {})} | custom-call | bytes 5111808 | tf_op jit(solution)/shard_map/edge_rows/pallas_call | solution.py:25
  (4 shorter events, 0.0 us)
Async XLA Ops:
  0.0 16.4 %copy-start.5 = (s32[1,4,2]{1,2,0:T(2,128)S(1)}, s32[1,4,2]{1,2,0:T(2,128)}, u32[]{:S(2)}) copy-start(s32[1,4,2]{1,2,0:T(2,128)} %param.12) | copy-start | bytes 100
  1.3 7.3 %collective-permute-start = (bf16[2,2,64,256]{3,2,1,0:T(8,128)(2,1)S(1)}, bf16[2,2,64,256]{3,2,1,0:T(8,128)(2,1)S(1)}, u32[]{:S(2)}, u32[]{:S(2)}) collective-permute-start(bf16[2,2,64,256]{3,2,1,0:T(8,128)(2,1)S(1)} %get-tuple-element.26), channel_id=1, source_target_pairs={{0,8},{1,9},{2,10},{3,11},{4,12},{5,13},{6,14},{7,15},{16,24},{17,... | collective-permute-start | bytes 393224 | tf_op jit(solution)/shard_map/ppermute | solution.py:435
  4.6 9.3 %collective-permute-start.1 = (bf16[2,2,64,256]{3,2,1,0:T(8,128)(2,1)S(1)}, bf16[2,2,64,256]{3,2,1,0:T(8,128)(2,1)S(1)}, u32[]{:S(2)}, u32[]{:S(2)}) collective-permute-start(bf16[2,2,64,256]{3,2,1,0:T(8,128)(2,1)S(1)} %get-tuple-element.27), channel_id=1, source_target_pairs={{8,16},{9,17},{10,18},{11,19},{12,20},{13,21},{14,22},{15,23},{24,... | collective-permute-start | bytes 393224 | tf_op jit(solution)/shard_map/ppermute | solution.py:435
  14.1 7.0 %collective-permute-start.2 = (bf16[2,384,128]{2,1,0:T(8,128)(2,1)S(1)}, bf16[2,384,128]{2,1,0:T(8,128)(2,1)S(1)}, u32[]{:S(2)}, u32[]{:S(2)}) collective-permute-start(bf16[2,384,128]{2,1,0:T(8,128)(2,1)S(1)} %get-tuple-element.28), channel_id=1, source_target_pairs={{1,2},{3,4},{5,6},{9,10},{11,12},{13,14},{17,18},{19,20},{21,22},{... | collective-permute-start | bytes 589832 | tf_op jit(solution)/shard_map/ppermute | solution.py:440
  16.0 5.1 %collective-permute-start.3 = (bf16[2,384,128]{2,1,0:T(8,128)(2,1)S(1)}, bf16[2,384,128]{2,1,0:T(8,128)(2,1)S(1)}, u32[]{:S(2)}, u32[]{:S(2)}) collective-permute-start(bf16[2,384,128]{2,1,0:T(8,128)(2,1)S(1)} %get-tuple-element.29), channel_id=1, source_target_pairs={{0,1},{2,3},{4,5},{6,7},{8,9},{10,11},{12,13},{14,15},{16,17},{18,... | collective-permute-start | bytes 589832 | tf_op jit(solution)/shard_map/ppermute | solution.py:440
  16.5 13.4 %copy-start.2 = (f32[2,128]{1,0:T(2,128)S(1)}, f32[2,128]{1,0:T(2,128)}, u32[]{:S(2)}) copy-start(f32[2,128]{1,0:T(2,128)} %phase_ref.1) | copy-start | bytes 3076
  16.5 13.4 %copy-start.3 = (f32[128,128]{1,0:T(8,128)S(1)}, f32[128,128]{1,0:T(8,128)}, u32[]{:S(2)}) copy-start(f32[128,128]{1,0:T(8,128)} %constant.5.clone.dft_imag_ref) | copy-start | bytes 196612
  16.5 13.4 %copy-start.4 = (f32[128,128]{1,0:T(8,128)S(1)}, f32[128,128]{1,0:T(8,128)}, u32[]{:S(2)}) copy-start(f32[128,128]{1,0:T(8,128)} %constant.4.clone.dft_real_ref) | copy-start | bytes 196612
  16.6 23.8 %copy-start = (f32[1,4,128,128]{3,2,1,0:T(8,128)S(1)}, f32[1,4,128,128]{3,2,1,0:T(8,128)}, u32[]{:S(2)}) copy-start(f32[1,4,128,128]{3,2,1,0:T(8,128)} %param.13) | copy-start | bytes 786436
  16.6 23.8 %copy-start.1 = (f32[2,128,128]{2,1,0:T(8,128)S(1)}, f32[2,128,128]{2,1,0:T(8,128)}, u32[]{:S(2)}) copy-start(f32[2,128,128]{2,1,0:T(8,128)} %probe_ref.1) | copy-start | bytes 393220
  22.0 14.1 %collective-permute-start.4 = (bf16[2,2,128,128]{3,2,1,0:T(8,128)(2,1)S(1)}, bf16[2,2,128,128]{3,2,1,0:T(8,128)(2,1)S(1)}, u32[]{:S(2)}, u32[]{:S(2)}) collective-permute-start(bf16[2,2,128,128]{3,2,1,0:T(8,128)(2,1)S(1)} %get-tuple-element.31), channel_id=1, source_target_pairs={{0,64},{64,0},{128,192},{192,128},{1,65},{65,1},{129,193},{193,129... | collective-permute-start | bytes 393224 | tf_op jit(solution)/shard_map/ppermute | solution.py:443
  25.4 10.8 %collective-permute-start.5 = (bf16[2,2,128,128]{3,2,1,0:T(8,128)(2,1)S(1)}, bf16[2,2,128,128]{3,2,1,0:T(8,128)(2,1)S(1)}, u32[]{:S(2)}, u32[]{:S(2)}) collective-permute-start(bf16[2,2,128,128]{3,2,1,0:T(8,128)(2,1)S(1)} %get-tuple-element.32), channel_id=1, source_target_pairs={{0,128},{64,192},{128,0},{192,64},{1,129},{65,193},{129,1},{193,65... | collective-permute-start | bytes 393224 | tf_op jit(solution)/shard_map/ppermute | solution.py:443
  29.9 10.6 %collective-permute-start.6 = (bf16[2,2,128,128]{3,2,1,0:T(8,128)(2,1)S(1)}, bf16[2,2,128,128]{3,2,1,0:T(8,128)(2,1)S(1)}, u32[]{:S(2)}, u32[]{:S(2)}) collective-permute-start(bf16[2,2,128,128]{3,2,1,0:T(8,128)(2,1)S(1)} %get-tuple-element.33), channel_id=1, source_target_pairs={{0,192},{64,128},{128,64},{192,0},{1,193},{65,129},{129,65},{193,1... | collective-permute-start | bytes 393224 | tf_op jit(solution)/shard_map/ppermute | solution.py:443
  46.3 13.5 %collective-permute-start.7 = (bf16[2,2,128,128]{3,2,1,0:T(8,128)(2,1)S(1)}, bf16[2,2,128,128]{3,2,1,0:T(8,128)(2,1)S(1)}, u32[]{:S(2)}, u32[]{:S(2)}) collective-permute-start(bf16[2,2,128,128]{3,2,1,0:T(8,128)(2,1)S(1)} %get-tuple-element.35), channel_id=1, source_target_pairs={{0,64},{64,0},{128,192},{192,128},{1,65},{65,1},{129,193},{193,129... | collective-permute-start | bytes 393224 | tf_op jit(solution)/shard_map/ppermute | solution.py:443
  49.3 12.1 %collective-permute-start.8 = (bf16[2,2,128,128]{3,2,1,0:T(8,128)(2,1)S(1)}, bf16[2,2,128,128]{3,2,1,0:T(8,128)(2,1)S(1)}, u32[]{:S(2)}, u32[]{:S(2)}) collective-permute-start(bf16[2,2,128,128]{3,2,1,0:T(8,128)(2,1)S(1)} %get-tuple-element.36), channel_id=1, source_target_pairs={{0,128},{64,192},{128,0},{192,64},{1,129},{65,193},{129,1},{193,65... | collective-permute-start | bytes 393224 | tf_op jit(solution)/shard_map/ppermute | solution.py:443
  52.3 13.0 %collective-permute-start.9 = (bf16[2,2,128,128]{3,2,1,0:T(8,128)(2,1)S(1)}, bf16[2,2,128,128]{3,2,1,0:T(8,128)(2,1)S(1)}, u32[]{:S(2)}, u32[]{:S(2)}) collective-permute-start(bf16[2,2,128,128]{3,2,1,0:T(8,128)(2,1)S(1)} %get-tuple-element.37), channel_id=1, source_target_pairs={{0,192},{64,128},{128,64},{192,0},{1,193},{65,129},{129,65},{193,1... | collective-permute-start | bytes 393224 | tf_op jit(solution)/shard_map/ppermute | solution.py:443
  66.5 7.0 %collective-permute-start.10 = (bf16[2,384,128]{2,1,0:T(8,128)(2,1)S(1)}, bf16[2,384,128]{2,1,0:T(8,128)(2,1)S(1)}, u32[]{:S(2)}, u32[]{:S(2)}) collective-permute-start(bf16[2,384,128]{2,1,0:T(8,128)(2,1)S(1)} %get-tuple-element.39), channel_id=1, source_target_pairs={{1,2},{3,4},{5,6},{9,10},{11,12},{13,14},{17,18},{19,20},{21,22},{... | collective-permute-start | bytes 589832 | tf_op jit(solution)/shard_map/ppermute | solution.py:440
  68.4 5.1 %collective-permute-start.11 = (bf16[2,384,128]{2,1,0:T(8,128)(2,1)S(1)}, bf16[2,384,128]{2,1,0:T(8,128)(2,1)S(1)}, u32[]{:S(2)}, u32[]{:S(2)}) collective-permute-start(bf16[2,384,128]{2,1,0:T(8,128)(2,1)S(1)} %get-tuple-element.40), channel_id=1, source_target_pairs={{0,1},{2,3},{4,5},{6,7},{8,9},{10,11},{12,13},{14,15},{16,17},{18,... | collective-permute-start | bytes 589832 | tf_op jit(solution)/shard_map/ppermute | solution.py:440
  73.6 7.9 %collective-permute-start.12 = (bf16[2,2,64,256]{3,2,1,0:T(8,128)(2,1)S(1)}, bf16[2,2,64,256]{3,2,1,0:T(8,128)(2,1)S(1)}, u32[]{:S(2)}, u32[]{:S(2)}) collective-permute-start(bf16[2,2,64,256]{3,2,1,0:T(8,128)(2,1)S(1)} %get-tuple-element.41), channel_id=1, source_target_pairs={{0,8},{1,9},{2,10},{3,11},{4,12},{5,13},{6,14},{7,15},{16,24},{17,... | collective-permute-start | bytes 393224 | tf_op jit(solution)/shard_map/ppermute | solution.py:435
  76.2 9.9 %collective-permute-start.13 = (bf16[2,2,64,256]{3,2,1,0:T(8,128)(2,1)S(1)}, bf16[2,2,64,256]{3,2,1,0:T(8,128)(2,1)S(1)}, u32[]{:S(2)}, u32[]{:S(2)}) collective-permute-start(bf16[2,2,64,256]{3,2,1,0:T(8,128)(2,1)S(1)} %get-tuple-element.42), channel_id=1, source_target_pairs={{8,16},{9,17},{10,18},{11,19},{12,20},{13,21},{14,22},{15,23},{24,... | collective-permute-start | bytes 393224 | tf_op jit(solution)/shard_map/ppermute | solution.py:435

commit v4 on v3

--- a/solution.py
+++ b/solution.py
@@ -397,26 +397,23 @@
         copy.wait()
 
 
-def edge_body(columns, ext_ref, rim_first_ref, rim_second_ref, *rest):
-    row_first_ref, row_second_ref, out_in, out_ref, held, sem = rest
+def edge_body(columns, which, ext_ref, rim_first_ref, rim_second_ref, row_ref, *rest):
+    out_in, out_ref, held, sem = rest
     del out_in
     size = out_ref.shape[-1]
     odd = odd_column()
-    flip = odd_row(columns)
-    blocks = ((0, RIM), (size - RIM, RIM))
-    copies = put_rows(out_ref, held, sem, blocks)
+    top = odd_row(columns) == (which == 0)
+    start = pl.multiple_of(jnp.where(top, 0, size - RIM), RIM)
+    copies = put_rows(out_ref, held, sem, ((start, RIM),))
+    slices = ext_ref.shape[1]
     for part in range(2):
-        for s in range(ext_ref.shape[1]):
-            for i, (start, rows) in enumerate(blocks):
-                refs = (odd, ext_ref, rim_first_ref, rim_second_ref, s, part)
-                pieces = halves_added(*refs, pl.ds(RIM + start, rows))
-                for tile, piece in enumerate(pieces):
-                    lanes = slice(tile * LANES, (tile + 1) * LANES)
-                    first = row_first_ref[s, part, :, lanes].astype(F32)
-                    second = row_second_ref[s, part, :, lanes].astype(F32)
-                    piece = piece + jnp.where(flip == (start == 0), first, second)
-                    held[part, s, i * RIM : (i + 1) * RIM, lanes] = piece
-                copies[(part * ext_ref.shape[1] + s) * 2 + i].start()
+        for s in range(slices):
+            refs = (odd, ext_ref, rim_first_ref, rim_second_ref, s, part)
+            pieces = halves_added(*refs, pl.ds(start + RIM, RIM))
+            for tile, piece in enumerate(pieces):
+                lanes = slice(tile * LANES, (tile + 1) * LANES)
+                held[part, s, :, lanes] = piece + row_ref[s, part, :, lanes].astype(F32)
+            copies[part * slices + s].start()
     for copy in copies:
         copy.wait()
 
@@ -538,20 +535,22 @@
         ),
         name="middle_rows",
     )
-    gradient = call(
-        functools.partial(edge_body, columns),
-        gradient,
-        (summed, *cols, *rows, middle),
-        specs=[VMEM] * 5 + [HBM],
-        outs=HBM,
-        scratch=(
-            pltpu.VMEM((2, slices, 2 * RIM, size), F32),
-            pltpu.SemaphoreType.DMA((2, slices, 2)),
-        ),
-        aliases={5: 0},
-        name="edge_rows",
-    )
-    return gradient[:, :, None]
+    result = middle
+    for which in range(2):
+        result = call(
+            functools.partial(edge_body, columns, which),
+            gradient,
+            (summed, *cols, rows[which], result),
+            specs=[VMEM] * 4 + [HBM],
+            outs=HBM,
+            scratch=(
+                pltpu.VMEM((2, slices, RIM, size), F32),
+                pltpu.SemaphoreType.DMA((2, slices, 1)),
+            ),
+            aliases={4: 0},
+            name=f"edge_rows_{which}",
+        )
+    return result[:, :, None]
 
 
 def solution(mesh):

time: 87.3 us -> 87.1 us (level)
    pallas_call x11 -> x12, Pallas kernels: 14.2 us -> 14.9 us  [call(): pl.pallas_call(body, out_shape=out_shape, in_specs=specs or [VMEM] * len(...]
  transfers between devices with their start and end apart: 14 -> 14, of which waited for: 11 -> 11; matrix products, arithmetic and copies ran while one was open for 0% -> 0% of each run, Pallas kernels for 4% -> 5%
where the time goes in v4:
time: 87.1 us; the launch traced here: 86.9 us
  waiting for transfers between devices  43 us (49%)
  starting transfers between devices  28.8 us (33%)
  Pallas kernels  14.9 us (17%)
    ppermute x6, waiting for transfers between devices, depth_swap(): return lax.ppermute(x, 'depth', [(i, i ^ by) for i in range(count)])  22.2 us
    pallas_call x12, Pallas kernels, call(): pl.pallas_call(body, out_shape=out_shape, in_specs=specs or [VMEM] * len(...  14.9 us
    ppermute x6, starting transfers between devices, depth_swap(): return lax.ppermute(x, 'depth', [(i, i ^ by) for i in range(count)])  14.5 us
    ppermute x4, waiting for transfers between devices, row_swap(): return lax.ppermute(x, 'tile', pairs)  11.4 us
    ppermute x4, starting transfers between devices, row_swap(): return lax.ppermute(x, 'tile', pairs)  9.95 us
    ppermute x4, waiting for transfers between devices, column_swap(): return lax.ppermute(x, 'tile', pairs)  9.36 us
    ppermute x4, starting transfers between devices, column_swap(): return lax.ppermute(x, 'tile', pairs)  4.36 us
  transfers between devices with their start and end apart: 14, of which 11 were waited for; matrix products, arithmetic and copies ran while one was open for 0% of the time, Pallas kernels for 5%

profile of v4, /device:TPU:34, one launch (start us, length us, event | category | flops | bytes accessed | tf_op | source)
XLA Modules:
  0.0 86.9 jit_solution(13345641048151882155)
XLA Ops:
  0.0 1.3 %row_rims_out.1 = (bf16[2,2,64,256]{3,2,1,0:T(8,128)(2,1)S(1)}, bf16[2,2,64,256]{3,2,1,0:T(8,128)(2,1)S(1)}) custom-call(f32[2,256,256]{2,1,0:T(8,128)} %bitcast.8, f32[2,256,256]{2,1,0:T(8,128)} %bitcast.10), custom_call_target="tpu_custom_call" | custom-call | flops 2621440 | bytes 1310720 | tf_op jit(solution)/shard_map/row_rims_out/pallas_call | solution.py:25
  1.3 3.3 %collective-permute-start = (bf16[2,2,64,256]{3,2,1,0:T(8,128)(2,1)S(1)}, bf16[2,2,64,256]{3,2,1,0:T(8,128)(2,1)S(1)}, u32[]{:S(2)}, u32[]{:S(2)}) collective-permute-start(bf16[2,2,64,256]{3,2,1,0:T(8,128)(2,1)S(1)} %get-tuple-element.26), channel_id=1, source_target_pairs={{0,8},{1,9},{2,10},{3,11},{4,12},{5,13},{6,14},{7,15},{16,24},{17,... | collective-permute-start | bytes 393224 | tf_op jit(solution)/shard_map/ppermute | solution.py:432
  4.6 2.2 %collective-permute-start.1 = (bf16[2,2,64,256]{3,2,1,0:T(8,128)(2,1)S(1)}, bf16[2,2,64,256]{3,2,1,0:T(8,128)(2,1)S(1)}, u32[]{:S(2)}, u32[]{:S(2)}) collective-permute-start(bf16[2,2,64,256]{3,2,1,0:T(8,128)(2,1)S(1)} %get-tuple-element.27), channel_id=1, source_target_pairs={{8,16},{9,17},{10,18},{11,19},{12,20},{13,21},{14,22},{15,23},{24,... | collective-permute-start | bytes 393224 | tf_op jit(solution)/shard_map/ppermute | solution.py:432
  6.8 1.8 %transmit.1.t_ref = bf16[2,2,256,256]{3,2,1,0:T(8,128)(2,1)S(1)} custom-call(f32[2,256,256]{2,1,0:T(8,128)} %bitcast.9, f32[2,256,256]{2,1,0:T(8,128)} %bitcast.11), custom_call_target="tpu_custom_call" | custom-call | flops 5242880 | bytes 1572864 | tf_op jit(solution)/shard_map/transmit/pallas_call | solution.py:25
  8.6 0.0 collective-permute-done.row_first_ref
  8.6 5.2 %collective-permute-done.1.row_second_ref = bf16[2,2,64,256]{3,2,1,0:T(8,128)(2,1)S(1)} collective-permute-done((bf16[2,2,64,256]{3,2,1,0:T(8,128)(2,1)S(1)}, bf16[2,2,64,256]{3,2,1,0:T(8,128)(2,1)S(1)}, u32[]{:S(2)}, u32[]{:S(2)}) %collective-permute-start.1) | collective-permute-done | bytes 131104 | tf_op jit(solution)/shard_map/ppermute | solution.py:432
  13.8 0.2 column_rims_out.1
  14.1 1.9 %collective-permute-start.2 = (bf16[2,384,128]{2,1,0:T(8,128)(2,1)S(1)}, bf16[2,384,128]{2,1,0:T(8,128)(2,1)S(1)}, u32[]{:S(2)}, u32[]{:S(2)}) collective-permute-start(bf16[2,384,128]{2,1,0:T(8,128)(2,1)S(1)} %get-tuple-element.28), channel_id=1, source_target_pairs={{1,2},{3,4},{5,6},{9,10},{11,12},{13,14},{17,18},{19,20},{21,22},{... | collective-permute-start | bytes 589832 | tf_op jit(solution)/shard_map/ppermute | solution.py:437
  16.0 0.4 collective-permute-start.3
  16.4 0.0 copy-done.5
  16.4 0.1 copy.13.pos_ref
  16.5 0.1 extend.1.ext_in
  16.6 0.0 copy-start
  16.6 0.0 copy-start.1
  16.6 4.4 %collective-permute-done.2.rim_first_ref = bf16[2,384,128]{2,1,0:T(8,128)(2,1)S(1)} collective-permute-done((bf16[2,384,128]{2,1,0:T(8,128)(2,1)S(1)}, bf16[2,384,128]{2,1,0:T(8,128)(2,1)S(1)}, u32[]{:S(2)}, u32[]{:S(2)}) %collective-permute-start.2) | collective-permute-done | bytes 196640 | tf_op jit(solution)/shard_map/ppermute | solution.py:437
  21.0 0.0 collective-permute-done.3.rim_second_ref
  21.1 1.0 %cut.1 = (f32[3,2,2,384,128]{4,3,2,1,0:T(8,128)S(1)}, bf16[2,2,128,128]{3,2,1,0:T(8,128)(2,1)S(1)}, bf16[2,2,128,128]{3,2,1,0:T(8,128)(2,1)S(1)}, bf16[2,2,128,1...) custom-call(s32[4,2]{1,0:T(4,128)S(1)} %copy.13.pos_ref, ...), custom_call_target="tpu_custom_call", output_to_operand_aliasing={{0}: (3, {})} | custom-call | bytes 5636128 | tf_op jit(solution)/shard_map/cut/pallas_call | solution.py:25
  22.0 3.4 %collective-permute-start.4 = (bf16[2,2,128,128]{3,2,1,0:T(8,128)(2,1)S(1)}, bf16[2,2,128,128]{3,2,1,0:T(8,128)(2,1)S(1)}, u32[]{:S(2)}, u32[]{:S(2)}) collective-permute-start(bf16[2,2,128,128]{3,2,1,0:T(8,128)(2,1)S(1)} %get-tuple-element.31), channel_id=1, source_target_pairs={{0,64},{64,0},{128,192},{192,128},{1,65},{65,1},{129,193},{193,129... | collective-permute-start | bytes 393224 | tf_op jit(solution)/shard_map/ppermute | solution.py:440
  25.4 4.5 %collective-permute-start.5 = (bf16[2,2,128,128]{3,2,1,0:T(8,128)(2,1)S(1)}, bf16[2,2,128,128]{3,2,1,0:T(8,128)(2,1)S(1)}, u32[]{:S(2)}, u32[]{:S(2)}) collective-permute-start(bf16[2,2,128,128]{3,2,1,0:T(8,128)(2,1)S(1)} %get-tuple-element.32), channel_id=1, source_target_pairs={{0,128},{64,192},{128,0},{192,64},{1,129},{65,193},{129,1},{193,65... | collective-permute-start | bytes 393224 | tf_op jit(solution)/shard_map/ppermute | solution.py:440
  29.9 0.0 collective-permute-start.6
  29.9 0.0 copy-done.2
  29.9 0.0 copy-done.3
  29.9 0.0 copy-done.4
  29.9 0.7 operators.1
  30.6 5.5 %collective-permute-done.4.rest_1_ = bf16[2,2,128,128]{3,2,1,0:T(8,128)(2,1)S(1)} collective-permute-done((bf16[2,2,128,128]{3,2,1,0:T(8,128)(2,1)S(1)}, bf16[2,2,128,128]{3,2,1,0:T(8,128)(2,1)S(1)}, u32[]{:S(2)}, u32[]{:S(2)}) %collective-permute-start.4) | collective-permute-done | bytes 131104 | tf_op jit(solution)/shard_map/ppermute | solution.py:440
  36.1 0.1 collective-permute-done.5.rest_2_
  36.2 4.3 %collective-permute-done.6.rest_3_ = bf16[2,2,128,128]{3,2,1,0:T(8,128)(2,1)S(1)} collective-permute-done((bf16[2,2,128,128]{3,2,1,0:T(8,128)(2,1)S(1)}, bf16[2,2,128,128]{3,2,1,0:T(8,128)(2,1)S(1)}, u32[]{:S(2)}, u32[]{:S(2)}) %collective-permute-start.6) | collective-permute-done | bytes 131104 | tf_op jit(solution)/shard_map/ppermute | solution.py:440
  40.4 0.0 copy-done
  40.4 5.9 %waves.1 = (bf16[2,2,128,128]{3,2,1,0:T(8,128)(2,1)S(1)}, bf16[2,2,128,128]{3,2,1,0:T(8,128)(2,1)S(1)}, bf16[2,2,128,128]{3,2,1,0:T(8,128)(2,1)S(1)}, bf16[2,2,128,128]{3,2,1,0:T(8,128)(2,1)S(1)}) custom-call(bf16[4,2,256,256]{3,2,1,0:T(8,128)(2,1)S(1)} %get-tuple-element.24.fwd_ref, bf16[4,256,256]{2,1,0:T(8,128)(2,1)S(1)} %get-tuple-element.25.bwd_ref, ...), custom_call_target="tpu_custom_call" | custom-call | flops 1207959552 | bytes 3014656 | tf_op jit(solution)/shard_map/waves/pallas_call | solution.py:25
  46.3 3.0 %collective-permute-start.7 = (bf16[2,2,128,128]{3,2,1,0:T(8,128)(2,1)S(1)}, bf16[2,2,128,128]{3,2,1,0:T(8,128)(2,1)S(1)}, u32[]{:S(2)}, u32[]{:S(2)}) collective-permute-start(bf16[2,2,128,128]{3,2,1,0:T(8,128)(2,1)S(1)} %get-tuple-element.35), channel_id=1, source_target_pairs={{0,64},{64,0},{128,192},{192,128},{1,65},{65,1},{129,193},{193,129... | collective-permute-start | bytes 393224 | tf_op jit(solution)/shard_map/ppermute | solution.py:440
  49.3 3.1 %collective-permute-start.8 = (bf16[2,2,128,128]{3,2,1,0:T(8,128)(2,1)S(1)}, bf16[2,2,128,128]{3,2,1,0:T(8,128)(2,1)S(1)}, u32[]{:S(2)}, u32[]{:S(2)}) collective-permute-start(bf16[2,2,128,128]{3,2,1,0:T(8,128)(2,1)S(1)} %get-tuple-element.36), channel_id=1, source_target_pairs={{0,128},{64,192},{128,0},{192,64},{1,129},{65,193},{129,1},{193,65... | collective-permute-start | bytes 393224 | tf_op jit(solution)/shard_map/ppermute | solution.py:440
  52.3 0.6 collective-permute-start.9
  53.0 6.8 %collective-permute-done.7.rest_1_ = bf16[2,2,128,128]{3,2,1,0:T(8,128)(2,1)S(1)} collective-permute-done((bf16[2,2,128,128]{3,2,1,0:T(8,128)(2,1)S(1)}, bf16[2,2,128,128]{3,2,1,0:T(8,128)(2,1)S(1)}, u32[]{:S(2)}, u32[]{:S(2)}) %collective-permute-start.7) | collective-permute-done | bytes 131104 | tf_op jit(solution)/shard_map/ppermute | solution.py:440
  59.8 1.6 %collective-permute-done.8.rest_2_ = bf16[2,2,128,128]{3,2,1,0:T(8,128)(2,1)S(1)} collective-permute-done((bf16[2,2,128,128]{3,2,1,0:T(8,128)(2,1)S(1)}, bf16[2,2,128,128]{3,2,1,0:T(8,128)(2,1)S(1)}, u32[]{:S(2)}, u32[]{:S(2)}) %collective-permute-start.8) | collective-permute-done | bytes 131104 | tf_op jit(solution)/shard_map/ppermute | solution.py:440
  61.4 3.9 %collective-permute-done.9.rest_3_ = bf16[2,2,128,128]{3,2,1,0:T(8,128)(2,1)S(1)} collective-permute-done((bf16[2,2,128,128]{3,2,1,0:T(8,128)(2,1)S(1)}, bf16[2,2,128,128]{3,2,1,0:T(8,128)(2,1)S(1)}, u32[]{:S(2)}, u32[]{:S(2)}) %collective-permute-start.9) | collective-permute-done | bytes 131104 | tf_op jit(solution)/shard_map/ppermute | solution.py:440
  65.3 1.2 %deposit.1 = (f32[3,2,2,384,128]{4,3,2,1,0:T(8,128)S(1)}, bf16[2,384,128]{2,1,0:T(8,128)(2,1)S(1)}, bf16[2,384,128]{2,1,0:T(8,128)(2,1)S(1)}) custom-call(s32[4,2]{1,0:T(4,128)S(1)} %copy.13.pos_ref, bf16[2,2,128,128]{3,2,1,0:T(8,128)(2,1)S(1)} %get-tuple-element.34.rest_0_, bf16[2,2,128,128]{3,2,1,0:T(8,128)(2,1)S(1)} %collective-permute-done.7.rest_1_, ...), custom_call_target="tpu_custom_call" | custom-call | bytes 3276832 | tf_op jit(solution)/shard_map/deposit/pallas_call | solution.py:25
  66.5 1.9 %collective-permute-start.10 = (bf16[2,384,128]{2,1,0:T(8,128)(2,1)S(1)}, bf16[2,384,128]{2,1,0:T(8,128)(2,1)S(1)}, u32[]{:S(2)}, u32[]{:S(2)}) collective-permute-start(bf16[2,384,128]{2,1,0:T(8,128)(2,1)S(1)} %get-tuple-element.39), channel_id=1, source_target_pairs={{1,2},{3,4},{5,6},{9,10},{11,12},{13,14},{17,18},{19,20},{21,22},{... | collective-permute-start | bytes 589832 | tf_op jit(solution)/shard_map/ppermute | solution.py:437
  68.4 0.1 collective-permute-start.11
  68.5 5.0 %collective-permute-done.10.rim_first_ref = bf16[2,384,128]{2,1,0:T(8,128)(2,1)S(1)} collective-permute-done((bf16[2,384,128]{2,1,0:T(8,128)(2,1)S(1)}, bf16[2,384,128]{2,1,0:T(8,128)(2,1)S(1)}, u32[]{:S(2)}, u32[]{:S(2)}) %collective-permute-start.10) | collective-permute-done | bytes 196640 | tf_op jit(solution)/shard_map/ppermute | solution.py:437
  73.5 0.0 collective-permute-done.11.rim_second_ref
  73.5 0.1 row_rims_back.1
  73.6 2.6 %collective-permute-start.13 = (bf16[2,2,64,256]{3,2,1,0:T(8,128)(2,1)S(1)}, bf16[2,2,64,256]{3,2,1,0:T(8,128)(2,1)S(1)}, u32[]{:S(2)}, u32[]{:S(2)}) collective-permute-start(bf16[2,2,64,256]{3,2,1,0:T(8,128)(2,1)S(1)} %get-tuple-element.42), channel_id=1, source_target_pairs={{0,8},{1,9},{2,10},{3,11},{4,12},{5,13},{6,14},{7,15},{16,24},{17,... | collective-permute-start | bytes 393224 | tf_op jit(solution)/shard_map/ppermute | solution.py:432
  76.2 1.9 %collective-permute-start.12 = (bf16[2,2,64,256]{3,2,1,0:T(8,128)(2,1)S(1)}, bf16[2,2,64,256]{3,2,1,0:T(8,128)(2,1)S(1)}, u32[]{:S(2)}, u32[]{:S(2)}) collective-permute-start(bf16[2,2,64,256]{3,2,1,0:T(8,128)(2,1)S(1)} %get-tuple-element.41), channel_id=1, source_target_pairs={{8,16},{9,17},{10,18},{11,19},{12,20},{13,21},{14,22},{15,23},{24,... | collective-permute-start | bytes 393224 | tf_op jit(solution)/shard_map/ppermute | solution.py:432
  78.1 1.0 %middle_rows.1.rest_0_ = f32[2,2,256,256]{3,2,1,0:T(8,128)} custom-call(f32[3,2,2,384,128]{4,3,2,1,0:T(8,128)S(1)} %get-tuple-element.38.ext_ref, bf16[2,384,128]{2,1,0:T(8,128)(2,1)S(1)} %collective-permute-done.10.rim_first_ref, bf16[2,384,128]{2,1,0:T(8,128)(2,1)S(1)} %collective-permute-done.11.rim_second_ref), custom_call_target="tpu_custom_call" | custom-call | bytes 3801088 | tf_op jit(solution)/shard_map/middle_rows/pallas_call | solution.py:25
  79.1 2.5 %collective-permute-done.13.row_ref = bf16[2,2,64,256]{3,2,1,0:T(8,128)(2,1)S(1)} collective-permute-done((bf16[2,2,64,256]{3,2,1,0:T(8,128)(2,1)S(1)}, bf16[2,2,64,256]{3,2,1,0:T(8,128)(2,1)S(1)}, u32[]{:S(2)}, u32[]{:S(2)}) %collective-permute-start.13) | collective-permute-done | bytes 131104 | tf_op jit(solution)/shard_map/ppermute | solution.py:432
  81.5 0.8 edge_rows_0.1.rest_0_
  82.4 3.7 %collective-permute-done.12.row_ref = bf16[2,2,64,256]{3,2,1,0:T(8,128)(2,1)S(1)} collective-permute-done((bf16[2,2,64,256]{3,2,1,0:T(8,128)(2,1)S(1)}, bf16[2,2,64,256]{3,2,1,0:T(8,128)(2,1)S(1)}, u32[]{:S(2)}, u32[]{:S(2)}) %collective-permute-start.12) | collective-permute-done | bytes 131104 | tf_op jit(solution)/shard_map/ppermute | solution.py:432
  86.1 0.8 edge_rows_1.1
  (5 shorter events, 0.0 us)
Async XLA Ops:
  0.0 16.4 %copy-start.5 = (s32[1,4,2]{1,2,0:T(2,128)S(1)}, s32[1,4,2]{1,2,0:T(2,128)}, u32[]{:S(2)}) copy-start(s32[1,4,2]{1,2,0:T(2,128)} %param.12) | copy-start | bytes 100
  1.3 7.3 %collective-permute-start = (bf16[2,2,64,256]{3,2,1,0:T(8,128)(2,1)S(1)}, bf16[2,2,64,256]{3,2,1,0:T(8,128)(2,1)S(1)}, u32[]{:S(2)}, u32[]{:S(2)}) collective-permute-start(bf16[2,2,64,256]{3,2,1,0:T(8,128)(2,1)S(1)} %get-tuple-element.26), channel_id=1, source_target_pairs={{0,8},{1,9},{2,10},{3,11},{4,12},{5,13},{6,14},{7,15},{16,24},{17,... | collective-permute-start | bytes 393224 | tf_op jit(solution)/shard_map/ppermute | solution.py:432
  4.6 9.3 %collective-permute-start.1 = (bf16[2,2,64,256]{3,2,1,0:T(8,128)(2,1)S(1)}, bf16[2,2,64,256]{3,2,1,0:T(8,128)(2,1)S(1)}, u32[]{:S(2)}, u32[]{:S(2)}) collective-permute-start(bf16[2,2,64,256]{3,2,1,0:T(8,128)(2,1)S(1)} %get-tuple-element.27), channel_id=1, source_target_pairs={{8,16},{9,17},{10,18},{11,19},{12,20},{13,21},{14,22},{15,23},{24,... | collective-permute-start | bytes 393224 | tf_op jit(solution)/shard_map/ppermute | solution.py:432
  14.1 7.0 %collective-permute-start.2 = (bf16[2,384,128]{2,1,0:T(8,128)(2,1)S(1)}, bf16[2,384,128]{2,1,0:T(8,128)(2,1)S(1)}, u32[]{:S(2)}, u32[]{:S(2)}) collective-permute-start(bf16[2,384,128]{2,1,0:T(8,128)(2,1)S(1)} %get-tuple-element.28), channel_id=1, source_target_pairs={{1,2},{3,4},{5,6},{9,10},{11,12},{13,14},{17,18},{19,20},{21,22},{... | collective-permute-start | bytes 589832 | tf_op jit(solution)/shard_map/ppermute | solution.py:437
  16.0 5.1 %collective-permute-start.3 = (bf16[2,384,128]{2,1,0:T(8,128)(2,1)S(1)}, bf16[2,384,128]{2,1,0:T(8,128)(2,1)S(1)}, u32[]{:S(2)}, u32[]{:S(2)}) collective-permute-start(bf16[2,384,128]{2,1,0:T(8,128)(2,1)S(1)} %get-tuple-element.29), channel_id=1, source_target_pairs={{0,1},{2,3},{4,5},{6,7},{8,9},{10,11},{12,13},{14,15},{16,17},{18,... | collective-permute-start | bytes 589832 | tf_op jit(solution)/shard_map/ppermute | solution.py:437
  16.5 13.4 %copy-start.2 = (f32[2,128]{1,0:T(2,128)S(1)}, f32[2,128]{1,0:T(2,128)}, u32[]{:S(2)}) copy-start(f32[2,128]{1,0:T(2,128)} %phase_ref.1) | copy-start | bytes 3076
  16.5 13.4 %copy-start.3 = (f32[128,128]{1,0:T(8,128)S(1)}, f32[128,128]{1,0:T(8,128)}, u32[]{:S(2)}) copy-start(f32[128,128]{1,0:T(8,128)} %constant.5.clone.dft_imag_ref) | copy-start | bytes 196612
  16.5 13.4 %copy-start.4 = (f32[128,128]{1,0:T(8,128)S(1)}, f32[128,128]{1,0:T(8,128)}, u32[]{:S(2)}) copy-start(f32[128,128]{1,0:T(8,128)} %constant.4.clone.dft_real_ref) | copy-start | bytes 196612
  16.6 23.8 %copy-start = (f32[1,4,128,128]{3,2,1,0:T(8,128)S(1)}, f32[1,4,128,128]{3,2,1,0:T(8,128)}, u32[]{:S(2)}) copy-start(f32[1,4,128,128]{3,2,1,0:T(8,128)} %param.13) | copy-start | bytes 786436
  16.6 23.8 %copy-start.1 = (f32[2,128,128]{2,1,0:T(8,128)S(1)}, f32[2,128,128]{2,1,0:T(8,128)}, u32[]{:S(2)}) copy-start(f32[2,128,128]{2,1,0:T(8,128)} %probe_ref.1) | copy-start | bytes 393220
  22.0 14.1 %collective-permute-start.4 = (bf16[2,2,128,128]{3,2,1,0:T(8,128)(2,1)S(1)}, bf16[2,2,128,128]{3,2,1,0:T(8,128)(2,1)S(1)}, u32[]{:S(2)}, u32[]{:S(2)}) collective-permute-start(bf16[2,2,128,128]{3,2,1,0:T(8,128)(2,1)S(1)} %get-tuple-element.31), channel_id=1, source_target_pairs={{0,64},{64,0},{128,192},{192,128},{1,65},{65,1},{129,193},{193,129... | collective-permute-start | bytes 393224 | tf_op jit(solution)/shard_map/ppermute | solution.py:440
  25.4 10.8 %collective-permute-start.5 = (bf16[2,2,128,128]{3,2,1,0:T(8,128)(2,1)S(1)}, bf16[2,2,128,128]{3,2,1,0:T(8,128)(2,1)S(1)}, u32[]{:S(2)}, u32[]{:S(2)}) collective-permute-start(bf16[2,2,128,128]{3,2,1,0:T(8,128)(2,1)S(1)} %get-tuple-element.32), channel_id=1, source_target_pairs={{0,128},{64,192},{128,0},{192,64},{1,129},{65,193},{129,1},{193,65... | collective-permute-start | bytes 393224 | tf_op jit(solution)/shard_map/ppermute | solution.py:440
  29.9 10.6 %collective-permute-start.6 = (bf16[2,2,128,128]{3,2,1,0:T(8,128)(2,1)S(1)}, bf16[2,2,128,128]{3,2,1,0:T(8,128)(2,1)S(1)}, u32[]{:S(2)}, u32[]{:S(2)}) collective-permute-start(bf16[2,2,128,128]{3,2,1,0:T(8,128)(2,1)S(1)} %get-tuple-element.33), channel_id=1, source_target_pairs={{0,192},{64,128},{128,64},{192,0},{1,193},{65,129},{129,65},{193,1... | collective-permute-start | bytes 393224 | tf_op jit(solution)/shard_map/ppermute | solution.py:440
  46.3 13.5 %collective-permute-start.7 = (bf16[2,2,128,128]{3,2,1,0:T(8,128)(2,1)S(1)}, bf16[2,2,128,128]{3,2,1,0:T(8,128)(2,1)S(1)}, u32[]{:S(2)}, u32[]{:S(2)}) collective-permute-start(bf16[2,2,128,128]{3,2,1,0:T(8,128)(2,1)S(1)} %get-tuple-element.35), channel_id=1, source_target_pairs={{0,64},{64,0},{128,192},{192,128},{1,65},{65,1},{129,193},{193,129... | collective-permute-start | bytes 393224 | tf_op jit(solution)/shard_map/ppermute | solution.py:440
  49.3 12.1 %collective-permute-start.8 = (bf16[2,2,128,128]{3,2,1,0:T(8,128)(2,1)S(1)}, bf16[2,2,128,128]{3,2,1,0:T(8,128)(2,1)S(1)}, u32[]{:S(2)}, u32[]{:S(2)}) collective-permute-start(bf16[2,2,128,128]{3,2,1,0:T(8,128)(2,1)S(1)} %get-tuple-element.36), channel_id=1, source_target_pairs={{0,128},{64,192},{128,0},{192,64},{1,129},{65,193},{129,1},{193,65... | collective-permute-start | bytes 393224 | tf_op jit(solution)/shard_map/ppermute | solution.py:440
  52.3 13.0 %collective-permute-start.9 = (bf16[2,2,128,128]{3,2,1,0:T(8,128)(2,1)S(1)}, bf16[2,2,128,128]{3,2,1,0:T(8,128)(2,1)S(1)}, u32[]{:S(2)}, u32[]{:S(2)}) collective-permute-start(bf16[2,2,128,128]{3,2,1,0:T(8,128)(2,1)S(1)} %get-tuple-element.37), channel_id=1, source_target_pairs={{0,192},{64,128},{128,64},{192,0},{1,193},{65,129},{129,65},{193,1... | collective-permute-start | bytes 393224 | tf_op jit(solution)/shard_map/ppermute | solution.py:440
  66.5 7.0 %collective-permute-start.10 = (bf16[2,384,128]{2,1,0:T(8,128)(2,1)S(1)}, bf16[2,384,128]{2,1,0:T(8,128)(2,1)S(1)}, u32[]{:S(2)}, u32[]{:S(2)}) collective-permute-start(bf16[2,384,128]{2,1,0:T(8,128)(2,1)S(1)} %get-tuple-element.39), channel_id=1, source_target_pairs={{1,2},{3,4},{5,6},{9,10},{11,12},{13,14},{17,18},{19,20},{21,22},{... | collective-permute-start | bytes 589832 | tf_op jit(solution)/shard_map/ppermute | solution.py:437
  68.4 5.1 %collective-permute-start.11 = (bf16[2,384,128]{2,1,0:T(8,128)(2,1)S(1)}, bf16[2,384,128]{2,1,0:T(8,128)(2,1)S(1)}, u32[]{:S(2)}, u32[]{:S(2)}) collective-permute-start(bf16[2,384,128]{2,1,0:T(8,128)(2,1)S(1)} %get-tuple-element.40), channel_id=1, source_target_pairs={{0,1},{2,3},{4,5},{6,7},{8,9},{10,11},{12,13},{14,15},{16,17},{18,... | collective-permute-start | bytes 589832 | tf_op jit(solution)/shard_map/ppermute | solution.py:437
  73.6 7.9 %collective-permute-start.13 = (bf16[2,2,64,256]{3,2,1,0:T(8,128)(2,1)S(1)}, bf16[2,2,64,256]{3,2,1,0:T(8,128)(2,1)S(1)}, u32[]{:S(2)}, u32[]{:S(2)}) collective-permute-start(bf16[2,2,64,256]{3,2,1,0:T(8,128)(2,1)S(1)} %get-tuple-element.42), channel_id=1, source_target_pairs={{0,8},{1,9},{2,10},{3,11},{4,12},{5,13},{6,14},{7,15},{16,24},{17,... | collective-permute-start | bytes 393224 | tf_op jit(solution)/shard_map/ppermute | solution.py:432
  76.2 9.9 %collective-permute-start.12 = (bf16[2,2,64,256]{3,2,1,0:T(8,128)(2,1)S(1)}, bf16[2,2,64,256]{3,2,1,0:T(8,128)(2,1)S(1)}, u32[]{:S(2)}, u32[]{:S(2)}) collective-permute-start(bf16[2,2,64,256]{3,2,1,0:T(8,128)(2,1)S(1)} %get-tuple-element.41), channel_id=1, source_target_pairs={{8,16},{9,17},{10,18},{11,19},{12,20},{13,21},{14,22},{15,23},{24,... | collective-permute-start | bytes 393224 | tf_op jit(solution)/shard_map/ppermute | solution.py:432
